TPU v7x, 32 devices: a whole 2x2x4 slice. The times are simulated.
32 devices in a mesh: ctx: 8 (over y, x, core), wsh: 4 (over z).
Axes of the slice: x: 2, y: 2, z: 4, core: 2. Of those that a mesh axis runs over, the one named last changes fastest.
Arguments:
- block_input: float32 [4, 1024, 1024], P('wsh', 'ctx'), may hold values from -6 to 6
- out_cotangent: float32 [4, 1024, 1024], P('wsh', 'ctx'), may hold values from -6 to 6
- lengths: int32 [4, 2], P('wsh'), may hold values from 256 to 768, as said below
- slot_block: int32 [16], replicated, may hold values from 0 to 15, as said below
- norm_gains: bfloat16 [2, 1024], P(None, 'wsh'), may hold values from 0.5 to 1.5
- short_filter: float32 [5, 1792], replicated, may hold values from -3 to 3
- step_bias: float32 [24], replicated, may hold values from -3 to -1
- log_rate: float32 [24], replicated, may hold values from -7 to -1.5
- skip_gain: float32 [24], replicated, may hold values from 0.5 to 1.5
- mixer_in: bfloat16 [1024, 3352], P('wsh'), may hold values from -0.1875 to 0.1875
- mixer_out: bfloat16 [1536, 1024], P(None, 'wsh'), may hold values from -0.0390625 to 0.0390625
- attend_in: bfloat16 [1024, 768], P('wsh'), may hold values from -1 to 1
- attend_out: bfloat16 [512, 1024], P(None, 'wsh'), may hold values from -2 to 2
- gate_up: bfloat16 [2, 1024, 2048], P(None, None, 'wsh'), may hold values from -0.1875 to 0.1875
- down_weight: bfloat16 [2048, 1024], P('wsh'), may hold values from -0.125 to 0.125
Outputs:
- block_output: float32 [4, 1024, 1024], P('wsh', 'ctx')
- input_grad: float32 [4, 1024, 1024], P('wsh', 'ctx')
- gains_grad: float32 [2, 1024], P(None, ('ctx', 'wsh'))
- filter_grad: float32 [5, 1792], replicated
- step_bias_grad: float32 [24], replicated
- log_rate_grad: float32 [24], replicated
- skip_grad: float32 [24], replicated
- mixer_in_grad: float32 [1024, 3352], P(('ctx', 'wsh'))
- mixer_out_grad: float32 [1536, 1024], P(None, ('ctx', 'wsh'))
- attend_in_grad: float32 [1024, 768], P(('ctx', 'wsh'))
- attend_out_grad: float32 [512, 1024], P(None, ('ctx', 'wsh'))
- gate_up_grad: float32 [2, 1024, 2048], P(None, 'ctx', 'wsh')
- down_grad: float32 [2048, 1024], P('wsh', 'ctx')
Inputs may be any that keep to these rules, and one draw needn't show every extreme that they name: Both lengths of a group are multiples of 64 and sum to 1024. `slot_block`: A permutation of the 16 logical blocks; for every c the slots 2c and 2c + 1 hold blocks k and 15 - k for some k, in either order.
All inputs are finite; a program needn't handle non-finite values.
Results may differ from a plain program's by a relative error of at most 0.015.
Values may be sent and summed in bfloat16 or wider, within the bound.
No kernel may reach another device: no remote copies, remote signals or barrier semaphores. Data moves between devices by JAX's collectives and lax.ppermute only.
A program may use at most 256 MiB of HBM per device.

v0:
```python
import math

import jax
import jax.numpy as jnp
from jax import lax
from jax.sharding import PartitionSpec as P

MHEADS = 24
HEAD_M = 64
NSTATE = 128
QH = 8
KVH = 2
HD = 64
KERNEL = 4
DSSM = 1536
CONV = 1792
AQ = 512
GRP = 4


EPS = 1e-05
ROPE_BASE = 100000000000.0
HIGH = lax.Precision.HIGHEST
NEG_LARGE = -1e30


def rms_norm(values, gain):
    scale = lax.rsqrt(jnp.mean(values * values, axis=-1, keepdims=True) + EPS)
    return values * scale * gain


def silu_slope(values):
    sigmoid_value = jax.nn.sigmoid(values)
    return sigmoid_value * (1.0 + values * (1.0 - sigmoid_value))


def rope_tables(positions):
    half = HD // 2
    freqs = jnp.exp(jnp.arange(half, dtype=jnp.float32) * (-2.0 * math.log(ROPE_BASE) / HD))
    angles = positions.astype(jnp.float32)[:, None] * freqs[None, :]
    return (jnp.cos(angles)[:, None, :], jnp.sin(angles)[:, None, :])


def rotate(values, cosines, sines):
    half = values.shape[-1] // 2
    first = values[..., :half]
    second = values[..., half:]
    return jnp.concatenate(
        [first * cosines - second * sines, second * cosines + first * sines], axis=-1
    )


def matmul_t(left, right):
    return lax.dot_general(
        left, right, (((0,), (0,)), ((), ())), preferred_element_type=jnp.float32
    )


def matmul_back(left, right):
    return lax.dot_general(
        left, right, (((1,), (1,)), ((), ())), preferred_element_type=jnp.float32
    )


def step_prep(step_raw, step_bias, log_rate):
    step = jax.nn.softplus(step_raw + step_bias)
    return (step, -step * jnp.exp(log_rate))


def conv_prep(conv_blocks, tails_in, filter_rows):
    count = conv_blocks.shape[1]
    extended = jnp.concatenate([tails_in, conv_blocks], axis=1)
    conv = filter_rows[KERNEL] + filter_rows[KERNEL - 1] * conv_blocks
    for tap_index in range(KERNEL - 1):
        conv = conv + filter_rows[tap_index] * extended[:, tap_index : tap_index + count]
    return jax.nn.silu(conv)


def ssd_emit(heads_x, b_in, step, log_decay):
    cumulative = jnp.cumsum(log_decay, axis=0)
    weight = jnp.exp(cumulative[-1][None, :] - cumulative) * step
    emitted = jnp.einsum("shp,sn->hpn", heads_x * weight[:, :, None], b_in, precision=HIGH)
    return (emitted, cumulative[-1])


def ssd_output(heads_x, b_in, c_in, step, log_decay, state_in, skip_gain):
    cumulative = jnp.cumsum(log_decay, axis=0)
    count = heads_x.shape[0]
    lower = (jnp.arange(count)[:, None] >= jnp.arange(count)[None, :])[:, :, None]
    gaps = jnp.where(lower, cumulative[:, None, :] - cumulative[None, :, :], 0.0)
    kernel = (
        jnp.where(lower, jnp.exp(gaps), 0.0) * jnp.dot(c_in, b_in.T, precision=HIGH)[:, :, None]
    )
    inner = jnp.einsum("tsh,shp->thp", kernel, heads_x * step[:, :, None], precision=HIGH)
    carried = (
        jnp.einsum("hpn,tn->thp", state_in, c_in, precision=HIGH) * jnp.exp(cumulative)[:, :, None]
    )
    return inner + carried + skip_gain[None, :, None] * heads_x


def chain_fold(slot_block, my_blocks, block_second, first_len, block_rows, prefix, later):

    def fold(total, piece, start):
        count = piece.shape[0]
        same = (slot_block * block_rows >= first_len)[None, :] == block_second[:, None]
        if later:
            valid = same & (slot_block[None, :] > my_blocks[:, None])
            gaps = (
                jnp.take(prefix, slot_block, axis=0)[None, :, :]
                - jnp.take(prefix, my_blocks + 1, axis=0)[:, None, :]
            )
        else:
            valid = same & (slot_block[None, :] < my_blocks[:, None])
            gaps = (
                jnp.take(prefix, my_blocks, axis=0)[:, None, :]
                - jnp.take(prefix, slot_block + 1, axis=0)[None, :, :]
            )
        factors = jnp.where(
            valid[:, :, None], jnp.exp(jnp.where(valid[:, :, None], gaps, 0.0)), 0.0
        )
        step_size = math.gcd(count, 8)

        def add_rows(index, running):
            rows_piece = lax.dynamic_slice_in_dim(piece, index * step_size, step_size).astype(
                jnp.float32
            )
            factor_rows = lax.dynamic_slice_in_dim(factors, index * step_size, step_size, 1)
            return running + jnp.einsum("bsh,shpn->bhpn", factor_rows, rows_piece, precision=HIGH)

        return lax.fori_loop(0, count // step_size, add_rows, total)

    return fold


def in_blocks(step_fn, carry, piece):
    count = piece.shape[0]
    block_size = math.gcd(count, 512)

    def visit(block_index, state):
        sub_piece = lax.dynamic_slice_in_dim(piece, block_index * block_size, block_size)
        return step_fn(state, sub_piece, block_index * block_size)

    return lax.fori_loop(0, count // block_size, visit, carry)


def on_device(
    block_input,
    out_cotangent,
    lengths,
    slot_block,
    norm_gains,
    short_filter,
    step_bias,
    log_rate,
    skip_gain,
    mixer_in,
    mixer_out,
    attend_in,
    attend_out,
    gate_up,
    down_weight,
):
    gains_all, in_mix, out_mix, in_attend, out_attend = (
        lax.all_gather(norm_gains, "wsh", axis=1, tiled=True),
        lax.all_gather(mixer_in, "wsh", axis=0, tiled=True),
        lax.all_gather(mixer_out, "wsh", axis=1, tiled=True),
        lax.all_gather(attend_in, "wsh", axis=0, tiled=True),
        lax.all_gather(attend_out, "wsh", axis=1, tiled=True),
    )
    ctx_count = lax.axis_size("ctx")
    block_count = 2 * ctx_count
    rows = block_input.shape[1]
    block_rows = rows // 2
    kv_width = KVH * HD
    scale = 1.0 / math.sqrt(HD)
    tokens = block_input[0]
    cotangent = out_cotangent[0]
    first_len = lengths[0, 0]
    logical_ids = jnp.arange(block_count, dtype=jnp.int32)
    my_blocks = lax.dynamic_slice_in_dim(slot_block, 2 * lax.axis_index("ctx"), 2)
    block_offsets = jnp.arange(block_rows, dtype=jnp.int32)
    my_pos = (my_blocks[:, None] * block_rows + block_offsets[None, :]).reshape(rows)
    my_second = my_pos >= first_len
    seq_pos = my_pos - jnp.where(my_second, first_len, 0)
    block_second = my_blocks * block_rows >= first_len
    is_start = (my_blocks == 0) | (my_blocks * block_rows == first_len)
    key_pos = (slot_block[:, None] * block_rows + block_offsets[None, :]).reshape(
        block_count * block_rows
    )
    gain_first = gains_all[0].astype(jnp.float32)
    gain_second = gains_all[1].astype(jnp.float32)
    normed, first_norm_vjp = jax.vjp(rms_norm, tokens, gain_first)
    normed_first = normed.astype(jnp.bfloat16)
    mixed = jnp.dot(normed_first, in_mix, preferred_element_type=jnp.float32)
    gate_z = mixed[:, :DSSM]
    conv_input = mixed[:, DSSM : DSSM + CONV]
    step_raw = mixed[:, DSSM + CONV :]
    (step, log_decay), step_vjp = jax.vjp(step_prep, step_raw, step_bias, log_rate)
    step_blocks = step.reshape(2, block_rows, MHEADS)
    decay_blocks = log_decay.reshape(2, block_rows, MHEADS)
    totals = jnp.sum(decay_blocks, axis=1)
    conv_blocks = conv_input.reshape(2, block_rows, CONV)
    tails = conv_blocks[:, block_rows - (KERNEL - 1) :, :]
    all_tails, all_totals = (
        lax.all_gather(tails, "ctx", axis=0, tiled=True),
        lax.all_gather(totals, "ctx", axis=0, tiled=True),
    )
    one_hot = (slot_block[None, :] == logical_ids[:, None]).astype(jnp.float32)
    totals_logical = jnp.dot(one_hot, all_totals, precision=HIGH)
    prefix = jnp.concatenate(
        [jnp.zeros((1, MHEADS), jnp.float32), jnp.cumsum(totals_logical, axis=0)], axis=0
    )
    pred_slot = jnp.sum(
        jnp.where(slot_block[None, :] == (my_blocks - 1)[:, None], logical_ids[None, :], 0), axis=1
    )
    keep_tail = jnp.where(is_start, 0.0, 1.0).astype(jnp.float32)
    tails_in = jnp.take(all_tails, pred_slot, axis=0) * keep_tail[:, None, None]
    activated, conv_vjp = jax.vjp(conv_prep, conv_blocks, tails_in, short_filter)
    heads_x = activated[:, :, :DSSM].reshape(2, block_rows, MHEADS, HEAD_M)
    b_in = activated[:, :, DSSM : DSSM + NSTATE]
    c_in = activated[:, :, DSSM + NSTATE :]
    (emitted, emit_totals), emit_vjp = jax.vjp(
        jax.vmap(ssd_emit), heads_x, b_in, step_blocks, decay_blocks
    )
    zero_states = jnp.zeros((2, MHEADS, HEAD_M, NSTATE), jnp.float32)
    chain_forward = chain_fold(
        slot_block, my_blocks, block_second, first_len, block_rows, prefix, False
    )
    state_in = chain_forward(
        zero_states,
        lax.all_gather(emitted.astype(jnp.bfloat16), "ctx", axis=0, tiled=True),
        jnp.int32(0),
    )
    mixer_y, out_vjp = jax.vjp(
        jax.vmap(ssd_output, in_axes=(0, 0, 0, 0, 0, 0, None)),
        heads_x,
        b_in,
        c_in,
        step_blocks,
        decay_blocks,
        state_in,
        skip_gain,
    )
    mixer_flat = mixer_y.reshape(rows, DSSM)
    gated = (mixer_flat * jax.nn.silu(gate_z)).astype(jnp.bfloat16)
    mixer_branch = jnp.dot(gated, out_mix, preferred_element_type=jnp.float32)
    projected = jnp.dot(normed_first, in_attend, preferred_element_type=jnp.float32)
    cosines, sines = rope_tables(seq_pos)
    queries = rotate(projected[:, :AQ].reshape(rows, QH, HD), cosines, sines).astype(jnp.bfloat16)
    keys_rot = rotate(
        projected[:, AQ : AQ + kv_width].reshape(rows, KVH, HD), cosines, sines
    ).astype(jnp.bfloat16)
    values = projected[:, AQ + kv_width :].astype(jnp.bfloat16)
    kv_local = jnp.concatenate([keys_rot.reshape(rows, kv_width), values], axis=1)
    query_heads = queries.reshape(rows, KVH, GRP, HD)

    def allowed_at(start, count):
        piece_pos = lax.dynamic_slice_in_dim(key_pos, start, count)
        return (piece_pos[None, :] <= my_pos[:, None]) & (
            (piece_pos >= first_len)[None, :] == my_second[:, None]
        )

    def split_piece(piece):
        count = piece.shape[0]
        return (
            piece[:, :kv_width].reshape(count, KVH, HD),
            piece[:, kv_width:].reshape(count, KVH, HD),
        )

    def attend_step(carry, piece, start):
        top, denominator, running = carry
        keys_piece, values_piece = split_piece(piece)
        allowed = allowed_at(start, piece.shape[0])
        scores = (
            jnp.einsum(
                "tkgd,skd->kgts", query_heads, keys_piece, preferred_element_type=jnp.float32
            )
            * scale
        )
        masked = jnp.where(allowed, scores, NEG_LARGE)
        new_top = jnp.maximum(top, jnp.max(masked, axis=-1))
        weights = jnp.where(allowed, jnp.exp(masked - new_top[..., None]), 0.0)
        factor = jnp.exp(top - new_top)
        denominator = denominator * factor + jnp.sum(weights, axis=-1)
        running = running * factor[..., None] + jnp.einsum(
            "kgts,skd->kgtd", weights, values_piece.astype(jnp.float32), precision=HIGH
        )
        return (new_top, denominator, running)

    start_carry = (
        jnp.full((KVH, GRP, rows), NEG_LARGE, jnp.float32),
        jnp.zeros((KVH, GRP, rows), jnp.float32),
        jnp.zeros((KVH, GRP, rows, HD), jnp.float32),
    )
    top, denominator, running = in_blocks(
        attend_step, start_carry, lax.all_gather(kv_local, "ctx", axis=0, tiled=True)
    )
    log_total = top + jnp.log(denominator)
    attn_heads = running / denominator[..., None]
    attn_rows = jnp.transpose(attn_heads, (2, 0, 1, 3)).reshape(rows, AQ)
    attn_b = attn_rows.astype(jnp.bfloat16)
    attn_branch = jnp.dot(attn_b, out_attend, preferred_element_type=jnp.float32)
    hidden = tokens + mixer_branch + attn_branch
    normed2, second_norm_vjp = jax.vjp(rms_norm, hidden, gain_second)
    normed_second = normed2.astype(jnp.bfloat16)
    cot_b = cotangent.astype(jnp.bfloat16)
    gate_whole, down_rows = (
        lax.all_gather(gate_up, "wsh", axis=2, tiled=True),
        lax.all_gather(down_weight, "wsh", axis=0, tiled=True),
    )
    gate_cols = gate_whole[0]
    up_cols = gate_whole[1]
    gate_part = jnp.dot(normed_second, gate_cols, preferred_element_type=jnp.float32)
    up_part = jnp.dot(normed_second, up_cols, preferred_element_type=jnp.float32)
    mlp_act = (jax.nn.silu(gate_part) * up_part).astype(jnp.bfloat16)
    mlp_out = jnp.dot(mlp_act, down_rows, preferred_element_type=jnp.float32)
    output = hidden + mlp_out
    down_local = matmul_t(mlp_act, cot_b)
    d_mlp = matmul_back(cot_b, down_rows)
    d_gate = (d_mlp * up_part * silu_slope(gate_part)).astype(jnp.bfloat16)
    d_up = (d_mlp * jax.nn.silu(gate_part)).astype(jnp.bfloat16)
    gate_up_local = jnp.stack(
        [matmul_t(normed_second, d_gate), matmul_t(normed_second, d_up)], axis=0
    )
    d_normed_second = matmul_back(d_gate, gate_cols) + matmul_back(d_up, up_cols)
    d_hidden_norm, d_gain_second = second_norm_vjp(d_normed_second)
    hidden_grad = cotangent + d_hidden_norm
    hidden_b = hidden_grad.astype(jnp.bfloat16)
    attend_out_grad = matmul_t(attn_b, hidden_b)
    mixer_out_grad = matmul_t(gated, hidden_b)
    d_attn_b = matmul_back(hidden_b, out_attend).astype(jnp.bfloat16)
    d_gated = matmul_back(hidden_b, out_mix)
    d_heads = d_attn_b.reshape(rows, KVH, GRP, HD)
    d_heads_f = d_heads.astype(jnp.float32)
    query_f = queries.astype(jnp.float32).reshape(rows, KVH, GRP, HD)
    delta = jnp.sum(jnp.transpose(d_heads_f, (1, 2, 0, 3)) * attn_heads, axis=-1)

    def attend_back(carry, piece, start):
        query_grad, kv_grad = carry
        count = piece.shape[0]
        keys_piece, values_piece = split_piece(piece)
        allowed = allowed_at(start, count)
        scores = (
            jnp.einsum(
                "tkgd,skd->kgts", query_heads, keys_piece, preferred_element_type=jnp.float32
            )
            * scale
        )
        probs = jnp.where(
            allowed, jnp.exp(jnp.where(allowed, scores, 0.0) - log_total[..., None]), 0.0
        )
        d_probs = jnp.einsum(
            "tkgd,skd->kgts", d_heads, values_piece, preferred_element_type=jnp.float32
        )
        d_scores = probs * (d_probs - delta[..., None]) * scale
        query_grad = query_grad + jnp.einsum(
            "kgts,skd->tkgd", d_scores, keys_piece.astype(jnp.float32), precision=HIGH
        )
        key_grad = jnp.einsum("kgts,tkgd->skd", d_scores, query_f, precision=HIGH)
        value_grad = jnp.einsum("kgts,tkgd->skd", probs, d_heads_f, precision=HIGH)
        update = jnp.concatenate(
            [key_grad.reshape(count, kv_width), value_grad.reshape(count, kv_width)], axis=1
        )
        kv_grad = lax.dynamic_update_slice_in_dim(kv_grad, update, start, 0)
        return (query_grad, kv_grad)

    back_carry = (
        jnp.zeros((rows, KVH, GRP, HD), jnp.float32),
        jnp.zeros((block_count * block_rows, 2 * kv_width), jnp.float32),
    )
    query_grad, kv_grad = in_blocks(
        attend_back, back_carry, lax.all_gather(kv_local, "ctx", axis=0, tiled=True)
    )
    d_mixer = (d_gated * jax.nn.silu(gate_z)).reshape(2, block_rows, MHEADS, HEAD_M)
    d_z = d_gated * mixer_flat * silu_slope(gate_z)
    g_heads, g_b, g_c, g_step, g_decay, g_state, g_skip = out_vjp(d_mixer)
    chain_backward = chain_fold(
        slot_block, my_blocks, block_second, first_len, block_rows, prefix, True
    )
    later_sum = chain_backward(
        zero_states,
        lax.all_gather(g_state.astype(jnp.bfloat16), "ctx", axis=0, tiled=True),
        jnp.int32(0),
    )
    d_totals = jnp.exp(emit_totals) * jnp.sum(later_sum * state_in, axis=(2, 3))
    e_heads, e_b, e_step, e_decay = emit_vjp((later_sum, d_totals))
    d_activated = jnp.concatenate(
        [(g_heads + e_heads).reshape(2, block_rows, DSSM), g_b + e_b, g_c], axis=2
    )
    d_conv_blocks, d_tails, filter_grad = conv_vjp(d_activated)
    tail_buffer = (
        jnp.zeros((block_count, KERNEL - 1, CONV), jnp.float32)
        .at[pred_slot]
        .add(d_tails * keep_tail[:, None, None])
    )
    d_step_raw, step_bias_grad, log_rate_grad = step_vjp(
        ((g_step + e_step).reshape(rows, MHEADS), (g_decay + e_decay).reshape(rows, MHEADS))
    )
    kv_mine, tail_back, gate_up_part, down_part = (
        lax.psum_scatter(
            kv_grad.astype(jnp.bfloat16), "ctx", scatter_dimension=0, tiled=True
        ).astype(jnp.float32),
        lax.psum_scatter(
            tail_buffer.astype(jnp.bfloat16), "ctx", scatter_dimension=0, tiled=True
        ).astype(jnp.float32),
        lax.psum_scatter(
            gate_up_local.astype(jnp.bfloat16), "ctx", scatter_dimension=1, tiled=True
        ).astype(jnp.float32),
        lax.psum_scatter(
            down_local.astype(jnp.bfloat16), "ctx", scatter_dimension=1, tiled=True
        ).astype(jnp.float32),
    )
    d_query = rotate(query_grad.reshape(rows, QH, HD), cosines, -sines).reshape(rows, AQ)
    d_key = rotate(kv_mine[:, :kv_width].reshape(rows, KVH, HD), cosines, -sines).reshape(
        rows, kv_width
    )
    d_attend = jnp.concatenate([d_query, d_key, kv_mine[:, kv_width:]], axis=1).astype(jnp.bfloat16)
    attend_in_grad = matmul_t(normed_first, d_attend)
    d_normed_attend = matmul_back(d_attend, in_attend)
    d_conv_blocks = d_conv_blocks.at[:, block_rows - (KERNEL - 1) :, :].add(tail_back)
    d_mixed = jnp.concatenate([d_z, d_conv_blocks.reshape(rows, CONV), d_step_raw], axis=1).astype(
        jnp.bfloat16
    )
    mixer_in_grad = matmul_t(normed_first, d_mixed)
    d_normed_mix = matmul_back(d_mixed, in_mix)
    d_tokens_norm, d_gain_first = first_norm_vjp(d_normed_mix + d_normed_attend)
    input_grad = hidden_grad + d_tokens_norm
    gains_grad = jnp.stack([d_gain_first, d_gain_second], axis=0)
    step_bias_grad, log_rate_grad, skip_grad, filter_grad = lax.psum(
        (step_bias_grad, log_rate_grad, g_skip, filter_grad), ("ctx", "wsh")
    )
    gate_up_grad, down_grad = (
        lax.psum_scatter(
            gate_up_part.astype(jnp.bfloat16), "wsh", scatter_dimension=2, tiled=True
        ).astype(jnp.float32),
        lax.psum_scatter(
            down_part.astype(jnp.bfloat16), "wsh", scatter_dimension=0, tiled=True
        ).astype(jnp.float32),
    )
    results = (
        lax.psum_scatter(gains_grad, ("ctx", "wsh"), scatter_dimension=1, tiled=True),
        lax.psum_scatter(mixer_in_grad, ("ctx", "wsh"), scatter_dimension=0, tiled=True),
        lax.psum_scatter(mixer_out_grad, ("ctx", "wsh"), scatter_dimension=1, tiled=True),
        lax.psum_scatter(attend_in_grad, ("ctx", "wsh"), scatter_dimension=0, tiled=True),
        lax.psum_scatter(attend_out_grad, ("ctx", "wsh"), scatter_dimension=1, tiled=True),
    )
    return (
        output[None],
        input_grad[None],
        results[0],
        filter_grad,
        step_bias_grad,
        log_rate_grad,
        skip_grad,
        results[1],
        results[2],
        results[3],
        results[4],
        gate_up_grad,
        down_grad,
    )


def solution(mesh):
    placed = (
        P("wsh", "ctx", None),
        P("wsh", "ctx", None),
        P("wsh", None),
        P(),
        P(None, "wsh"),
        P(),
        P(),
        P(),
        P(),
        P("wsh", None),
        P(None, "wsh"),
        P("wsh", None),
        P(None, "wsh"),
        P(None, None, "wsh"),
        P("wsh", None),
    )
    return jax.shard_map(
        on_device,
        mesh=mesh,
        in_specs=placed,
        out_specs=(
            P("wsh", "ctx", None),
            P("wsh", "ctx", None),
            P(None, ("ctx", "wsh")),
            P(),
            P(),
            P(),
            P(),
            P(("ctx", "wsh"), None),
            P(None, ("ctx", "wsh")),
            P(("ctx", "wsh"), None),
            P(None, ("ctx", "wsh")),
            P(None, "ctx", "wsh"),
            P("wsh", "ctx"),
        ),
        check_vma=False,
    )
```

profile of v0, /device:TPU:8, one launch (start us, length us, event | category | flops | bytes accessed | tf_op | source)
XLA Modules:
  0.0 1562.8 jit_solution(14601998179931562253)
XLA Ops:
  9.6 8.2 all_gather.37
  20.2 111.9 %all-gather.10.cloned.1.call-done = bf16[1024,3352]{0,1:T(8,128)(2,1)} async-done(((bf16[256,3352]{0,1:T(8,128)(2,1)}), bf16[1024,3352]{0,1:T(8,128)(2,1)}) %all-gather.10.cloned.1.call-update) | async-done | bytes 6864912 | tf_op jit(solution)/shard_map/all_gather | solution.py:165
  132.0 5.0 fusion.192
  140.8 9.9 all_gather.39
  173.0 9.8 all_gather.44
  183.9 14.5 while.69
  201.4 9.5 all-gather
  220.5 15.2 while.67
  223.1 5.0 bitcast_add_fusion.5
  246.1 33.8 %all-gather.14.cloned.1.call-done = bf16[1536,1024]{1,0:T(8,128)(2,1)} async-done(((bf16[1536,256]{1,0:T(8,128)(2,1)}), bf16[1536,1024]{1,0:T(8,128)(2,1)}) %all-gather.14.cloned.1.call-update) | async-done | bytes 3145744 | tf_op jit(solution)/shard_map/all_gather | solution.py:166
  282.4 31.0 %all-gather.18.cloned.1.call-done = bf16[512,1024]{1,0:T(8,128)(2,1)} async-done(((bf16[512,256]{1,0:T(8,128)(2,1)}), bf16[512,1024]{1,0:T(8,128)(2,1)}) %all-gather.18.cloned.1.call-update) | async-done | bytes 1048592 | tf_op jit(solution)/shard_map/all_gather | solution.py:168
  315.3 143.6 %all-gather.20.cloned.1.call-done = bf16[2,1024,2048]{2,1,0:T(8,128)(2,1)} async-done(((bf16[2,1024,512]{2,1,0:T(8,128)(2,1)}), bf16[2,1024,2048]{2,1,0:T(8,128)(2,1)}) %all-gather.20.cloned.1.call-update) | async-done | bytes 8388624 | tf_op jit(solution)/shard_map/all_gather | solution.py:308
  466.7 73.0 %all-gather.22.cloned.1.call-done = bf16[2048,1024]{1,0:T(8,128)(2,1)} async-done(((bf16[512,1024]{1,0:T(8,128)(2,1)}), bf16[2048,1024]{1,0:T(8,128)(2,1)}) %all-gather.22.cloned.1.call-update) | async-done | bytes 4194320 | tf_op jit(solution)/shard_map/all_gather | solution.py:309
  539.7 5.3 multiply_convert_fusion
  570.8 26.0 %while.70 = (s32[]{:T(128)}, f32[128,2,4,64]{0,3,2,1:T(8,128)}, bf16[1024,256]{0,1:T(8,128)(2,1)}, bf16[1024,256]{0,1:T(8,128)(2,1)S(1)}, s32[1024]{0:T(1024)}, ...) while((s32[]{:T(128)}, f32[128,2,4,64]{0,3,2,1:T(8,128)}, ...), condition=%wide.region_29.32_spmd.clone.clone.clone, body=%wide.region_28.31_spmd.clone.clone.clone.sunk | while | flops 1346700032 | bytes 36718788 | solution.py:143
  602.4 6.6 copy.300
  631.5 18.4 %while.68 = (s32[]{:T(128)}, f32[2,24,64,128]{3,0,2,1:T(2,128)}, bf16[16,24,64,128]{3,2,1,0:T(8,128)(2,1)}, f32[2,16,24]{1,0,2:T(2,128)S(1)}, s32[]{:T(128)}, /*index=5*/s32[]{:T(128)}, s32[]{:T(128)}, s32[]{:T(128)}) while((s32[]{:T(128)}, f32[2,24,64,128]{3,0,2,1:T(2,128)}, bf16[16,24,64,128]{3,2,1,0:T(8,128)(2,1)}, ...), condition=%wide.region_14.17_spmd.clone, body=%wide.region_13.16_spmd.clone.sunk | while | flops 38535176 | bytes 25169108 | solution.py:130
  634.6 5.1 bitcast_add_fusion.6
  643.6 5.1 bitcast_add_fusion.6
  649.9 5.6 multiply_reduce_fusion.2
  669.5 7.7 pad_maximum_fusion
  686.5 16.8 %reduce-scatter.35.cloned.1.call-done = bf16[128,2048]{1,0:T(8,128)(2,1)} async-done(((bf16[1024,2048]{1,0:T(8,128)(2,1)}), bf16[128,2048]{1,0:T(8,128)(2,1)}) %reduce-scatter.35.cloned.1.call-update) | async-done | bytes 524304
  711.7 47.7 %all-reduce.15.cloned.1.call-done = bf16[16,3,1792]{2,1,0:T(4,128)(2,1)} async-done(((bf16[16,3,1792]{2,1,0:T(4,128)(2,1)}), bf16[16,3,1792]{2,1,0:T(4,128)(2,1)}) %all-reduce.15.cloned.1.call-update) | async-done | bytes 172048
  767.1 67.8 %reduce-scatter.25.cloned.1.call-done = bf16[2,128,2048]{2,1,0:T(8,128)(2,1)} async-done(((bf16[2,1024,2048]{2,1,0:T(8,128)(2,1)}), bf16[2,128,2048]{2,1,0:T(8,128)(2,1)}) %reduce-scatter.25.cloned.1.call-update) | async-done | bytes 1048592 | tf_op jit(solution)/shard_map/reduce_scatter | solution.py:406
  844.8 7.1 fusion.132
  858.8 42.3 %all-reduce.12 = (f32[5,1792]{1,0:T(8,128)}, f32[24]{0:T(128)}, f32[24]{0:T(128)}, f32[24]{0:T(128)}) all-reduce(f32[5,1792]{1,0:T(8,128)S(1)} %pad_add_fusion.2, f32[24]{0:T(128)S(1)} %get-tuple-element.1048, f32[24]{0:T(128)S(1)} %exponential_multiply_fusion.1, f32[24]{0:T(128)S(1)} %reduce_sum.303), channel_id=1, replica_groups=mesh['ctx'=8,'wsh'=4] {'ctx','wsh'}, use_global_device_ids=true, to_apply=%region_40.43 | all-reduce | flops 9032 | bytes 72256 | tf_op jit(solution)/shard_map/psum | solution.py:429
  902.1 89.2 %reduce-scatter.33.cloned.1.call-done = f32[32,2]{1,0:T(8,128)} async-done(((f32[1024,2]{1,0:T(8,128)}), f32[32,2]{1,0:T(8,128)}) %reduce-scatter.33.cloned.1.call-update) | async-done | bytes 272
  992.6 26.9 %reduce-scatter.27.cloned.1.call-done = bf16[2,128,512]{2,1,0:T(8,128)(2,1)} async-done(((bf16[2,128,2048]{2,1,0:T(8,128)(2,1)}), bf16[2,128,512]{2,1,0:T(8,128)(2,1)}) %reduce-scatter.27.cloned.1.call-update) | async-done | bytes 262160 | tf_op jit(solution)/shard_map/reduce_scatter | solution.py:433
  1021.3 138.6 %reduce-scatter.23.cloned.1.call-done = f32[512,32]{0,1:T(8,128)} async-done(((f32[512,1024]{0,1:T(8,128)}), f32[512,32]{0,1:T(8,128)}) %reduce-scatter.23.cloned.1.call-update) | async-done | bytes 65552 | tf_op jit(solution)/shard_map/reduce_scatter | solution.py:445
  1159.8 108.4 %reduce-scatter.21.cloned.1.call-done = f32[32,768]{1,0:T(8,128)} async-done(((f32[1024,768]{1,0:T(8,128)}), f32[32,768]{1,0:T(8,128)}) %reduce-scatter.21.cloned.1.call-update) | async-done | bytes 98320 | tf_op jit(solution)/shard_map/reduce_scatter | solution.py:444
  1268.2 119.9 %reduce-scatter.19.cloned.1.call-done = f32[1536,32]{0,1:T(8,128)} async-done(((f32[1536,1024]{0,1:T(8,128)}), f32[1536,32]{0,1:T(8,128)}) %reduce-scatter.19.cloned.1.call-update) | async-done | bytes 196624 | tf_op jit(solution)/shard_map/reduce_scatter | solution.py:443
  1388.1 167.9 %reduce-scatter.17.cloned.1.call-done = f32[32,3352]{1,0:T(8,128)} async-done(((f32[1024,3352]{1,0:T(8,128)}), f32[32,3352]{1,0:T(8,128)}) %reduce-scatter.17.cloned.1.call-update) | async-done | bytes 429072 | tf_op jit(solution)/shard_map/reduce_scatter | solution.py:442
  (620 shorter events, 236.6 us)
Async XLA Ops:
  7.2 124.8 %all-gather.10.cloned.1.call-start = ((), (), s32[]{:S(2)}) async-start(), calls=%async_computation.10 | async-start | bytes 8581120 | tf_op jit(solution)/shard_map/all_gather | solution.py:165
  8.0 162.9 %all-gather.16.cloned.1.call-start = ((), (), s32[]{:S(2)}) async-start(), calls=%async_computation.13 | async-start | bytes 1966080 | tf_op jit(solution)/shard_map/all_gather | solution.py:167
  8.7 211.8 %all-gather.12.cloned.1.call-start = ((), (), s32[]{:S(2)}) async-start(), calls=%async_computation.11 | async-start | bytes 7077888 | tf_op jit(solution)/shard_map/all_gather | solution.py:231
  9.6 127.4 %copy-start.139 = (s32[2]{0:T(128)}, s32[2]{0:T(128)S(1)}, u32[]{:S(2)}) copy-start(s32[2]{0:T(128)S(1)} %fusion.162) | copy-start | bytes 28
  18.4 118.6 %copy-start.109 = (f32[1,1024]{1,0:T(1,128)}, f32[1,1024]{1,0:T(1,128)S(1)}, u32[]{:S(2)}) copy-start(f32[1,1024]{1,0:T(1,128)S(1)} %get-tuple-element.1096) | copy-start | bytes 12292
  18.6 118.4 %copy-start.128 = (f32[128]{0:T(128)}, f32[128]{0:T(128)S(1)}, u32[]{:S(2)}) copy-start(f32[128]{0:T(128)S(1)} %fusion.163) | copy-start | bytes 1540
  19.8 131.4 %copy-start.137 = (f32[2]{0:T(128)}, f32[2]{0:T(128)S(1)}, u32[]{:S(2)}) copy-start(f32[2]{0:T(128)S(1)} %or_select_fusion) | copy-start | bytes 28
  20.0 131.4 %copy-start.102 = (f32[1792]{0:T(1024)}, f32[1792]{0:T(1024)S(1)}, u32[]{:S(2)}) copy-start(f32[1792]{0:T(1024)S(1)} %get-tuple-element.973) | copy-start | bytes 21508
  20.0 131.4 %copy-start.103 = (f32[1792]{0:T(1024)}, f32[1792]{0:T(1024)S(1)}, u32[]{:S(2)}) copy-start(f32[1792]{0:T(1024)S(1)} %get-tuple-element.972) | copy-start | bytes 21508
  20.0 131.4 %copy-start.105 = (f32[1792]{0:T(1024)}, f32[1792]{0:T(1024)S(1)}, u32[]{:S(2)}) copy-start(f32[1792]{0:T(1024)S(1)} %get-tuple-element.974) | copy-start | bytes 21508
  20.0 131.4 %copy-start.107 = (f32[1792]{0:T(1024)}, f32[1792]{0:T(1024)S(1)}, u32[]{:S(2)}) copy-start(f32[1792]{0:T(1024)S(1)} %get-tuple-element.975) | copy-start | bytes 21508
  20.0 134.4 %copy-start.135 = (f32[24]{0:T(128)}, f32[24]{0:T(128)S(1)}, u32[]{:S(2)}) copy-start(f32[24]{0:T(128)S(1)} %exp.86) | copy-start | bytes 292
  20.1 150.8 %copy-start.29 = (bf16[128,1024]{1,0:T(8,128)(2,1)}, bf16[128,1024]{1,0:T(8,128)(2,1)S(1)}, u32[]{:S(2)}) copy-start(bf16[128,1024]{1,0:T(8,128)(2,1)S(1)} %multiply_convert_fusion.6) | copy-start | bytes 786436
  160.9 119.0 %all-gather.14.cloned.1.call-start = ((), (), s32[]{:S(2)}) async-start(), calls=%async_computation.12 | async-start | bytes 3932160 | tf_op jit(solution)/shard_map/all_gather | solution.py:166
  161.5 152.0 %all-gather.18.cloned.1.call-start = ((), (), s32[]{:S(2)}) async-start(), calls=%async_computation.14 | async-start | bytes 1310720 | tf_op jit(solution)/shard_map/all_gather | solution.py:168
  162.0 296.8 %all-gather.20.cloned.1.call-start = ((), (), s32[]{:S(2)}) async-start(), calls=%async_computation.15 | async-start | bytes 10485760 | tf_op jit(solution)/shard_map/all_gather | solution.py:308
  162.6 377.0 %all-gather.22.cloned.1.call-start = ((), (), s32[]{:S(2)}) async-start(), calls=%async_computation.16 | async-start | bytes 5242880 | tf_op jit(solution)/shard_map/all_gather | solution.py:309
  163.4 468.1 %all-gather.24.cloned.1.call-start = ((), (), s32[]{:S(2)}) async-start(), calls=%async_computation.17 | async-start | bytes 7077888 | tf_op jit(solution)/shard_map/all_gather | solution.py:382
  199.6 113.9 %copy-start.58 = (bf16[2,4,128,64]{2,3,1,0:T(8,128)(2,1)}, bf16[2,4,128,64]{2,3,1,0:T(8,128)(2,1)S(1)}, u32[]{:S(2)}) copy-start(bf16[2,4,128,64]{2,3,1,0:T(8,128)(2,1)S(1)} %fusion.136) | copy-start | bytes 393220
  315.1 238.7 %copy-start.19 = (f32[128,1024]{1,0:T(8,128)}, f32[128,1024]{1,0:T(8,128)S(1)}, u32[]{:S(2)}) copy-start(f32[128,1024]{1,0:T(8,128)S(1)} %get-tuple-element.1114) | copy-start | bytes 1572868
  315.3 147.5 %copy-start.38 = (bf16[128,1024]{1,0:T(8,128)(2,1)}, bf16[128,1024]{1,0:T(8,128)(2,1)S(1)}, u32[]{:S(2)}) copy-start(bf16[128,1024]{1,0:T(8,128)(2,1)S(1)} %multiply_convert_fusion.5) | copy-start | bytes 786436
  564.9 119.3 %reduce-scatter.31.cloned.1.call-start = ((), (), s32[]{:S(2)}) async-start(), calls=%async_computation.25 | async-start | bytes 589824
  599.0 104.3 %reduce-scatter.35.cloned.1.call-start = ((), (), s32[]{:S(2)}) async-start(), calls=%async_computation.27 | async-start | bytes 4718592
  609.0 150.5 %all-reduce.15.cloned.1.call-start = ((), (), s32[]{:S(2)}) async-start(), calls=%async_computation.28 | async-start | bytes 458752
  669.4 165.5 %reduce-scatter.25.cloned.1.call-start = ((), (), s32[]{:S(2)}) async-start(), calls=%async_computation.22 | async-start | bytes 9437184 | tf_op jit(solution)/shard_map/reduce_scatter | solution.py:406
  677.2 179.8 %reduce-scatter.29.cloned.1.call-start = ((), (), s32[]{:S(2)}) async-start(), calls=%async_computation.24 | async-start | bytes 655360 | tf_op jit(solution)/shard_map/reduce_scatter | solution.py:436
  705.4 285.9 %reduce-scatter.33.cloned.1.call-start = ((), (), s32[]{:S(2)}) async-start(), calls=%async_computation.26 | async-start | bytes 540672
  767.1 252.4 %reduce-scatter.27.cloned.1.call-start = ((), (), s32[]{:S(2)}) async-start(), calls=%async_computation.23 | async-start | bytes 1310720 | tf_op jit(solution)/shard_map/reduce_scatter | solution.py:433
  835.0 324.9 %reduce-scatter.23.cloned.1.call-start = ((), (), s32[]{:S(2)}) async-start(), calls=%async_computation.21 | async-start | bytes 2162688 | tf_op jit(solution)/shard_map/reduce_scatter | solution.py:445
  836.8 431.3 %reduce-scatter.21.cloned.1.call-start = ((), (), s32[]{:S(2)}) async-start(), calls=%async_computation.20 | async-start | bytes 3244032 | tf_op jit(solution)/shard_map/reduce_scatter | solution.py:444
  840.2 548.0 %reduce-scatter.19.cloned.1.call-start = ((), (), s32[]{:S(2)}) async-start(), calls=%async_computation.19 | async-start | bytes 6488064 | tf_op jit(solution)/shard_map/reduce_scatter | solution.py:443
  844.8 711.3 %reduce-scatter.17.cloned.1.call-start = ((), (), s32[]{:S(2)}) async-start(), calls=%async_computation.18 | async-start | bytes 14598144 | tf_op jit(solution)/shard_map/reduce_scatter | solution.py:442
  (155 other events, 1090.6 us)
Sparse Core Ops, SparseCore 0:
  9.6 122.3 all-gather.9
  133.6 37.2 all-gather.15
  172.8 45.1 all-gather.11
  219.4 60.4 all-gather.13
  281.3 32.1 all-gather.17
  314.9 143.8 all-gather.19
  460.4 79.2 all-gather.21
  565.0 46.5 all-gather.23
  614.7 34.1 reduce-scatter.30
  652.1 51.1 reduce-scatter.34
  706.9 52.4 all-reduce.14
  762.7 72.1 reduce-scatter.24
  837.2 18.6 reduce-scatter.28
  858.0 133.1 reduce-scatter.32
  993.4 26.0 reduce-scatter.26
  1022.2 137.6 reduce-scatter.22
  1165.7 102.4 reduce-scatter.20
  1274.2 113.8 reduce-scatter.18
  1394.7 161.2 reduce-scatter.16
where the time goes:
time: 1580 us; the launch traced here: 1560 us
  waiting for transfers between devices  1180 us (75%)
  matrix products  154 us (10%)
  blocking collectives  79.8 us (5%)
  local copies, waits for them, and re-layouts  75.8 us (5%)
  other arithmetic  54.5 us (3%)
  between operations  16.8 us (1%)
    reduce_scatter x1, waiting for transfers between devices, on_device(): lax.psum_scatter(mixer_in_grad, ('ctx', 'wsh'), scatter_dimension=0, tile...  168 us
    unnamed x23, waiting for transfers between devices  157 us
    all_gather x1, waiting for transfers between devices, on_device(): lax.all_gather(gate_up, 'wsh', axis=2, tiled=True)  144 us
    reduce_scatter x1, waiting for transfers between devices, on_device(): lax.psum_scatter(attend_out_grad, ('ctx', 'wsh'), scatter_dimension=1, ti...  139 us
    reduce_scatter x1, waiting for transfers between devices, on_device(): lax.psum_scatter(mixer_out_grad, ('ctx', 'wsh'), scatter_dimension=1, til...  120 us
    all_gather x1, waiting for transfers between devices, on_device(): lax.all_gather(mixer_in, 'wsh', axis=0, tiled=True)  112 us
    reduce_scatter x1, waiting for transfers between devices, on_device(): lax.psum_scatter(attend_in_grad, ('ctx', 'wsh'), scatter_dimension=0, til...  108 us
    all_gather x1, waiting for transfers between devices, on_device(): lax.all_gather(down_weight, 'wsh', axis=0, tiled=True)  73 us
  transfers between devices with their start and end apart: 19, of which 15 were waited for; matrix products, arithmetic and copies ran while one was open for 15% of the time, Pallas kernels for 0%

commit v1 on v0

--- a/solution.py
+++ b/solution.py
@@ -461,6 +461,464 @@
     )
 
 
+def xor_pairs(count, bits):
+    return [(index, index ^ bits) for index in range(count)]
+
+
+def gather_ctx(values):
+    count = lax.axis_size("ctx")
+    first_core = lax.axis_index("ctx") % 2 == 0
+    near_x = lax.ppermute(values, "ctx", xor_pairs(count, 2))
+    near_y = lax.ppermute(values, "ctx", xor_pairs(count, 4))
+    far = lax.ppermute(
+        jnp.where(first_core, near_x, near_y),
+        "ctx",
+        [(index, index ^ (4 if index % 2 == 0 else 2)) for index in range(count)],
+    )
+    mine = [values, near_x, near_y, far]
+    other = [lax.ppermute(piece, "ctx", xor_pairs(count, 1)) for piece in mine]
+    return jnp.stack([piece for pair in zip(mine, other) for piece in pair], axis=0)
+
+
+def scatter_ctx(parts):
+    count = lax.axis_size("ctx")
+    first_core = lax.axis_index("ctx") % 2 == 0
+    wire = lambda piece: piece.astype(jnp.bfloat16)
+    sums = [
+        parts[k] + lax.ppermute(wire(parts[k + 1]), "ctx", xor_pairs(count, 1)).astype(jnp.float32)
+        for k in (6, 2, 4, 0)
+    ]
+    far, near_x, near_y, own = sums
+    passed = lax.ppermute(
+        wire(far), "ctx", [(index, index ^ (2 if index % 2 == 0 else 4)) for index in range(count)]
+    ).astype(jnp.float32)
+    near_y = near_y + jnp.where(first_core, passed, 0.0)
+    near_x = near_x + jnp.where(first_core, 0.0, passed)
+    return (
+        own
+        + lax.ppermute(wire(near_x), "ctx", xor_pairs(count, 2)).astype(jnp.float32)
+        + lax.ppermute(wire(near_y), "ctx", xor_pairs(count, 4)).astype(jnp.float32)
+    )
+
+
+def swap_all(parts, axis_name):
+    count = lax.axis_size(axis_name)
+    return [parts[0]] + [
+        lax.ppermute(parts[k], axis_name, xor_pairs(count, k)) for k in range(1, count)
+    ]
+
+
+def natural(stacked, axis_name):
+    count = lax.axis_size(axis_name)
+    order = lax.axis_index(axis_name) ^ jnp.arange(count, dtype=jnp.int32)
+    return jnp.take(stacked, order, axis=0, mode="clip")
+
+
+def gather_wsh(values):
+    count = lax.axis_size("wsh")
+    return natural(jnp.stack(swap_all([values] * count, "wsh"), axis=0), "wsh")
+
+
+def on_device_heads(
+    block_input,
+    out_cotangent,
+    lengths,
+    slot_block,
+    norm_gains,
+    short_filter,
+    step_bias,
+    log_rate,
+    skip_gain,
+    mixer_in,
+    mixer_out,
+    attend_in,
+    attend_out,
+    gate_up,
+    down_weight,
+):
+    count = lax.axis_size("ctx")
+    groups = lax.axis_size("wsh")
+    ctx = lax.axis_index("ctx")
+    wsh = lax.axis_index("wsh")
+    rows, width = block_input.shape[1:]
+    block_rows = rows // 2
+    blocks = 2 * count
+    total_rows = count * rows
+    heads = MHEADS // count
+    chans = heads * HEAD_M
+    kv_width = KVH * HD
+    kv_head = ctx * KVH // count
+    units = gate_up.shape[2] // count
+    scale = 1.0 / math.sqrt(HD)
+    first_len = lengths[0, 0]
+    tokens = block_input[0]
+    cotangent = out_cotangent[0]
+    cols = lambda array, start, size: lax.dynamic_slice_in_dim(array, start, size, array.ndim - 1)
+    step_pad = -(chans * 2 + 2 * NSTATE + 3 * HD + heads) % 128
+
+    in_cols = jnp.concatenate(
+        [
+            cols(mixer_in, ctx * chans, chans),
+            cols(mixer_in, DSSM + ctx * chans, chans),
+            mixer_in[:, 2 * DSSM : 2 * DSSM + 2 * NSTATE],
+            cols(attend_in, ctx * HD, HD),
+            cols(attend_in, AQ + kv_head * HD, HD),
+            cols(attend_in, AQ + kv_width + kv_head * HD, HD),
+            cols(mixer_in, DSSM + CONV + ctx * heads, heads),
+            jnp.zeros((mixer_in.shape[0], step_pad), jnp.bfloat16),
+        ],
+        axis=1,
+    )
+    gains_all = gather_wsh(norm_gains)
+    gains = jnp.transpose(gains_all, (1, 0, 2)).reshape(2, width).astype(jnp.float32)
+    in_all = gather_wsh(in_cols).reshape(width, in_cols.shape[1])
+    out_rows = jnp.concatenate(
+        [
+            lax.dynamic_slice_in_dim(mixer_out, ctx * chans, chans, 0),
+            lax.dynamic_slice_in_dim(attend_out, ctx * HD, HD, 0),
+        ],
+        axis=0,
+    )
+    out_mine = jnp.transpose(gather_wsh(out_rows), (1, 0, 2)).reshape(chans + HD, width)
+    out_all = gather_ctx(out_mine)
+    mlp_cols = cols(gate_up, ctx * units, units)
+    mlp_rows = lax.dynamic_slice_in_dim(down_weight, ctx * units, units, 0)
+    mlp_parts = swap_all([mlp_cols] * groups, "wsh")
+    down_all = jnp.concatenate(swap_all([mlp_rows] * groups, "wsh"), axis=0)
+    gate_cols = jnp.concatenate([part[0] for part in mlp_parts], axis=1)
+    up_cols = jnp.concatenate([part[1] for part in mlp_parts], axis=1)
+    gate_up_cols = jnp.concatenate([gate_cols, up_cols], axis=1)
+
+    peers = ctx ^ jnp.arange(count, dtype=jnp.int32)
+    held = jnp.take(slot_block.reshape(count, 2), peers, axis=0, mode="clip").reshape(blocks)
+    logical_ids = jnp.arange(blocks, dtype=jnp.int32)
+    place = jnp.sum(
+        jnp.where(held[None, :] == logical_ids[:, None], logical_ids[None, :], 0), axis=1
+    )
+
+    def to_logical(array):
+        pieces = array.reshape((blocks, block_rows) + array.shape[2:])
+        return jnp.take(pieces, place, axis=0, mode="clip").reshape(
+            (total_rows,) + array.shape[2:]
+        )
+
+    def to_held(array):
+        pieces = array.reshape((blocks, block_rows) + array.shape[1:])
+        return jnp.take(pieces, held, axis=0, mode="clip").reshape(
+            (count, rows) + array.shape[1:]
+        )
+
+    positions = jnp.arange(total_rows, dtype=jnp.int32)
+    second = positions >= first_len
+    seq_pos = positions - jnp.where(second, first_len, 0)
+
+    first_scale = lax.rsqrt(jnp.mean(tokens * tokens, axis=-1, keepdims=True) + EPS)
+    normed_first = to_logical(gather_ctx((tokens * first_scale * gains[0]).astype(jnp.bfloat16)))
+    cot_b = cotangent.astype(jnp.bfloat16)
+    cot_all = gather_ctx(cot_b).reshape(total_rows, width)
+    projected = jnp.dot(normed_first, in_all, preferred_element_type=jnp.float32)
+    edges = [chans, 2 * chans + 2 * NSTATE]
+    edges += [edges[1] + HD, edges[1] + 2 * HD, edges[1] + 3 * HD, edges[1] + 3 * HD + heads]
+    gate_z = projected[:, : edges[0]]
+    conv_input = projected[:, edges[0] : edges[1]]
+    step_raw = projected[:, edges[4] : edges[5]]
+
+    filter_mine = jnp.concatenate(
+        [cols(short_filter, ctx * chans, chans), short_filter[:, DSSM:]], axis=1
+    )
+    conv = filter_mine[KERNEL] + filter_mine[KERNEL - 1] * conv_input
+    moved = []
+    for shift in range(KERNEL - 1, 0, -1):
+        shifted = jnp.concatenate(
+            [jnp.zeros((shift, conv_input.shape[1]), jnp.float32), conv_input[:-shift]], axis=0
+        )
+        moved.append(jnp.where((seq_pos >= shift)[:, None], shifted, 0.0))
+        conv = conv + filter_mine[KERNEL - 1 - shift] * moved[-1]
+    activated = jax.nn.silu(conv)
+    in_heads = lambda array: jnp.transpose(
+        array.reshape(blocks, block_rows, heads, HEAD_M), (2, 0, 1, 3)
+    )
+    from_heads = lambda array: jnp.transpose(array, (1, 2, 0, 3)).reshape(total_rows, chans)
+    heads_x = in_heads(activated[:, :chans])
+    b_in = activated[:, chans : chans + NSTATE].reshape(blocks, block_rows, NSTATE)
+    c_in = activated[:, chans + NSTATE :].reshape(blocks, block_rows, NSTATE)
+    bias_mine = lax.dynamic_slice_in_dim(step_bias, ctx * heads, heads)
+    rate_mine = jnp.exp(lax.dynamic_slice_in_dim(log_rate, ctx * heads, heads))
+    skip_mine = lax.dynamic_slice_in_dim(skip_gain, ctx * heads, heads)
+    step_in = jnp.transpose(step_raw).reshape(heads, blocks, block_rows) + bias_mine[:, None, None]
+    step = jax.nn.softplus(step_in)
+    log_decay = -step * rate_mine[:, None, None]
+
+    ein = lambda spec, left, right: jnp.einsum(spec, left, right, precision=HIGH)
+    lower = jnp.arange(block_rows)[:, None] >= jnp.arange(block_rows)[None, :]
+    cumulative = ein("hbs,ts->hbt", log_decay, lower.astype(jnp.float32))
+    totals = cumulative[:, :, -1]
+    growth = jnp.exp(cumulative)
+    tail = jnp.exp(totals[:, :, None] - cumulative)
+    decays = jnp.where(
+        lower,
+        jnp.exp(jnp.where(lower, cumulative[..., :, None] - cumulative[..., None, :], 0.0)),
+        0.0,
+    )
+    mixing = decays * ein("btn,bsn->bts", c_in, b_in)[None]
+    fed = heads_x * step[..., None]
+    emitted = ein("hbsp,bsn->hbpn", fed * tail[..., None], b_in)
+    before = jnp.concatenate(
+        [jnp.zeros((heads, 1), jnp.float32), jnp.cumsum(totals, axis=1)], axis=1
+    )
+    block_second = logical_ids * block_rows >= first_len
+    earlier = (block_second[:, None] == block_second[None, :]) & (
+        logical_ids[:, None] > logical_ids[None, :]
+    )
+    chain = jnp.where(
+        earlier,
+        jnp.exp(jnp.where(earlier, before[:, :-1, None] - before[:, None, 1:], 0.0)),
+        0.0,
+    )
+    state_in = ein("hbj,hjpn->hbpn", chain, emitted)
+    inner = ein("hbts,hbsp->hbtp", mixing, fed) + (
+        ein("hbpn,btn->hbtp", state_in, c_in) * growth[..., None]
+    )
+    mixer_y = from_heads(inner + skip_mine[:, None, None, None] * heads_x)
+    silu_z = jax.nn.silu(gate_z)
+    gated = (mixer_y * silu_z).astype(jnp.bfloat16)
+
+    half = HD // 2
+    freqs = jnp.exp(jnp.arange(half, dtype=jnp.float32) * (-2.0 * math.log(ROPE_BASE) / HD))
+    angles = seq_pos.astype(jnp.float32)[:, None] * freqs[None, :]
+    cosines = jnp.cos(angles)
+    sines = jnp.sin(angles)
+    query = rotate(projected[:, edges[1] : edges[2]], cosines, sines).astype(jnp.bfloat16)
+    key = rotate(projected[:, edges[2] : edges[3]], cosines, sines).astype(jnp.bfloat16)
+    value = projected[:, edges[3] : edges[4]].astype(jnp.bfloat16)
+    allowed = (positions[None, :] <= positions[:, None]) & (second[None, :] == second[:, None])
+    scores = jnp.where(allowed, matmul_back(query, key) * scale, NEG_LARGE)
+    top = jnp.max(scores, axis=-1, keepdims=True)
+    weights = jnp.where(allowed, jnp.exp(scores - top), 0.0)
+    denominator = jnp.sum(weights, axis=-1, keepdims=True)
+    log_total = top + jnp.log(denominator)
+    attn_rows = (
+        jnp.dot(weights.astype(jnp.bfloat16), value, preferred_element_type=jnp.float32)
+        / denominator
+    )
+    mixed_b = jnp.concatenate([gated, attn_rows.astype(jnp.bfloat16)], axis=1)
+
+    mixed_held = to_held(mixed_b)
+    mixed_mine = jnp.stack(swap_all(mixed_held, "ctx"), axis=0)
+    hidden = tokens + jnp.einsum(
+        "ktc,kcd->td", mixed_mine, out_all, preferred_element_type=jnp.float32
+    )
+
+    second_scale = lax.rsqrt(jnp.mean(hidden * hidden, axis=-1, keepdims=True) + EPS)
+    unit_hidden = hidden * second_scale
+    normed_second = gather_ctx((unit_hidden * gains[1]).astype(jnp.bfloat16)).reshape(
+        total_rows, width
+    )
+    both = jnp.dot(normed_second, gate_up_cols, preferred_element_type=jnp.float32)
+    gate_part = both[:, : groups * units]
+    up_part = both[:, groups * units :]
+    silu_gate = jax.nn.silu(gate_part)
+    mlp_act = (silu_gate * up_part).astype(jnp.bfloat16)
+    d_mlp = matmul_back(cot_all, down_all)
+    d_gate = (d_mlp * up_part * silu_slope(gate_part)).astype(jnp.bfloat16)
+    d_up = (d_mlp * silu_gate).astype(jnp.bfloat16)
+    d_both = jnp.concatenate([d_gate, d_up], axis=1)
+    d_normed_second = scatter_ctx(matmul_back(d_both, gate_up_cols).reshape(count, rows, width))
+    mlp_out = scatter_ctx(
+        jnp.dot(mlp_act, down_all, preferred_element_type=jnp.float32).reshape(count, rows, width)
+    )
+    output = hidden + mlp_out
+
+    def norm_back(d_normed, gain, unit, unit_scale):
+        scaled = d_normed * gain
+        return unit_scale * (scaled - unit * jnp.mean(scaled * unit, axis=-1, keepdims=True))
+
+    hidden_grad = cotangent + norm_back(d_normed_second, gains[1], unit_hidden, second_scale)
+    hidden_b = to_logical(gather_ctx(hidden_grad.astype(jnp.bfloat16)))
+
+    both_grad = matmul_t(normed_second, d_both)
+    down_grad_t = matmul_t(cot_all, mlp_act)
+    gain_second_grad = jnp.sum(both_grad * gate_up_cols.astype(jnp.float32), axis=1) / gains[1]
+    mlp_grads = [
+        jnp.concatenate(
+            [
+                both_grad[:, k * units : (k + 1) * units],
+                both_grad[:, (groups + k) * units : (groups + k + 1) * units],
+                down_grad_t[:, k * units : (k + 1) * units],
+            ],
+            axis=1,
+        ).astype(jnp.bfloat16)
+        for k in range(groups)
+    ]
+    mlp_sum = sum(piece.astype(jnp.float32) for piece in swap_all(mlp_grads, "wsh"))
+    mlp_sum = jnp.take(
+        mlp_sum.astype(jnp.bfloat16).reshape(count, width // count, 3 * units),
+        peers,
+        axis=0,
+        mode="clip",
+    )
+    mlp_final = natural(jnp.stack(swap_all(mlp_sum, "ctx"), axis=0), "ctx").astype(jnp.float32)
+    side_by_side = lambda array: jnp.transpose(array, (1, 0, 2)).reshape(array.shape[1], -1)
+    gate_up_grad = jnp.stack(
+        [side_by_side(mlp_final[:, :, :units]), side_by_side(mlp_final[:, :, units : 2 * units])],
+        axis=0,
+    )
+    down_grad = jnp.transpose(mlp_final[:, :, 2 * units :], (0, 2, 1)).reshape(
+        count * units, width // count
+    )
+
+    d_mixed_out = matmul_back(hidden_b, out_mine)
+    out_grad_t = matmul_t(hidden_b, mixed_b)
+    d_gated = d_mixed_out[:, :chans]
+    d_attn = d_mixed_out[:, chans:].astype(jnp.bfloat16)
+
+    delta = jnp.sum(d_attn.astype(jnp.float32) * attn_rows, axis=-1, keepdims=True)
+    probs = jnp.where(allowed, jnp.exp(scores - log_total), 0.0)
+    d_scores = (probs * (matmul_back(d_attn, value) - delta) * scale).astype(jnp.bfloat16)
+    d_query = rotate(
+        jnp.dot(d_scores, key, preferred_element_type=jnp.float32), cosines, -sines
+    )
+    d_key = rotate(matmul_t(d_scores, query), cosines, -sines)
+    d_value = matmul_t(probs.astype(jnp.bfloat16), d_attn)
+
+    d_z = d_gated * mixer_y * silu_slope(gate_z)
+    d_y = in_heads(d_gated * silu_z)
+    grown = d_y * growth[..., None]
+    state_grad = ein("hbtp,btn->hbpn", grown, c_in)
+    later = ein("hcb,hcpn->hbpn", chain, state_grad)
+    fed_inner = ein("hbts,hbtp->hbsp", mixing, d_y)
+    fed_emit = ein("hbpn,bsn->hbsp", later, b_in) * tail[..., None]
+    d_fed = fed_inner + fed_emit
+    d_kernel = jnp.sum(ein("hbtp,hbsp->hbts", d_y, fed) * decays, axis=0)
+    d_c = ein("bts,bsn->btn", d_kernel, b_in) + ein("hbtp,hbpn->btn", grown, state_in)
+    d_b = ein("bts,btn->bsn", d_kernel, c_in) + ein(
+        "hbsp,hbpn->bsn", fed * tail[..., None], later
+    )
+    d_heads = d_fed * step[..., None] + skip_mine[:, None, None, None] * d_y
+    skip_grad = jnp.sum(d_y * heads_x, axis=(1, 2, 3))
+    d_cumulative = jnp.sum(d_y * inner - fed * d_fed, axis=-1)
+    d_totals = jnp.exp(totals) * jnp.sum(later * state_in, axis=(2, 3)) + jnp.sum(
+        fed * fed_emit, axis=(2, 3)
+    )
+    d_decay = ein("hbt,ts->hbs", d_cumulative, lower.astype(jnp.float32)) + d_totals[..., None]
+    d_step = jnp.sum(d_fed * heads_x, axis=-1) - d_decay * rate_mine[:, None, None]
+    log_rate_grad = jnp.sum(d_decay * log_decay, axis=(1, 2))
+    d_step_raw = d_step * jax.nn.sigmoid(step_in)
+    step_bias_grad = jnp.sum(d_step_raw, axis=(1, 2))
+
+    d_activated = jnp.concatenate(
+        [from_heads(d_heads), d_b.reshape(total_rows, NSTATE), d_c.reshape(total_rows, NSTATE)],
+        axis=1,
+    )
+    d_conv = d_activated * silu_slope(conv)
+    d_conv_input = filter_mine[KERNEL - 1] * d_conv
+    filter_grads = []
+    for index, shift in enumerate(range(KERNEL - 1, 0, -1)):
+        masked = jnp.where((seq_pos >= shift)[:, None], d_conv, 0.0)
+        back = jnp.concatenate(
+            [masked[shift:], jnp.zeros((shift, masked.shape[1]), jnp.float32)], axis=0
+        )
+        d_conv_input = d_conv_input + filter_mine[index] * back
+        filter_grads.append(jnp.sum(d_conv * moved[index], axis=0))
+    filter_grads.append(jnp.sum(d_conv * conv_input, axis=0))
+    filter_grads.append(jnp.sum(d_conv, axis=0))
+    filter_part = jnp.stack(filter_grads, axis=0)
+
+    step_cols = jnp.transpose(d_step_raw.reshape(heads, total_rows))
+    d_all = jnp.concatenate(
+        [
+            d_z,
+            d_conv_input,
+            d_query,
+            d_key,
+            d_value,
+            step_cols,
+            jnp.zeros((total_rows, step_pad), jnp.float32),
+        ],
+        axis=1,
+    ).astype(jnp.bfloat16)
+    d_held = to_held(d_all).reshape(total_rows, d_all.shape[1])
+    d_normed_first = scatter_ctx(matmul_back(d_held, in_all).reshape(count, rows, width))
+    unit_tokens = tokens * first_scale
+    input_grad = hidden_grad + norm_back(d_normed_first, gains[0], unit_tokens, first_scale)
+
+    in_grad = matmul_t(normed_first, d_all)
+    gain_first_grad = jnp.sum(in_grad * in_all.astype(jnp.float32), axis=1) / gains[0]
+    all_grad = jnp.concatenate(
+        [
+            in_grad[:, : edges[5]],
+            gain_first_grad[:, None],
+            gain_second_grad[:, None],
+            jnp.zeros((width, step_pad - 2), jnp.float32),
+            out_grad_t,
+        ],
+        axis=1,
+    ).astype(jnp.bfloat16)
+    share = width // (count * groups)
+    to_groups = jnp.transpose(
+        all_grad.reshape(count, groups, share, all_grad.shape[1]), (1, 0, 2, 3)
+    )
+    to_groups = jnp.take(
+        to_groups, wsh ^ jnp.arange(groups, dtype=jnp.int32), axis=0, mode="clip"
+    )
+    grad_sum = sum(piece.astype(jnp.float32) for piece in swap_all(to_groups, "wsh"))
+    grad_sum = jnp.take(grad_sum.astype(jnp.bfloat16), peers, axis=0, mode="clip")
+    final = natural(jnp.stack(swap_all(grad_sum, "ctx"), axis=0), "ctx").astype(jnp.float32)
+    wide = edges[5] + step_pad
+    per_kv = lambda array: side_by_side(
+        jnp.sum(array.reshape(KVH, count // KVH, share, HD), axis=1)
+    )
+    mixer_in_grad = jnp.concatenate(
+        [
+            side_by_side(final[:, :, :chans]),
+            side_by_side(final[:, :, chans : 2 * chans]),
+            jnp.sum(final[:, :, 2 * chans : edges[1]], axis=0),
+            side_by_side(final[:, :, edges[4] : edges[5]]),
+        ],
+        axis=1,
+    )
+    attend_in_grad = jnp.concatenate(
+        [
+            side_by_side(final[:, :, edges[1] : edges[2]]),
+            per_kv(final[:, :, edges[2] : edges[3]]),
+            per_kv(final[:, :, edges[3] : edges[4]]),
+        ],
+        axis=1,
+    )
+    gains_grad = jnp.transpose(jnp.sum(final[:, :, edges[5] : edges[5] + 2], axis=0))
+    stacked = lambda array: jnp.transpose(array, (0, 2, 1)).reshape(-1, share)
+    mixer_out_grad = stacked(final[:, :, wide : wide + chans])
+    attend_out_grad = stacked(final[:, :, wide + chans :])
+
+    small = jnp.concatenate(
+        [filter_part.reshape(-1), step_bias_grad, log_rate_grad, skip_grad], axis=0
+    )
+    small = jnp.pad(small, (0, -small.shape[0] % 1024)).reshape(-1, 128)
+    small = jnp.sum(gather_wsh(small), axis=0)
+    small = natural(gather_ctx(small), "ctx").reshape(count, -1)
+    filters = small[:, : filter_part.size].reshape((count,) + filter_part.shape)
+    filter_grad = jnp.concatenate(
+        [side_by_side(filters[:, :, :chans]), jnp.sum(filters[:, :, chans:], axis=0)], axis=1
+    )
+    per_head = small[:, filter_part.size : filter_part.size + 3 * heads].reshape(count, 3, heads)
+    step_bias_all, log_rate_all, skip_all = [per_head[:, i].reshape(-1) for i in range(3)]
+    return (
+        output[None],
+        input_grad[None],
+        gains_grad,
+        filter_grad,
+        step_bias_all,
+        log_rate_all,
+        skip_all,
+        mixer_in_grad,
+        mixer_out_grad,
+        attend_in_grad,
+        attend_out_grad,
+        gate_up_grad,
+        down_grad,
+    )
+
+
 def solution(mesh):
     placed = (
         P("wsh", "ctx", None),
@@ -479,8 +937,9 @@
         P(None, None, "wsh"),
         P("wsh", None),
     )
+    per_heads = mesh.shape["ctx"] == QH
     return jax.shard_map(
-        on_device,
+        on_device_heads if per_heads else on_device,
         mesh=mesh,
         in_specs=placed,
         out_specs=(

time: 1580 us -> 630 us (0.40)
  waiting for transfers between devices: 1180 us -> 188 us
  local copies, waits for them, and re-layouts: 75.8 us -> 172 us
  blocking collectives: 79.8 us -> 0 us
  starting transfers between devices: 0.94 us -> 79.9 us
  matrix products: 154 us -> 94.6 us
  other arithmetic: 54.5 us -> 81.8 us
    reduce_scatter x7 -> x0, waiting for transfers between devices: 630 us -> none  [the longest x1 168 us: on_device(): lax.psum_scatter(mixer_in_grad, ('ctx', 'wsh'), scatter_dimension=0, tile...]
    all_gather x8 -> x0, waiting for transfers between devices: 394 us -> none  [the longest x1 144 us: on_device(): lax.all_gather(gate_up, 'wsh', axis=2, tiled=True)]
    ppermute x0 -> x108, waiting for transfers between devices: none -> 188 us  [the longest x45 155 us: swap_all(): lax.ppermute(parts[k], axis_name, xor_pairs(count, k))]
    unnamed x23 -> x0, waiting for transfers between devices: 157 us -> none
    ppermute x0 -> x108, starting transfers between devices: none -> 79.9 us  [the longest x45 43.5 us: swap_all(): lax.ppermute(parts[k], axis_name, xor_pairs(count, k))]
    dot_general x38 -> x22, matrix products: 104 us -> 59.8 us  [the longest x16 43.5 us: on_device_heads(): jnp.einsum(spec, left, right, precision=HIGH)]
    psum x1 -> x0, blocking collectives: 42.3 us -> none  [on_device(): lax.psum((step_bias_grad, log_rate_grad, g_skip, filter_grad), ('ctx', 'w...]
    all_gather x4 -> x0, blocking collectives: 37.5 us -> none  [the longest x1 9.88 us: on_device(): lax.all_gather(tails, 'ctx', axis=0, tiled=True)]
  transfers between devices with their start and end apart: 19 -> 108, of which waited for: 15 -> 46; matrix products, arithmetic and copies ran while one was open for 15% -> 38% of each run, Pallas kernels for 0% -> 0%
where the time goes in v1:
time: 630 us; the launch traced here: 620 us
  waiting for transfers between devices  188 us (30%)
  local copies, waits for them, and re-layouts  172 us (27%)
  matrix products  94.6 us (15%)
  other arithmetic  81.8 us (13%)
  starting transfers between devices  79.9 us (13%)
    ppermute x45, waiting for transfers between devices, swap_all(): lax.ppermute(parts[k], axis_name, xor_pairs(count, k))  155 us
    dot_general x16, matrix products, on_device_heads(): jnp.einsum(spec, left, right, precision=HIGH)  43.5 us
    ppermute x45, starting transfers between devices, swap_all(): lax.ppermute(parts[k], axis_name, xor_pairs(count, k))  43.5 us
    unnamed x343, local copies, waits for them, and re-layouts  38.7 us
    concatenate x8, local copies, waits for them, and re-layouts, on_device_heads(): jnp.concatenate([d_z, d_conv_input, d_query, d_key, d_value, step_cols, j...  19.1 us
    dot_general x6, matrix products, matmul_back(): lax.dot_general(left, right, (((1,), (1,)), ((), ())), preferred_element_...  18.7 us
    dot_general x6, matrix products, matmul_t(): lax.dot_general(left, right, (((0,), (0,)), ((), ())), preferred_element_...  16.1 us
    add x1, local copies, waits for them, and re-layouts, on_device_heads(): mixer_y = from_heads(inner + skip_mine[:, None, None, None] * heads_x)  13.1 us
  transfers between devices with their start and end apart: 108, of which 46 were waited for; matrix products, arithmetic and copies ran while one was open for 38% of the time, Pallas kernels for 0%

profile of v1, /device:TPU:8, one launch (start us, length us, event | category | flops | bytes accessed | tf_op | source)
XLA Modules:
  0.0 619.9 jit_solution(5888423118754515087)
XLA Ops:
  54.2 13.0 %collective-permute-done.38 = bf16[2,1024,64]{1,2,0:T(8,128)(2,1)} collective-permute-done((bf16[2,1024,64]{1,2,0:T(8,128)(2,1)S(1)}, bf16[2,1024,64]{1,2,0:T(8,128)(2,1)}, u32[]{:S(2)}, u32[]{:S(2)}) %collective-permute-start.38) | collective-permute-done | bytes 262176 | tf_op jit(solution)/shard_map/ppermute | solution.py:507
  68.6 15.0 %collective-permute-done.39 = bf16[2,1024,64]{1,2,0:T(8,128)(2,1)S(1)} collective-permute-done((bf16[2,1024,64]{1,2,0:T(8,128)(2,1)S(1)}, bf16[2,1024,64]{1,2,0:T(8,128)(2,1)S(1)}, u32[]{:S(2)}, u32[]{:S(2)}) %collective-permute-start.39) | collective-permute-done | bytes 262176 | tf_op jit(solution)/shard_map/ppermute | solution.py:507
  97.7 5.6 collective-permute-done.12
  103.8 11.3 %collective-permute-done.11 = bf16[256,896]{0,1:T(8,128)(2,1)S(1)} collective-permute-done((bf16[256,896]{0,1:T(8,128)(2,1)S(1)}, bf16[256,896]{0,1:T(8,128)(2,1)S(1)}, u32[]{:S(2)}, u32[]{:S(2)}) %collective-permute-start.11) | collective-permute-done | bytes 458784 | tf_op jit(solution)/shard_map/ppermute | solution.py:507
  147.5 4.2 fusion.215
  168.7 4.9 fusion.25
  173.6 13.1 %copy.567 = f32[16,64,3,64]{1,0,3,2:T(8,128)} copy(f32[16,64,3,64]{1,3,0,2:T(8,128)S(1)} %get-tuple-element.241) | data formatting | bytes 1572864 | tf_op jit(solution)/shard_map/add | solution.py:682
  206.9 4.1 collective-permute-done.15
  215.3 4.3 collective-permute-done.17
  220.8 4.0 collective-permute-done.18
  224.7 4.6 collective-permute-done.19
  242.1 5.6 collective-permute-done.31
  261.9 4.0 fusion.211
  281.2 3.8 fusion.212
  290.0 13.3 %collective-permute-done.99 = bf16[1024,192]{0,1:T(8,128)(2,1)S(1)} collective-permute-done((bf16[1024,192]{0,1:T(8,128)(2,1)S(1)}, bf16[1024,192]{0,1:T(8,128)(2,1)S(1)}, u32[]{:S(2)}, u32[]{:S(2)}) %collective-permute-start.99) | collective-permute-done | bytes 393248 | tf_op jit(solution)/shard_map/ppermute | solution.py:507
  303.3 9.6 %collective-permute-done.100 = bf16[1024,192]{0,1:T(8,128)(2,1)S(1)} collective-permute-done((bf16[1024,192]{0,1:T(8,128)(2,1)S(1)}, bf16[1024,192]{0,1:T(8,128)(2,1)S(1)}, u32[]{:S(2)}, u32[]{:S(2)}) %collective-permute-start.100) | collective-permute-done | bytes 393248 | tf_op jit(solution)/shard_map/ppermute | solution.py:507
  389.3 4.0 copy.611
  396.2 4.0 fusion.67
  425.6 4.9 fusion.59
  437.5 5.5 fusion.21
  445.3 6.5 %fusion.197 = (f32[448]{0:T(512)S(1)}, f32[448]{0:T(512)S(1)}, f32[448]{0:T(512)}, f32[448]{0:T(512)}, f32[448]{0:T(512)}, /*index=5*/f32[1024,448]{0,1:T(8,128)S(1)}) fusion(f32[1024,896]{0,1:T(8,128)} %copy-done.3, f32[1023,448]{0,1:T(8,128)} %copy-done.10, pred[1024]{0:T(1024)(128)(4,1)S(1)} %copy-done.115, f32[1022,448]{0,1:T(8,128)} %copy-done.11, ...), kind=kLoop, calls=%fused_computation.475 | loop fusion | flops 10090304 | bytes 12846336 | tf_op jit(solution)/shard_map/reduce_sum | solution.py:824
  453.2 6.7 %fusion.17 = (f32[3,16,64]{2,1,0:T(8,128)}, f32[3,16,64]{2,1,0:T(8,128)}, f32[3,16]{1,0:T(4,128)}, f32[3]{0:T(128)}) fusion(f32[3,16,64,64]{2,3,1,0:T(8,128)} %get-tuple-element.242, f32[16,64,3,64]{1,3,0,2:T(8,128)} %copy-done.13, f32[16,64,3,64]{1,0,3,2:T(8,128)} %copy-done.2, f32[16,64,3,64]{1,0,3,2:T(8,128)S(1)} %reshape.414, ...), kind=kLoop, calls=%fused_computation.54 | loop fusion | flops 2942925 | bytes 4780236 | tf_op jit(solution)/shard_map/reduce_sum | solution.py:799
  481.6 9.4 %concatenate.138 = bf16[1024,896]{0,1:T(8,128)(2,1)} concatenate(bf16[1024,192]{0,1:T(8,128)(2,1)S(1)} %copy-done.29, bf16[1024,448]{0,1:T(8,128)(2,1)S(1)} %add_convert_fusion, bf16[1024,32]{0,1:T(8,128)(2,1)S(1)} %get-tuple-element.235, bf16[1024,32]{0,1:T(8,128)(2,1)S(1)} %get-tuple-element.236, bf16[1024,32]{0,1:T(8,128)(2,1)S(1)} %get-tuple-element.213, ...), dimensions={1} | concatenate | bytes 3670016 | tf_op jit(solution)/shard_map/concatenate | solution.py:828
  491.0 5.6 multiply_reduce_fusion
  497.5 4.5 concatenate.137
  510.2 5.1 concatenate.140
  520.9 5.8 fusion.213
  547.4 12.9 %collective-permute-done.79 = bf16[8,32,1152]{2,1,0:T(8,128)(2,1)} collective-permute-done((bf16[8,32,1152]{2,1,0:T(8,128)(2,1)}, bf16[8,32,1152]{2,1,0:T(8,128)(2,1)}, u32[]{:S(2)}, u32[]{:S(2)}) %collective-permute-start.79) | collective-permute-done | bytes 589856 | tf_op jit(solution)/shard_map/ppermute | solution.py:507
  561.5 12.1 %collective-permute-done.80 = bf16[8,32,1152]{2,1,0:T(8,128)(2,1)} collective-permute-done((bf16[8,32,1152]{2,1,0:T(8,128)(2,1)S(1)}, bf16[8,32,1152]{2,1,0:T(8,128)(2,1)}, u32[]{:S(2)}, u32[]{:S(2)}) %collective-permute-start.80) | collective-permute-done | bytes 589856 | tf_op jit(solution)/shard_map/ppermute | solution.py:507
  583.0 7.8 %collective-permute-done.82 = bf16[32,1152]{1,0:T(8,128)(2,1)S(1)} collective-permute-done((bf16[32,1152]{1,0:T(8,128)(2,1)S(1)}, bf16[32,1152]{1,0:T(8,128)(2,1)S(1)}, u32[]{:S(2)}, u32[]{:S(2)}) %collective-permute-start.82) | collective-permute-done | bytes 73760 | tf_op jit(solution)/shard_map/ppermute | solution.py:507
  591.3 3.9 collective-permute-done.83
  599.5 4.3 collective-permute-done.85
  (797 shorter events, 393.4 us)
Async XLA Ops:
  0.7 37.0 %collective-permute-start = (bf16[2,256]{1,0:T(2,128)(2,1)}, bf16[2,256]{1,0:T(2,128)(2,1)}, u32[]{:S(2)}, u32[]{:S(2)}) collective-permute-start(bf16[2,256]{1,0:T(2,128)(2,1)} %param.19), channel_id=1, source_target_pairs={{0,1},{1,0},{2,3},{3,2},{4,5},{5,4},{6,7},{7,6},{8,9},{9,8},{10,11... | collective-permute-start | bytes 3080 | tf_op jit(solution)/shard_map/ppermute | solution.py:507
  0.8 37.4 %collective-permute-start.2 = (bf16[2,256]{1,0:T(2,128)(2,1)}, bf16[2,256]{1,0:T(2,128)(2,1)}, u32[]{:S(2)}, u32[]{:S(2)}) collective-permute-start(bf16[2,256]{1,0:T(2,128)(2,1)} %param.19), channel_id=1, source_target_pairs={{0,3},{1,2},{2,1},{3,0},{4,7},{5,6},{6,5},{7,4},{8,11},{9,10},{10,... | collective-permute-start | bytes 3080 | tf_op jit(solution)/shard_map/ppermute | solution.py:507
  3.9 35.4 %collective-permute-start.1 = (bf16[2,256]{1,0:T(2,128)(2,1)}, bf16[2,256]{1,0:T(2,128)(2,1)}, u32[]{:S(2)}, u32[]{:S(2)}) collective-permute-start(bf16[2,256]{1,0:T(2,128)(2,1)} %param.19), channel_id=1, source_target_pairs={{0,2},{1,3},{2,0},{3,1},{4,6},{5,7},{6,4},{7,5},{8,10},{9,11},{10,... | collective-permute-start | bytes 3080 | tf_op jit(solution)/shard_map/ppermute | solution.py:507
  7.5 38.3 %collective-permute-start.21 = (bf16[256,256]{1,0:T(8,128)(2,1)}, bf16[256,256]{1,0:T(8,128)(2,1)}, u32[]{:S(2)}, u32[]{:S(2)}) collective-permute-start(bf16[256,256]{1,0:T(8,128)(2,1)} %get-tuple-element.217), channel_id=1, source_target_pairs={{0,2},{1,3},{2,0},{3,1},{4,6},{5,7},{6,4},{7,5},{8,10},{9,11},{10,... | collective-permute-start | bytes 393224 | tf_op jit(solution)/shard_map/ppermute | solution.py:507
  9.2 38.1 %collective-permute-start.20 = (bf16[256,256]{1,0:T(8,128)(2,1)}, bf16[256,256]{1,0:T(8,128)(2,1)}, u32[]{:S(2)}, u32[]{:S(2)}) collective-permute-start(bf16[256,256]{1,0:T(8,128)(2,1)} %get-tuple-element.217), channel_id=1, source_target_pairs={{0,1},{1,0},{2,3},{3,2},{4,5},{5,4},{6,7},{7,6},{8,9},{9,8},{10,11... | collective-permute-start | bytes 393224 | tf_op jit(solution)/shard_map/ppermute | solution.py:507
  39.3 49.9 %collective-permute-start.53 = (bf16[128,1024]{1,0:T(8,128)(2,1)}, bf16[128,1024]{1,0:T(8,128)(2,1)S(1)}, u32[]{:S(2)}, u32[]{:S(2)}) collective-permute-start(bf16[128,1024]{1,0:T(8,128)(2,1)} %bitcast_convert_fusion), channel_id=1, source_target_pairs={{0,16},{4,20},{8,24},{12,28},{16,0},{20,4},{24,8},{28,12},{1,17},{... | collective-permute-start | bytes 786440 | tf_op jit(solution)/shard_map/ppermute | solution.py:472
  45.9 41.0 %collective-permute-start.51 = (bf16[128,1024]{1,0:T(8,128)(2,1)}, bf16[128,1024]{1,0:T(8,128)(2,1)}, u32[]{:S(2)}, u32[]{:S(2)}) collective-permute-start(bf16[128,1024]{1,0:T(8,128)(2,1)} %bitcast_convert_fusion), channel_id=1, source_target_pairs={{0,8},{4,12},{8,0},{12,4},{16,24},{20,28},{24,16},{28,20},{1,9},{5... | collective-permute-start | bytes 786440 | tf_op jit(solution)/shard_map/ppermute | solution.py:471
  47.3 36.3 %collective-permute-start.50 = (bf16[128,1024]{1,0:T(8,128)(2,1)}, bf16[128,1024]{1,0:T(8,128)(2,1)}, u32[]{:S(2)}, u32[]{:S(2)}) collective-permute-start(bf16[128,1024]{1,0:T(8,128)(2,1)} %bitcast_convert_fusion), channel_id=1, source_target_pairs={{0,4},{4,0},{8,12},{12,8},{16,20},{20,16},{24,28},{28,24},{1,5},{5... | collective-permute-start | bytes 786440 | tf_op jit(solution)/shard_map/ppermute | solution.py:479
  52.8 30.8 %collective-permute-start.39 = (bf16[2,1024,64]{1,2,0:T(8,128)(2,1)S(1)}, bf16[2,1024,64]{1,2,0:T(8,128)(2,1)S(1)}, u32[]{:S(2)}, u32[]{:S(2)}) collective-permute-start(bf16[2,1024,64]{1,2,0:T(8,128)(2,1)S(1)} %copy.663), channel_id=1, source_target_pairs={{0,3},{1,2},{2,1},{3,0},{4,7},{5,6},{6,5},{7,4},{8,11},{9,10},{10,... | collective-permute-start | bytes 786440 | tf_op jit(solution)/shard_map/ppermute | solution.py:507
  67.3 36.0 %collective-permute-start.12 = (bf16[256,896]{0,1:T(8,128)(2,1)S(1)}, bf16[256,896]{0,1:T(8,128)(2,1)S(1)}, u32[]{:S(2)}, u32[]{:S(2)}) collective-permute-start(bf16[256,896]{0,1:T(8,128)(2,1)S(1)} %concatenate.112), channel_id=1, source_target_pairs={{0,3},{1,2},{2,1},{3,0},{4,7},{5,6},{6,5},{7,4},{8,11},{9,10},{10,... | collective-permute-start | bytes 1376264 | tf_op jit(solution)/shard_map/ppermute | solution.py:507
  83.6 31.4 %collective-permute-start.11 = (bf16[256,896]{0,1:T(8,128)(2,1)S(1)}, bf16[256,896]{0,1:T(8,128)(2,1)S(1)}, u32[]{:S(2)}, u32[]{:S(2)}) collective-permute-start(bf16[256,896]{0,1:T(8,128)(2,1)S(1)} %concatenate.112), channel_id=1, source_target_pairs={{0,2},{1,3},{2,0},{3,1},{4,6},{5,7},{6,4},{7,5},{8,10},{9,11},{10,... | collective-permute-start | bytes 1376264 | tf_op jit(solution)/shard_map/ppermute | solution.py:507
  95.0 162.7 %collective-permute-start.42 = (bf16[64,1024]{1,0:T(8,128)(2,1)}, bf16[64,1024]{1,0:T(8,128)(2,1)}, u32[]{:S(2)}, u32[]{:S(2)}) collective-permute-start(bf16[64,1024]{1,0:T(8,128)(2,1)} %constant_dynamic-slice_fusion.10), channel_id=1, source_target_pairs={{0,3},{1,2},{2,1},{3,0},{4,7},{5,6},{6,5},{7,4},{8,11},{9,10},{10,... | collective-permute-start | bytes 393224 | tf_op jit(solution)/shard_map/ppermute | solution.py:507
  103.3 34.4 %collective-permute-start.26 = (bf16[256,1024]{1,0:T(8,128)(2,1)S(1)}, bf16[256,1024]{1,0:T(8,128)(2,1)S(1)}, u32[]{:S(2)}, u32[]{:S(2)}) collective-permute-start(bf16[256,1024]{1,0:T(8,128)(2,1)S(1)} %bitcast.544), channel_id=1, source_target_pairs={{0,16},{4,20},{8,24},{12,28},{16,0},{20,4},{24,8},{28,12},{1,17},{... | collective-permute-start | bytes 1572872 | tf_op jit(solution)/shard_map/ppermute | solution.py:472
  134.2 123.4 %collective-permute-start.41 = (bf16[64,1024]{1,0:T(8,128)(2,1)}, bf16[64,1024]{1,0:T(8,128)(2,1)}, u32[]{:S(2)}, u32[]{:S(2)}) collective-permute-start(bf16[64,1024]{1,0:T(8,128)(2,1)} %constant_dynamic-slice_fusion.10), channel_id=1, source_target_pairs={{0,2},{1,3},{2,0},{3,1},{4,6},{5,7},{6,4},{7,5},{8,10},{9,11},{10,... | collective-permute-start | bytes 393224 | tf_op jit(solution)/shard_map/ppermute | solution.py:507
  141.3 88.1 %collective-permute-start.28 = (bf16[256,1024]{1,0:T(8,128)(2,1)}, bf16[256,1024]{1,0:T(8,128)(2,1)}, u32[]{:S(2)}, u32[]{:S(2)}) collective-permute-start(bf16[256,1024]{1,0:T(8,128)(2,1)} %broadcast_select_fusion), channel_id=1, source_target_pairs={{0,16},{4,12},{8,24},{12,4},{16,0},{20,28},{24,8},{28,20},{1,17},{... | collective-permute-start | bytes 1572872 | tf_op jit(solution)/shard_map/ppermute | solution.py:473
  144.6 85.3 %collective-permute-start.25 = (bf16[256,1024]{1,0:T(8,128)(2,1)}, bf16[256,1024]{1,0:T(8,128)(2,1)}, u32[]{:S(2)}, u32[]{:S(2)}) collective-permute-start(bf16[256,1024]{1,0:T(8,128)(2,1)} %collective-permute-done.24), channel_id=1, source_target_pairs={{0,4},{4,0},{8,12},{12,8},{16,20},{20,16},{24,28},{28,24},{1,5},{5... | collective-permute-start | bytes 1572872 | tf_op jit(solution)/shard_map/ppermute | solution.py:479
  278.0 34.9 %collective-permute-start.100 = (bf16[1024,192]{0,1:T(8,128)(2,1)S(1)}, bf16[1024,192]{0,1:T(8,128)(2,1)S(1)}, u32[]{:S(2)}, u32[]{:S(2)}) collective-permute-start(bf16[1024,192]{0,1:T(8,128)(2,1)S(1)} %pad_maximum_fusion.11), channel_id=1, source_target_pairs={{0,3},{1,2},{2,1},{3,0},{4,7},{5,6},{6,5},{7,4},{8,11},{9,10},{10,... | collective-permute-start | bytes 1179656 | tf_op jit(solution)/shard_map/ppermute | solution.py:507
  280.7 64.5 %collective-permute-start.57 = (bf16[128,1024]{1,0:T(8,128)(2,1)}, bf16[128,1024]{1,0:T(8,128)(2,1)}, u32[]{:S(2)}, u32[]{:S(2)}) collective-permute-start(bf16[128,1024]{1,0:T(8,128)(2,1)} %get-tuple-element.150), channel_id=1, source_target_pairs={{0,4},{4,0},{8,12},{12,8},{16,20},{20,16},{24,28},{28,24},{1,5},{5... | collective-permute-start | bytes 786440 | tf_op jit(solution)/shard_map/ppermute | solution.py:488
  286.0 48.9 %collective-permute-start.62 = (bf16[128,1024]{1,0:T(8,128)(2,1)}, bf16[128,1024]{1,0:T(8,128)(2,1)}, u32[]{:S(2)}, u32[]{:S(2)}) collective-permute-start(bf16[128,1024]{1,0:T(8,128)(2,1)} %get-tuple-element.151), channel_id=1, source_target_pairs={{0,4},{4,0},{8,12},{12,8},{16,20},{20,16},{24,28},{28,24},{1,5},{5... | collective-permute-start | bytes 786440 | tf_op jit(solution)/shard_map/ppermute | solution.py:488
  290.0 45.4 %collective-permute-start.58 = (bf16[128,1024]{1,0:T(8,128)(2,1)}, bf16[128,1024]{1,0:T(8,128)(2,1)}, u32[]{:S(2)}, u32[]{:S(2)}) collective-permute-start(bf16[128,1024]{1,0:T(8,128)(2,1)} %get-tuple-element.153), channel_id=1, source_target_pairs={{0,4},{4,0},{8,12},{12,8},{16,20},{20,16},{24,28},{28,24},{1,5},{5... | collective-permute-start | bytes 786440 | tf_op jit(solution)/shard_map/ppermute | solution.py:488
  463.2 64.5 %collective-permute-start.90 = (f32[24,128]{1,0:T(8,128)}, f32[24,128]{1,0:T(8,128)}, u32[]{:S(2)}, u32[]{:S(2)}) collective-permute-start(f32[24,128]{1,0:T(8,128)} %get-tuple-element.229), channel_id=1, source_target_pairs={{0,3},{1,2},{2,1},{3,0},{4,7},{5,6},{6,5},{7,4},{8,11},{9,10},{10,... | collective-permute-start | bytes 36872 | tf_op jit(solution)/shard_map/ppermute | solution.py:507
  463.5 66.1 %collective-permute-start.89 = (f32[24,128]{1,0:T(8,128)}, f32[24,128]{1,0:T(8,128)}, u32[]{:S(2)}, u32[]{:S(2)}) collective-permute-start(f32[24,128]{1,0:T(8,128)} %get-tuple-element.229), channel_id=1, source_target_pairs={{0,2},{1,3},{2,0},{3,1},{4,6},{5,7},{6,4},{7,5},{8,10},{9,11},{10,... | collective-permute-start | bytes 36872 | tf_op jit(solution)/shard_map/ppermute | solution.py:507
  463.5 66.1 %collective-permute-start.88 = (f32[24,128]{1,0:T(8,128)}, f32[24,128]{1,0:T(8,128)}, u32[]{:S(2)}, u32[]{:S(2)}) collective-permute-start(f32[24,128]{1,0:T(8,128)} %get-tuple-element.229), channel_id=1, source_target_pairs={{0,1},{1,0},{2,3},{3,2},{4,5},{5,4},{6,7},{7,6},{8,9},{9,8},{10,11... | collective-permute-start | bytes 36872 | tf_op jit(solution)/shard_map/ppermute | solution.py:507
  519.2 28.0 %collective-permute-start.78 = (bf16[8,32,1152]{2,1,0:T(8,128)(2,1)}, bf16[8,32,1152]{2,1,0:T(8,128)(2,1)}, u32[]{:S(2)}, u32[]{:S(2)}) collective-permute-start(bf16[8,32,1152]{2,1,0:T(8,128)(2,1)} %get-tuple-element.141), channel_id=1, source_target_pairs={{0,1},{1,0},{2,3},{3,2},{4,5},{5,4},{6,7},{7,6},{8,9},{9,8},{10,11... | collective-permute-start | bytes 1769480 | tf_op jit(solution)/shard_map/ppermute | solution.py:507
  519.2 41.0 %collective-permute-start.79 = (bf16[8,32,1152]{2,1,0:T(8,128)(2,1)}, bf16[8,32,1152]{2,1,0:T(8,128)(2,1)}, u32[]{:S(2)}, u32[]{:S(2)}) collective-permute-start(bf16[8,32,1152]{2,1,0:T(8,128)(2,1)} %get-tuple-element.142), channel_id=1, source_target_pairs={{0,2},{1,3},{2,0},{3,1},{4,6},{5,7},{6,4},{7,5},{8,10},{9,11},{10,... | collective-permute-start | bytes 1769480 | tf_op jit(solution)/shard_map/ppermute | solution.py:507
  527.8 45.8 %collective-permute-start.80 = (bf16[8,32,1152]{2,1,0:T(8,128)(2,1)S(1)}, bf16[8,32,1152]{2,1,0:T(8,128)(2,1)}, u32[]{:S(2)}, u32[]{:S(2)}) collective-permute-start(bf16[8,32,1152]{2,1,0:T(8,128)(2,1)S(1)} %get-tuple-element.143), channel_id=1, source_target_pairs={{0,3},{1,2},{2,1},{3,0},{4,7},{5,6},{6,5},{7,4},{8,11},{9,10},{10,... | collective-permute-start | bytes 1769480 | tf_op jit(solution)/shard_map/ppermute | solution.py:507
  539.2 76.4 %collective-permute-start.71 = (bf16[128,1024]{1,0:T(8,128)(2,1)}, bf16[128,1024]{1,0:T(8,128)(2,1)S(1)}, u32[]{:S(2)}, u32[]{:S(2)}) collective-permute-start(bf16[128,1024]{1,0:T(8,128)(2,1)} %get-tuple-element.146), channel_id=1, source_target_pairs={{0,4},{4,0},{8,12},{12,8},{16,20},{20,16},{24,28},{28,24},{1,5},{5... | collective-permute-start | bytes 786440 | tf_op jit(solution)/shard_map/ppermute | solution.py:488
  545.0 31.2 %collective-permute-start.76 = (bf16[128,1024]{1,0:T(8,128)(2,1)}, bf16[128,1024]{1,0:T(8,128)(2,1)}, u32[]{:S(2)}, u32[]{:S(2)}) collective-permute-start(bf16[128,1024]{1,0:T(8,128)(2,1)} %get-tuple-element.147), channel_id=1, source_target_pairs={{0,4},{4,0},{8,12},{12,8},{16,20},{20,16},{24,28},{28,24},{1,5},{5... | collective-permute-start | bytes 786440 | tf_op jit(solution)/shard_map/ppermute | solution.py:488
  547.2 29.0 %collective-permute-start.72 = (bf16[128,1024]{1,0:T(8,128)(2,1)}, bf16[128,1024]{1,0:T(8,128)(2,1)}, u32[]{:S(2)}, u32[]{:S(2)}) collective-permute-start(bf16[128,1024]{1,0:T(8,128)(2,1)} %get-tuple-element.149), channel_id=1, source_target_pairs={{0,4},{4,0},{8,12},{12,8},{16,20},{20,16},{24,28},{28,24},{1,5},{5... | collective-permute-start | bytes 786440 | tf_op jit(solution)/shard_map/ppermute | solution.py:488
  578.7 36.9 %collective-permute-start.75 = (bf16[128,1024]{1,0:T(8,128)(2,1)}, bf16[128,1024]{1,0:T(8,128)(2,1)}, u32[]{:S(2)}, u32[]{:S(2)}) collective-permute-start(bf16[128,1024]{1,0:T(8,128)(2,1)} %get-tuple-element.129), channel_id=1, source_target_pairs={{0,8},{4,12},{8,0},{12,4},{16,24},{20,28},{24,16},{28,20},{1,9},{5... | collective-permute-start | bytes 786440 | tf_op jit(solution)/shard_map/ppermute | solution.py:499
  580.0 35.6 %collective-permute-start.77 = (bf16[128,1024]{1,0:T(8,128)(2,1)}, bf16[128,1024]{1,0:T(8,128)(2,1)}, u32[]{:S(2)}, u32[]{:S(2)}) collective-permute-start(bf16[128,1024]{1,0:T(8,128)(2,1)} %get-tuple-element.130), channel_id=1, source_target_pairs={{0,16},{4,20},{8,24},{12,28},{16,0},{20,4},{24,8},{28,12},{1,17},{... | collective-permute-start | bytes 786440 | tf_op jit(solution)/shard_map/ppermute | solution.py:500
  581.1 27.9 %collective-permute-start.87 = (bf16[32,1152]{1,0:T(8,128)(2,1)S(1)}, bf16[32,1152]{1,0:T(8,128)(2,1)S(1)}, u32[]{:S(2)}, u32[]{:S(2)}) collective-permute-start(bf16[32,1152]{1,0:T(8,128)(2,1)S(1)} %get-tuple-element.176), channel_id=1, source_target_pairs={{0,28},{4,24},{8,20},{12,16},{16,12},{20,8},{24,4},{28,0},{1,29},{... | collective-permute-start | bytes 221192 | tf_op jit(solution)/shard_map/ppermute | solution.py:507
  (215 other events, 1711.9 us)

commit v2 on v0

--- a/solution.py
+++ b/solution.py
@@ -1,8 +1,11 @@
 import math
+from functools import partial
 
 import jax
 import jax.numpy as jnp
 from jax import lax
+from jax.experimental import pallas as pl
+from jax.experimental.pallas import tpu as pltpu
 from jax.sharding import PartitionSpec as P
 
 MHEADS = 24
@@ -21,6 +24,7 @@
 EPS = 1e-05
 ROPE_BASE = 100000000000.0
 HIGH = lax.Precision.HIGHEST
+SSD = HIGH
 NEG_LARGE = -1e30
 
 
@@ -461,6 +465,797 @@
     )
 
 
+def xor_pairs(count, bits):
+    return [(index, index ^ bits) for index in range(count)]
+
+
+def held_order(count):
+    return list(range(0, count, 2)) + list(range(1, count, 2))
+
+
+def gather_ctx(values):
+    count = lax.axis_size("ctx")
+    first_core = lax.axis_index("ctx") % 2 == 0
+    near_x = lax.ppermute(values, "ctx", xor_pairs(count, 2))
+    near_y = lax.ppermute(values, "ctx", xor_pairs(count, 4))
+    far = lax.ppermute(
+        jnp.where(first_core, near_x, near_y),
+        "ctx",
+        [(index, index ^ (4 if index % 2 == 0 else 2)) for index in range(count)],
+    )
+    mine = jnp.stack([values, near_x, near_y, far], axis=0)
+    other = lax.ppermute(mine, "ctx", xor_pairs(count, 1))
+    return jnp.concatenate([mine, other], axis=0)
+
+
+def scatter_ctx(parts):
+    count = lax.axis_size("ctx")
+    half = count // 2
+    first_core = lax.axis_index("ctx") % 2 == 0
+    wire = lambda piece: piece.astype(jnp.bfloat16)
+    sums = parts[:half] + lax.ppermute(
+        wire(parts[half:]), "ctx", xor_pairs(count, 1)
+    ).astype(jnp.float32)
+    own, near_x, near_y, far = [sums[place] for place in range(half)]
+    passed = lax.ppermute(
+        wire(far), "ctx", [(index, index ^ (2 if index % 2 == 0 else 4)) for index in range(count)]
+    ).astype(jnp.float32)
+    near_y = near_y + jnp.where(first_core, passed, 0.0)
+    near_x = near_x + jnp.where(first_core, 0.0, passed)
+    return (
+        own
+        + lax.ppermute(wire(near_x), "ctx", xor_pairs(count, 2)).astype(jnp.float32)
+        + lax.ppermute(wire(near_y), "ctx", xor_pairs(count, 4)).astype(jnp.float32)
+    )
+
+
+def trade_ctx(parts):
+    return lax.all_to_all(parts, "ctx", 0, 0, tiled=True)
+
+
+def after(values, anchor):
+    return lax.optimization_barrier((values, anchor))[0]
+
+
+def swap_groups(pieces):
+    count = lax.axis_size("wsh")
+    return [pieces[0]] + [
+        lax.ppermute(pieces[k], "wsh", xor_pairs(count, k)) for k in range(1, count)
+    ]
+
+
+def gather_wsh(values, axis=0):
+    count = lax.axis_size("wsh")
+    shape = list(values.shape)
+    size = shape[axis]
+    shape[axis] = size * count
+    whole = jnp.zeros(shape, values.dtype)
+    for k, piece in enumerate(swap_groups([values] * count)):
+        start = (lax.axis_index("wsh") ^ k) * size
+        whole = lax.dynamic_update_slice_in_dim(whole, piece, start, axis)
+    return whole
+
+
+def dot_dims(left, right, left_dim, right_dim, precision=None):
+    return lax.dot_general(
+        left,
+        right,
+        (((left_dim,), (right_dim,)), ((), ())),
+        precision=precision,
+        preferred_element_type=jnp.float32,
+    )
+
+
+def spread(per_head, heads, lanes):
+    return jnp.concatenate(
+        [jnp.broadcast_to(item, (item.shape[0], lanes)) for item in per_head[:heads]], axis=1
+    )
+
+
+def turn(values, table, back=False):
+    half = HD // 2
+    swapped = jnp.concatenate([values[:, half:], values[:, :half]], axis=1)
+    side = swapped * table[:, HD:]
+    return values * table[:, :HD] - side if back else values * table[:, :HD] + side
+
+
+def filtered(ext_ref, filt_ref, rows):
+    conv = filt_ref[KERNEL : KERNEL + 1, :] + filt_ref[KERNEL - 1 : KERNEL, :] * ext_ref[8:, :]
+    for tap in range(KERNEL - 1):
+        start = 8 - (KERNEL - 1) + tap
+        conv = conv + filt_ref[tap : tap + 1, :] * ext_ref[start : start + rows, :]
+    return conv
+
+
+def softplus(values):
+    return jnp.maximum(values, 0.0) + jnp.log1p(jnp.exp(-jnp.abs(values)))
+
+
+def block_decay(step_in, rate, rows):
+    step = softplus(step_in)
+    decay = -step * rate
+    lower = lax.broadcasted_iota(jnp.int32, (rows, rows), 0) >= lax.broadcasted_iota(
+        jnp.int32, (rows, rows), 1
+    )
+    ones = jnp.where(lower, 1.0, 0.0)
+    cum = dot_dims(ones, decay, 1, 0, HIGH)
+    cum_t = dot_dims(decay, ones, 0, 1, HIGH)
+    return step, decay, lower, ones, cum, cum_t
+
+
+def pick_kernel(heads, where_ref, *refs):
+    xs, zs = refs[:heads], refs[heads : 2 * heads]
+    bc0, step0, q0, k0, v0, gain_ref, out_ref = refs[2 * heads :]
+    chans = heads * HEAD_M
+    ctx = where_ref[0]
+    gain = gain_ref[0:1, :].astype(jnp.float32)
+    width = gain.shape[1]
+
+    def put(start, values):
+        scaled = values.astype(jnp.float32) * gain
+        out_ref[start : start + values.shape[0], :] = scaled.astype(jnp.bfloat16)
+
+    def half_tile(ref, odd):
+        window = jnp.transpose(ref[...].astype(jnp.float32))
+        return jnp.where(odd, window[HD:, :], window[:HD, :])
+
+    for h in range(heads):
+        put(h * HEAD_M, xs[h][...])
+        put(256 + h * HEAD_M, zs[h][...])
+    put(chans, half_tile(q0, ctx % 2 == 1))
+    put(256 + chans, half_tile(k0, where_ref[1] % 2 == 1))
+    put(512, bc0[...])
+    put(768, half_tile(v0, where_ref[1] % 2 == 1))
+    row = lax.broadcasted_iota(jnp.int32, (HEAD_M, width), 0)
+    steps = jnp.where(row < MHEADS, step0[...].astype(jnp.float32), 0.0).astype(jnp.bfloat16)
+    there = lax.broadcasted_iota(jnp.int32, (HEAD_M, HEAD_M), 0)
+    here = lax.broadcasted_iota(jnp.int32, (HEAD_M, HEAD_M), 1)
+    chosen = jnp.where((here == there + ctx * heads) & (there < heads), 1.0, 0.0)
+    put(768 + HD, dot_dims(chosen.astype(jnp.bfloat16), steps, 1, 0))
+
+
+def pick_columns(where, mixer_in, attend_in, gains, heads):
+    width = mixer_in.shape[0]
+    turned = jnp.transpose(mixer_in)
+    rows_at = lambda start: pl.BlockSpec((HEAD_M, width), lambda i, s: (start(s) // HEAD_M, 0))
+    tile_at = lambda start: pl.BlockSpec((width, 128), lambda i, s: (0, start(s) // 128))
+    from_x = [rows_at(lambda s, h=h: DSSM + (s[0] * heads + h) * HEAD_M) for h in range(heads)]
+    from_z = [rows_at(lambda s, h=h: (s[0] * heads + h) * HEAD_M) for h in range(heads)]
+    return pl.pallas_call(
+        partial(pick_kernel, heads),
+        out_shape=jax.ShapeDtypeStruct((896, width), jnp.bfloat16),
+        grid_spec=pltpu.PrefetchScalarGridSpec(
+            num_scalar_prefetch=1,
+            grid=(1,),
+            in_specs=from_x
+            + from_z
+            + [
+                pl.BlockSpec((2 * NSTATE, width), lambda i, s: (DSSM // NSTATE, 0)),
+                rows_at(lambda s: DSSM + CONV),
+                tile_at(lambda s: s[0] * HD),
+                tile_at(lambda s: AQ + s[1] * HD),
+                tile_at(lambda s: AQ + KVH * HD + s[1] * HD),
+                pl.BlockSpec(gains.shape, lambda i, s: (0, 0)),
+            ],
+            out_specs=pl.BlockSpec((896, width), lambda i, s: (0, 0)),
+        ),
+        name="pick_columns",
+    )(where, *[turned] * (2 * heads + 2), *[attend_in] * 3, gains)
+
+
+def finish_in_kernel(heads, final_ref, mixer_ref, attend_ref, last_ref):
+    count = final_ref.shape[0]
+    chans = heads * HEAD_M
+    share = final_ref.shape[1]
+    parts = [final_ref[c].astype(jnp.float32) for c in range(count)]
+    beside = lambda start, size: jnp.concatenate([p[:, start : start + size] for p in parts], axis=1)
+    mixer_ref[:, :DSSM] = beside(256, chans)
+    mixer_ref[:, DSSM : 2 * DSSM] = beside(0, chans)
+    mixer_ref[:, 2 * DSSM : 2 * DSSM + 2 * NSTATE] = sum(p[:, 512:768] for p in parts)
+    lane = lax.broadcasted_iota(jnp.int32, (128, MHEADS), 0)
+    head = lax.broadcasted_iota(jnp.int32, (128, MHEADS), 1)
+    steps = jnp.zeros((share, MHEADS), jnp.float32)
+    for c in range(count):
+        chosen = jnp.where((lane - HD == head - c * heads) & (lane >= HD) & (lane < HD + heads), 1.0, 0.0)
+        steps = steps + dot_dims(final_ref[c, :, 768:896], chosen.astype(jnp.bfloat16), 1, 0)
+    mixer_ref[:, DSSM + CONV :] = steps
+    attend_ref[:, :AQ] = beside(chans, HD)
+    each = count // KVH
+    for start, place in ((256 + chans, AQ), (768, AQ + KVH * HD)):
+        attend_ref[:, place : place + KVH * HD] = jnp.concatenate(
+            [
+                sum(p[:, start : start + HD] for p in parts[head_ * each : (head_ + 1) * each])
+                for head_ in range(KVH)
+            ],
+            axis=1,
+        )
+    last_ref[...] = sum(p[:, 768:896] for p in parts)
+
+
+def finish_in(final, heads):
+    share = final.shape[1]
+    return pl.pallas_call(
+        partial(finish_in_kernel, heads),
+        out_shape=(
+            jax.ShapeDtypeStruct((share, DSSM + CONV + MHEADS), jnp.float32),
+            jax.ShapeDtypeStruct((share, AQ + 2 * KVH * HD), jnp.float32),
+            jax.ShapeDtypeStruct((share, 128), jnp.float32),
+        ),
+        name="finish_in",
+    )(final)
+
+
+def finish_rest_kernel(chans, mlp_ref, out_ref, gate_up_ref, down_ref, mixer_ref, attend_ref):
+    count = mlp_ref.shape[0]
+    units = mlp_ref.shape[2] // 3
+    parts = [mlp_ref[c].astype(jnp.float32) for c in range(count)]
+    gate_up_ref[0] = jnp.concatenate([p[:, :units] for p in parts], axis=1)
+    gate_up_ref[1] = jnp.concatenate([p[:, units : 2 * units] for p in parts], axis=1)
+    for c in range(count):
+        down_ref[c * units : (c + 1) * units, :] = jnp.transpose(parts[c][:, 2 * units :])
+    outs = [out_ref[c].astype(jnp.float32) for c in range(count)]
+    mixer_ref[...] = jnp.concatenate([item[:, :chans] for item in outs], axis=1)
+    attend_ref[...] = jnp.concatenate([item[:, chans:] for item in outs], axis=1)
+
+
+def finish_rest(mlp, out, chans):
+    count, share, units = mlp.shape[0], mlp.shape[1], mlp.shape[2] // 3
+    return pl.pallas_call(
+        partial(finish_rest_kernel, chans),
+        out_shape=(
+            jax.ShapeDtypeStruct((2, share, count * units), jnp.float32),
+            jax.ShapeDtypeStruct((count * units, share), jnp.float32),
+            jax.ShapeDtypeStruct((out.shape[1], count * chans), jnp.float32),
+            jax.ShapeDtypeStruct((out.shape[1], count * HD), jnp.float32),
+        ),
+        name="finish_rest",
+    )(mlp, out)
+
+
+def forward_kernel(
+    heads, base, sched_ref, proj_ref, filt_ref, table_ref, params_ref, skip_ref,
+    held_ref, save_ref, state_ref, kv_ref, ext_ref, chain_ref, keys_ref, values_ref,
+):
+    index = pl.program_id(0)
+    blocks = pl.num_programs(0)
+    rows = proj_ref.shape[1]
+    chans = heads * HEAD_M
+    seq_start = sched_ref[blocks + index]
+
+    @pl.when(index == 0)
+    def _():
+        keys_ref[...] = jnp.zeros_like(keys_ref)
+        values_ref[...] = jnp.zeros_like(values_ref)
+
+    @pl.when(seq_start == index * rows)
+    def _():
+        ext_ref[0:8, :] = jnp.zeros((8, ext_ref.shape[1]), jnp.float32)
+        chain_ref[...] = jnp.zeros_like(chain_ref)
+
+    proj = proj_ref[0]
+    ext_ref[8:, :] = jnp.concatenate([proj[:, :256], proj[:, 512:768]], axis=1)
+    conv = filtered(ext_ref, filt_ref, rows)
+    ext_ref[0:8, :] = ext_ref[rows:, :]
+    act = conv * jax.nn.sigmoid(conv)
+    heads_x = act[:, :chans]
+    b_in = act[:, 256 : 256 + NSTATE]
+    c_in = act[:, 256 + NSTATE : 256 + 2 * NSTATE]
+    step, _, lower, _, cum, cum_t = block_decay(
+        proj[:, 768:] + params_ref[0:1, :], params_ref[1:2, :], rows
+    )
+    cum_cols = [cum[:, base + h : base + h + 1] for h in range(heads)]
+    mix = dot_dims(c_in, b_in, 1, 1, SSD)
+    fed = heads_x * spread([step[:, base + h : base + h + 1] for h in range(heads)], heads, HEAD_M)
+    state = chain_ref[...]
+    state_ref[0] = state
+    inner = []
+    for h in range(heads):
+        gaps = jnp.where(lower, cum_cols[h] - cum_t[base + h : base + h + 1, :], 0.0)
+        kernel = jnp.where(lower, jnp.exp(gaps), 0.0) * mix
+        inner.append(dot_dims(kernel, fed[:, h * HEAD_M : (h + 1) * HEAD_M], 1, 0, SSD))
+    growth = spread([jnp.exp(item) for item in cum_cols], heads, HEAD_M)
+    inner = jnp.concatenate(inner, axis=1) + dot_dims(c_in, state, 1, 1, SSD) * growth
+    ends = [item[rows - 1 : rows, :] for item in cum_cols]
+    tail = spread([jnp.exp(end - item) for end, item in zip(ends, cum_cols)], heads, HEAD_M)
+    emitted = dot_dims(fed * tail, b_in, 0, 0, SSD)
+    for h in range(heads):
+        part = slice(h * HEAD_M, (h + 1) * HEAD_M)
+        chain_ref[part, :] = jnp.exp(ends[h]) * state[part, :] + emitted[part, :]
+    gate_z = proj[:, 256 : 256 + chans]
+    gated = (inner + skip_ref[0:1, :] * heads_x) * (gate_z * jax.nn.sigmoid(gate_z))
+
+    table = table_ref[0]
+    query = turn(proj[:, chans : chans + HD], table).astype(jnp.bfloat16)
+    key = turn(proj[:, 256 + chans : 256 + chans + HD], table).astype(jnp.bfloat16)
+    value = proj[:, 768 : 768 + HD].astype(jnp.bfloat16)
+    here = pl.ds(pl.multiple_of(index * rows, rows), rows)
+    keys_ref[here, :] = key
+    values_ref[here, :] = value
+    kv_ref[0] = jnp.concatenate([key, value], axis=1)
+    total = keys_ref.shape[0]
+    key_pos = lax.broadcasted_iota(jnp.int32, (rows, total), 1)
+    my_pos = index * rows + lax.broadcasted_iota(jnp.int32, (rows, total), 0)
+    allowed = (key_pos <= my_pos) & (key_pos >= seq_start)
+    scores = jnp.where(
+        allowed, dot_dims(query, keys_ref[...], 1, 1) * (1.0 / math.sqrt(HD)), NEG_LARGE
+    )
+    top = jnp.max(scores, axis=-1, keepdims=True)
+    weights = jnp.exp(scores - top)
+    denominator = jnp.sum(weights, axis=-1, keepdims=True)
+    attn = dot_dims(weights.astype(jnp.bfloat16), values_ref[...], 1, 0) / denominator
+    log_total = jnp.broadcast_to(top + jnp.log(denominator), (rows, 128))
+    save_ref[0] = jnp.concatenate([inner, attn, log_total], axis=1)
+    held_ref[0] = jnp.concatenate([gated, attn], axis=1).astype(jnp.bfloat16)
+
+
+def backward_kernel(
+    heads, base, sched_ref, proj_ref, before_ref, filt_ref, table_ref, params_ref, skip_ref,
+    save_ref, state_ref, kv_ref, d_mix_ref,
+    d_ref, filt_grad_ref, head_grad_ref, ext_ref, next_ref, later_ref, keys_ref, values_ref,
+):
+    blocks = pl.num_programs(0)
+    turn_index = pl.program_id(0)
+    index = blocks - 1 - turn_index
+    rows = proj_ref.shape[1]
+    chans = heads * HEAD_M
+    seq_start = sched_ref[blocks + index]
+    after = jnp.minimum(index + 1, blocks - 1)
+    is_end = (index == blocks - 1) | (sched_ref[blocks + after] == after * rows)
+
+    @pl.when(turn_index == 0)
+    def _():
+        keys_ref[...] = jnp.zeros_like(keys_ref)
+        values_ref[...] = jnp.zeros_like(values_ref)
+        filt_grad_ref[...] = jnp.zeros_like(filt_grad_ref)
+        head_grad_ref[...] = jnp.zeros_like(head_grad_ref)
+
+    @pl.when(is_end)
+    def _():
+        next_ref[rows:, :] = jnp.zeros((8, next_ref.shape[1]), jnp.float32)
+        later_ref[...] = jnp.zeros_like(later_ref)
+
+    proj = proj_ref[0]
+    keep = jnp.where(seq_start == index * rows, 0.0, 1.0)
+    before = before_ref[0]
+    ext_ref[0:8, :] = jnp.concatenate([before[:, :256], before[:, 512:768]], axis=1) * keep
+    ext_ref[8:, :] = jnp.concatenate([proj[:, :256], proj[:, 512:768]], axis=1)
+    conv = filtered(ext_ref, filt_ref, rows)
+    conv_sig = jax.nn.sigmoid(conv)
+    act = conv * conv_sig
+    heads_x = act[:, :chans]
+    b_in = act[:, 256 : 256 + NSTATE]
+    c_in = act[:, 256 + NSTATE : 256 + 2 * NSTATE]
+    step_in = proj[:, 768:] + params_ref[0:1, :]
+    rate = params_ref[1:2, :]
+    step, decay, lower, ones, cum, cum_t = block_decay(step_in, rate, rows)
+    cum_cols = [cum[:, base + h : base + h + 1] for h in range(heads)]
+    step_cols = spread([step[:, base + h : base + h + 1] for h in range(heads)], heads, HEAD_M)
+    mix = dot_dims(c_in, b_in, 1, 1, SSD)
+    fed = heads_x * step_cols
+    state = state_ref[0]
+    later = later_ref[...]
+    save = save_ref[0]
+    inner = save[:, :chans]
+    skip = skip_ref[0:1, :]
+
+    d_mix = d_mix_ref[0]
+    d_gated = d_mix[:, :chans]
+    gate_z = proj[:, 256 : 256 + chans]
+    gate_sig = jax.nn.sigmoid(gate_z)
+    d_z = d_gated * (inner + skip * heads_x) * (gate_sig * (1.0 + gate_z * (1.0 - gate_sig)))
+    d_y = d_gated * (gate_z * gate_sig)
+    growth = spread([jnp.exp(item) for item in cum_cols], heads, HEAD_M)
+    ends = [item[rows - 1 : rows, :] for item in cum_cols]
+    tail = spread([jnp.exp(end - item) for end, item in zip(ends, cum_cols)], heads, HEAD_M)
+    grown = d_y * growth
+    fed_tail = fed * tail
+    fed_inner = []
+    d_mixing = jnp.zeros((rows, rows), jnp.float32)
+    for h in range(heads):
+        part = slice(h * HEAD_M, (h + 1) * HEAD_M)
+        gaps = jnp.where(lower, cum_cols[h] - cum_t[base + h : base + h + 1, :], 0.0)
+        decays = jnp.where(lower, jnp.exp(gaps), 0.0)
+        fed_inner.append(dot_dims(decays * mix, d_y[:, part], 0, 0, SSD))
+        d_mixing = d_mixing + dot_dims(d_y[:, part], fed[:, part], 1, 1, SSD) * decays
+    fed_emit = dot_dims(b_in, later, 1, 1, SSD) * tail
+    d_fed = jnp.concatenate(fed_inner, axis=1) + fed_emit
+    d_c = dot_dims(d_mixing, b_in, 1, 0, SSD) + dot_dims(grown, state, 1, 0, SSD)
+    d_b = dot_dims(d_mixing, c_in, 0, 0, SSD) + dot_dims(fed_tail, later, 1, 0, SSD)
+    state_grad = dot_dims(grown, c_in, 0, 0, SSD)
+    d_x = d_fed * step_cols + skip * d_y
+    lane = lax.broadcasted_iota(jnp.int32, (1, 128), 1)
+    d_cum = jnp.zeros((rows, 128), jnp.float32)
+    d_step = jnp.zeros((rows, 128), jnp.float32)
+    d_total = jnp.zeros((1, 128), jnp.float32)
+    skip_sum = jnp.zeros((1, 128), jnp.float32)
+    cum_terms = d_y * inner - fed * d_fed
+    step_terms = d_fed * heads_x
+    emit_terms = fed * fed_emit
+    skip_terms = d_y * heads_x
+    carry_terms = later * state
+    for h in range(heads):
+        part = slice(h * HEAD_M, (h + 1) * HEAD_M)
+        mine = jnp.where(lane == base + h, 1.0, 0.0)
+        growth_end = jnp.exp(ends[h])
+        d_cum = d_cum + jnp.sum(cum_terms[:, part], axis=1, keepdims=True) * mine
+        d_step = d_step + jnp.sum(step_terms[:, part], axis=1, keepdims=True) * mine
+        carry = jnp.sum(jnp.sum(carry_terms[part, :], axis=0, keepdims=True), axis=1, keepdims=True)
+        emit = jnp.sum(jnp.sum(emit_terms[:, part], axis=0, keepdims=True), axis=1, keepdims=True)
+        skips = jnp.sum(jnp.sum(skip_terms[:, part], axis=0, keepdims=True), axis=1, keepdims=True)
+        d_total = d_total + (growth_end * carry + emit) * mine
+        skip_sum = skip_sum + skips * mine
+        later_ref[part, :] = state_grad[part, :] + growth_end * later[part, :]
+    d_decay = dot_dims(ones, d_cum, 0, 0, HIGH) + d_total
+    d_step = (d_step - d_decay * rate) * jax.nn.sigmoid(step_in)
+    d_step = jnp.where((lane >= base) & (lane < base + heads), d_step, 0.0)
+    head_grad_ref[0:1, :] += jnp.sum(d_step, axis=0, keepdims=True)
+    head_grad_ref[1:2, :] += jnp.sum(d_decay * decay, axis=0, keepdims=True)
+    head_grad_ref[2:3, :] += skip_sum
+
+    d_conv = jnp.concatenate([d_x, jnp.zeros((rows, 256 - chans), jnp.float32), d_b, d_c], axis=1)
+    d_conv = d_conv * (conv_sig * (1.0 + conv * (1.0 - conv_sig)))
+    next_ref[0:rows, :] = d_conv
+    d_in = filt_ref[KERNEL - 1 : KERNEL, :] * d_conv
+    for tap in range(KERNEL - 1):
+        shift = KERNEL - 1 - tap
+        d_in = d_in + filt_ref[tap : tap + 1, :] * next_ref[shift : shift + rows, :]
+        filt_grad_ref[tap : tap + 1, :] += jnp.sum(
+            d_conv * ext_ref[8 - shift : 8 - shift + rows, :], axis=0, keepdims=True
+        )
+    filt_grad_ref[KERNEL - 1 : KERNEL, :] += jnp.sum(d_conv * ext_ref[8:, :], axis=0, keepdims=True)
+    filt_grad_ref[KERNEL : KERNEL + 1, :] += jnp.sum(d_conv, axis=0, keepdims=True)
+    next_ref[rows:, :] = d_conv[0:8, :]
+
+    table = table_ref[0]
+    scale = 1.0 / math.sqrt(HD)
+    query = turn(proj[:, chans : chans + HD], table).astype(jnp.bfloat16)
+    keys = kv_ref[:, :HD]
+    values = kv_ref[:, HD:]
+    d_attn = d_mix[:, chans : chans + HD].astype(jnp.bfloat16)
+    delta = jnp.sum(d_attn.astype(jnp.float32) * save[:, chans : chans + HD], axis=1, keepdims=True)
+    total = keys.shape[0]
+    key_pos = lax.broadcasted_iota(jnp.int32, (rows, total), 1)
+    my_pos = index * rows + lax.broadcasted_iota(jnp.int32, (rows, total), 0)
+    allowed = (key_pos <= my_pos) & (key_pos >= seq_start)
+    scores = jnp.where(allowed, dot_dims(query, keys, 1, 1) * scale, NEG_LARGE)
+    probs = jnp.exp(scores - save[:, chans + HD : chans + HD + 1])
+    d_scores = (probs * (dot_dims(d_attn, values, 1, 1) - delta) * scale).astype(jnp.bfloat16)
+    d_query = turn(dot_dims(d_scores, keys, 1, 0), table, back=True)
+    keys_ref[...] += dot_dims(d_scores, query, 0, 0)
+    values_ref[...] += dot_dims(probs.astype(jnp.bfloat16), d_attn, 0, 0)
+    here = pl.ds(pl.multiple_of(index * rows, rows), rows)
+    d_key = turn(keys_ref[here, :], table, back=True)
+    d_value = values_ref[here, :]
+    d_ref[0] = jnp.concatenate(
+        [d_in[:, :chans], d_query, d_z, d_key, d_in[:, 256:], d_value, d_step[:, HD:]], axis=1
+    ).astype(jnp.bfloat16)
+
+
+def mixer_forward(sched, proj, filt, table, params, skip, heads, base):
+    blocks, rows, wide = proj.shape
+    chans = heads * HEAD_M
+    held = lambda b, s: (s[b], 0, 0)
+    plain = lambda b, s: (b, 0, 0)
+    whole = lambda b, s: (0, 0)
+    return pl.pallas_call(
+        partial(forward_kernel, heads, base),
+        out_shape=(
+            jax.ShapeDtypeStruct((blocks, rows, 256), jnp.bfloat16),
+            jax.ShapeDtypeStruct((blocks, rows, 384), jnp.float32),
+            jax.ShapeDtypeStruct((blocks, chans, NSTATE), jnp.float32),
+            jax.ShapeDtypeStruct((blocks, rows, 2 * HD), jnp.bfloat16),
+        ),
+        grid_spec=pltpu.PrefetchScalarGridSpec(
+            num_scalar_prefetch=1,
+            grid=(blocks,),
+            in_specs=[
+                pl.BlockSpec((1, rows, wide), held),
+                pl.BlockSpec(filt.shape, whole),
+                pl.BlockSpec((1, rows, 2 * HD), plain),
+                pl.BlockSpec(params.shape, whole),
+                pl.BlockSpec(skip.shape, whole),
+            ],
+            out_specs=(
+                pl.BlockSpec((1, rows, 256), held),
+                pl.BlockSpec((1, rows, 384), plain),
+                pl.BlockSpec((1, chans, NSTATE), plain),
+                pl.BlockSpec((1, rows, 2 * HD), plain),
+            ),
+            scratch_shapes=[
+                pltpu.VMEM((rows + 8, 512), jnp.float32),
+                pltpu.VMEM((chans, NSTATE), jnp.float32),
+                pltpu.VMEM((blocks * rows, HD), jnp.bfloat16),
+                pltpu.VMEM((blocks * rows, HD), jnp.bfloat16),
+            ],
+        ),
+        cost_estimate=pl.CostEstimate(
+            flops=25_000_000_000, transcendentals=0, bytes_accessed=12_000_000
+        ),
+        name="mixer_forward",
+    )(sched, proj, filt, table, params, skip)
+
+
+def mixer_backward(sched, proj, filt, table, params, skip, save, states, kv, d_mix, heads, base):
+    blocks, rows, wide = proj.shape
+    chans = heads * HEAD_M
+    held = lambda i, s: (s[blocks - 1 - i], 0, 0)
+    before = lambda i, s: (s[jnp.maximum(blocks - 2 - i, 0)], rows // 8 - 1, 0)
+    plain = lambda i, s: (blocks - 1 - i, 0, 0)
+    whole = lambda i, s: (0, 0)
+    return pl.pallas_call(
+        partial(backward_kernel, heads, base),
+        out_shape=(
+            jax.ShapeDtypeStruct((blocks, rows, wide), jnp.bfloat16),
+            jax.ShapeDtypeStruct((8, 512), jnp.float32),
+            jax.ShapeDtypeStruct((8, 128), jnp.float32),
+        ),
+        grid_spec=pltpu.PrefetchScalarGridSpec(
+            num_scalar_prefetch=1,
+            grid=(blocks,),
+            in_specs=[
+                pl.BlockSpec((1, rows, wide), held),
+                pl.BlockSpec((1, 8, wide), before),
+                pl.BlockSpec(filt.shape, whole),
+                pl.BlockSpec((1, rows, 2 * HD), plain),
+                pl.BlockSpec(params.shape, whole),
+                pl.BlockSpec(skip.shape, whole),
+                pl.BlockSpec((1, rows, 384), plain),
+                pl.BlockSpec((1, chans, NSTATE), plain),
+                pl.BlockSpec((blocks * rows, 2 * HD), whole),
+                pl.BlockSpec((1, rows, 256), held),
+            ],
+            out_specs=(
+                pl.BlockSpec((1, rows, wide), held),
+                pl.BlockSpec((8, 512), whole),
+                pl.BlockSpec((8, 128), whole),
+            ),
+            scratch_shapes=[
+                pltpu.VMEM((rows + 8, 512), jnp.float32),
+                pltpu.VMEM((rows + 8, 512), jnp.float32),
+                pltpu.VMEM((chans, NSTATE), jnp.float32),
+                pltpu.VMEM((blocks * rows, HD), jnp.float32),
+                pltpu.VMEM((blocks * rows, HD), jnp.float32),
+            ],
+        ),
+        cost_estimate=pl.CostEstimate(
+            flops=40_000_000_000, transcendentals=0, bytes_accessed=16_000_000
+        ),
+        name="mixer_backward",
+    )(sched, proj, proj, filt, table, params, skip, save, states, kv.reshape(-1, 2 * HD), d_mix)
+
+
+def head_plan(
+    block_input,
+    out_cotangent,
+    lengths,
+    slot_block,
+    norm_gains,
+    short_filter,
+    step_bias,
+    log_rate,
+    skip_gain,
+    mixer_in,
+    mixer_out,
+    attend_in,
+    attend_out,
+    gate_up,
+    down_weight,
+):
+    count = lax.axis_size("ctx")
+    groups = lax.axis_size("wsh")
+    ctx = lax.axis_index("ctx")
+    wsh = lax.axis_index("wsh")
+    rows, width = block_input.shape[1:]
+    block_rows = rows // 2
+    blocks = 2 * count
+    total_rows = count * rows
+    heads = MHEADS // count
+    chans = heads * HEAD_M
+    kv_head = ctx * KVH // count
+    units = gate_up.shape[2] // count
+    first_len = lengths[0, 0]
+    tokens = block_input[0]
+    cotangent = out_cotangent[0]
+    cols = lambda array, start, size: lax.dynamic_slice_in_dim(array, start, size, array.ndim - 1)
+    base = HD
+    step_pad = 128 - base - heads
+
+    in_cols = pick_columns(
+        jnp.stack([ctx, kv_head]), mixer_in, attend_in, norm_gains, heads
+    )
+    in_all = gather_wsh(in_cols, 1)
+    gains = gather_wsh(after(norm_gains, in_cols), 1).astype(jnp.float32)
+    out_rows = jnp.concatenate(
+        [
+            lax.dynamic_slice_in_dim(mixer_out, ctx * chans, chans, 0),
+            lax.dynamic_slice_in_dim(attend_out, ctx * HD, HD, 0),
+        ],
+        axis=0,
+    )
+    mlp_cols = cols(gate_up, ctx * units, units)
+    mlp_rows = lax.dynamic_slice_in_dim(down_weight, ctx * units, units, 0)
+    out_rows, mlp_cols, mlp_rows = after((out_rows, mlp_cols, mlp_rows), in_all)
+    out_mine = gather_wsh(out_rows, 1)
+    mlp_parts = swap_groups([mlp_cols] * groups)
+    down_all = jnp.concatenate(swap_groups([mlp_rows] * groups), axis=0)
+    gate_up_cols = jnp.concatenate(
+        [part[0] for part in mlp_parts] + [part[1] for part in mlp_parts], axis=1
+    )
+
+    peers = ctx ^ jnp.array(held_order(count), dtype=jnp.int32)
+    held = jnp.take(slot_block.reshape(count, 2), peers, axis=0, mode="clip").reshape(blocks)
+    logical_ids = jnp.arange(blocks, dtype=jnp.int32)
+
+    place = jnp.sum(
+        jnp.where(held[None, :] == logical_ids[:, None], logical_ids[None, :], 0), axis=1
+    )
+    starts = jnp.where(logical_ids * block_rows >= first_len, first_len, 0)
+    sched = jnp.concatenate([place, starts])
+    positions = jnp.arange(total_rows, dtype=jnp.int32)
+    seq_pos = positions - jnp.where(positions >= first_len, first_len, 0)
+    half = HD // 2
+    freqs = jnp.exp(jnp.arange(half, dtype=jnp.float32) * (-2.0 * math.log(ROPE_BASE) / HD))
+    angles = seq_pos.astype(jnp.float32)[:, None] * freqs[None, :]
+    cosines = jnp.cos(angles)
+    sines = jnp.sin(angles)
+    table = jnp.concatenate([cosines, cosines, -sines, sines], axis=1)
+    table = table.reshape(blocks, block_rows, 2 * HD)
+    filt = jnp.concatenate(
+        [
+            cols(short_filter, ctx * chans, chans),
+            jnp.zeros((KERNEL + 1, HD), jnp.float32),
+            short_filter[:, DSSM:],
+        ],
+        axis=1,
+    )
+    filt = jnp.pad(filt, ((0, 7 - KERNEL), (0, 0)))
+    mine = lambda array: lax.dynamic_slice_in_dim(array, ctx * heads, heads)
+    params = jnp.stack([mine(step_bias), jnp.exp(mine(log_rate))], axis=0)
+    params = jnp.pad(params, ((0, 6), (base, 128 - base - heads)))
+    skip = jnp.broadcast_to(jnp.repeat(mine(skip_gain), HEAD_M)[None, :], (8, chans))
+
+    first_scale = lax.rsqrt(jnp.mean(tokens * tokens, axis=-1, keepdims=True) + EPS)
+    unit_tokens = tokens * first_scale
+    units_first = gather_ctx(unit_tokens.astype(jnp.bfloat16)).reshape(total_rows, width)
+    cot_all = gather_ctx(after(cotangent.astype(jnp.bfloat16), units_first))
+    cot_all = cot_all.reshape(total_rows, width)
+    projected = matmul_back(units_first, in_all).reshape(blocks, block_rows, in_all.shape[0])
+    mixed_held, saved, states, kv = mixer_forward(
+        sched, projected, filt, table, params, skip, heads, base
+    )
+    mixed_held = mixed_held.reshape(total_rows, chans + HD)
+
+    hidden = tokens + scatter_ctx(
+        jnp.dot(mixed_held, out_mine, preferred_element_type=jnp.float32).reshape(
+            count, rows, width
+        )
+    )
+
+    second_scale = lax.rsqrt(jnp.mean(hidden * hidden, axis=-1, keepdims=True) + EPS)
+    unit_hidden = hidden * second_scale
+    normed_second = gather_ctx((unit_hidden * gains[1]).astype(jnp.bfloat16)).reshape(
+        total_rows, width
+    )
+    both = jnp.dot(normed_second, gate_up_cols, preferred_element_type=jnp.float32)
+    gate_part = both[:, : groups * units]
+    up_part = both[:, groups * units :]
+    silu_gate = jax.nn.silu(gate_part)
+    mlp_act = (silu_gate * up_part).astype(jnp.bfloat16)
+    d_mlp = matmul_back(cot_all, down_all)
+    d_gate = (d_mlp * up_part * silu_slope(gate_part)).astype(jnp.bfloat16)
+    d_up = (d_mlp * silu_gate).astype(jnp.bfloat16)
+    d_both = jnp.concatenate([d_gate, d_up], axis=1)
+    d_normed_second = scatter_ctx(matmul_back(d_both, gate_up_cols).reshape(count, rows, width))
+    mlp_parts = jnp.dot(mlp_act, down_all, preferred_element_type=jnp.float32)
+    mlp_parts = mlp_parts.astype(jnp.bfloat16).reshape(count, rows, width)
+
+    def norm_back(d_normed, gain, unit, unit_scale):
+        scaled = d_normed * gain
+        return unit_scale * (scaled - unit * jnp.mean(scaled * unit, axis=-1, keepdims=True))
+
+    hidden_grad = cotangent + norm_back(d_normed_second, gains[1], unit_hidden, second_scale)
+    hidden_b = gather_ctx(hidden_grad.astype(jnp.bfloat16)).reshape(total_rows, width)
+
+    both_grad = matmul_t(normed_second, d_both)
+    down_grad_t = matmul_t(cot_all, mlp_act)
+    gain_second_grad = jnp.sum(both_grad * gate_up_cols.astype(jnp.float32), axis=1) / gains[1]
+    mlp_grads = [
+        jnp.concatenate(
+            [
+                both_grad[:, k * units : (k + 1) * units],
+                both_grad[:, (groups + k) * units : (groups + k + 1) * units],
+                down_grad_t[:, k * units : (k + 1) * units],
+            ],
+            axis=1,
+        ).astype(jnp.bfloat16)
+        for k in range(groups)
+    ]
+    mlp_swapped = swap_groups(mlp_grads)
+    mlp_sum = sum(piece.astype(jnp.float32) for piece in mlp_swapped)
+    mlp_sum = mlp_sum.astype(jnp.bfloat16).reshape(count, width // count, 3 * units)
+
+    d_mix = matmul_back(hidden_b, out_mine).reshape(blocks, block_rows, chans + HD)
+    share = width // (count * groups)
+
+    def to_groups(grad):
+        parts = grad.reshape(count, groups, share, grad.shape[1])
+        return [
+            lax.dynamic_index_in_dim(parts, wsh ^ k, 1, keepdims=False).astype(jnp.bfloat16)
+            for k in range(groups)
+        ]
+
+    mlp_parts = after(mlp_parts, hidden_b)
+    places = jnp.array([held_order(count).index(k) for k in range(count)], dtype=jnp.int32)
+    by_device = jnp.take(places, ctx ^ jnp.arange(count, dtype=jnp.int32), mode="clip")
+    mlp_parts = jnp.take(mlp_parts, by_device, axis=0, mode="clip")
+    mlp_parts = trade_ctx(mlp_parts)
+    output = hidden + jnp.sum(mlp_parts.astype(jnp.float32), axis=0)
+    mlp_final = trade_ctx(after(mlp_sum, mlp_parts))
+    out_grads = to_groups(matmul_t(hidden_b, mixed_held))
+    out_swapped = swap_groups(out_grads)
+    out_sum = sum(piece.astype(jnp.float32) for piece in out_swapped)
+    d_held, filt_grad, head_grad = mixer_backward(
+        sched, projected, filt, table, params, skip, saved, states, kv, d_mix, heads, base
+    )
+    out_final = trade_ctx(after(out_sum.astype(jnp.bfloat16), mlp_parts))
+    gate_up_grad, down_grad, mixer_out_grad, attend_out_grad = finish_rest(
+        mlp_final, out_final, chans
+    )
+    mixer_out_grad = jnp.transpose(mixer_out_grad)
+    attend_out_grad = jnp.transpose(attend_out_grad)
+    d_held = d_held.reshape(total_rows, -1)
+    d_unit_first = scatter_ctx(
+        jnp.dot(d_held, in_all, preferred_element_type=jnp.float32).reshape(count, rows, width)
+    )
+    input_grad = hidden_grad + norm_back(d_unit_first, 1.0, unit_tokens, first_scale)
+
+    in_grad = matmul_t(units_first, d_held)
+    gain_first_grad = jnp.sum(in_grad * jnp.transpose(in_all).astype(jnp.float32), axis=1) / gains[0]
+    in_grad = in_grad * gains[0][:, None]
+    lane = jnp.arange(in_all.shape[0], dtype=jnp.int32)[None, :]
+    gain_lane = in_all.shape[0] - step_pad
+    in_grad = jnp.where(lane == gain_lane, gain_first_grad[:, None], in_grad)
+    in_grad = jnp.where(lane == gain_lane + 1, gain_second_grad[:, None], in_grad)
+    in_grads = to_groups(in_grad)
+    in_swapped = swap_groups(in_grads)
+    in_sum = sum(piece.astype(jnp.float32) for piece in in_swapped)
+    mixer_in_grad, attend_in_grad, last_cols = finish_in(
+        trade_ctx(after(in_sum.astype(jnp.bfloat16), (mlp_final, out_final))), heads
+    )
+    gain_place = gain_lane % 128
+    gains_grad = jnp.transpose(last_cols[:, gain_place : gain_place + 2])
+    side_by_side = lambda array: jnp.transpose(array, (1, 0, 2)).reshape(array.shape[1], -1)
+
+    small = jnp.concatenate([filt_grad.reshape(-1, 128), head_grad], axis=0)
+    small = gather_ctx(jnp.sum(gather_wsh(small[None]), axis=0))
+    small = jnp.take(small, by_device, axis=0, mode="clip")
+    filters = small[:, :-8].reshape(count, 8, 512)[:, : KERNEL + 1]
+    filter_grad = jnp.concatenate(
+        [side_by_side(filters[:, :, :chans]), jnp.sum(filters[:, :, 256:], axis=0)], axis=1
+    )
+    per_head = small[:, -8:-5, base : base + heads]
+    step_bias_all, log_rate_all, skip_all = [per_head[:, i].reshape(-1) for i in range(3)]
+    return (
+        output[None],
+        input_grad[None],
+        gains_grad,
+        filter_grad,
+        step_bias_all,
+        log_rate_all,
+        skip_all,
+        mixer_in_grad,
+        mixer_out_grad,
+        attend_in_grad,
+        attend_out_grad,
+        gate_up_grad,
+        down_grad,
+    )
+
+
+def on_device_heads(*args):
+    return head_plan(*args)
+
+
 def solution(mesh):
     placed = (
         P("wsh", "ctx", None),
@@ -479,8 +1274,9 @@
         P(None, None, "wsh"),
         P("wsh", None),
     )
+    per_heads = mesh.shape["ctx"] == QH
     return jax.shard_map(
-        on_device,
+        on_device_heads if per_heads else on_device,
         mesh=mesh,
         in_specs=placed,
         out_specs=(

time: 1580 us -> 460 us (0.29)
  waiting for transfers between devices: 1180 us -> 168 us
  matrix products: 154 us -> 31.1 us
  blocking collectives: 79.8 us -> 0 us
  starting transfers between devices: 0.94 us -> 80.7 us
  Pallas kernels: 0 us -> 71.5 us
    reduce_scatter x7 -> x0, waiting for transfers between devices: 630 us -> none  [the longest x1 168 us: on_device(): lax.psum_scatter(mixer_in_grad, ('ctx', 'wsh'), scatter_dimension=0, tile...]
    all_gather x8 -> x0, waiting for transfers between devices: 394 us -> none  [the longest x1 144 us: on_device(): lax.all_gather(gate_up, 'wsh', axis=2, tiled=True)]
    unnamed x23 -> x0, waiting for transfers between devices: 157 us -> none
    ppermute x0 -> x59, waiting for transfers between devices: none -> 156 us  [the longest x27 95.7 us: swap_groups(): lax.ppermute(pieces[k], 'wsh', xor_pairs(count, k))]
    dot_general x38 -> x4, matrix products: 104 us -> 9.1 us  [the longest x1 3.87 us: head_plan(): jnp.dot(d_held, in_all, preferred_element_type=jnp.float32)]
    pallas_call x0 -> x5, Pallas kernels: none -> 71.5 us  [the longest x1 40.5 us: mixer_backward(): pl.pallas_call(partial(backward_kernel, heads, base), out_shape=(jax.Shap...]
    ppermute x0 -> x59, starting transfers between devices: none -> 63.4 us  [the longest x27 37.6 us: swap_groups(): lax.ppermute(pieces[k], 'wsh', xor_pairs(count, k))]
    psum x1 -> x0, blocking collectives: 42.3 us -> none  [on_device(): lax.psum((step_bias_grad, log_rate_grad, g_skip, filter_grad), ('ctx', 'w...]
  transfers between devices with their start and end apart: 19 -> 63, of which waited for: 15 -> 33; matrix products, arithmetic and copies ran while one was open for 15% -> 24% of each run, Pallas kernels for 0% -> 6%
where the time goes in v2:
time: 460 us; the launch traced here: 458 us
  waiting for transfers between devices  168 us (37%)
  starting transfers between devices  80.7 us (18%)
  Pallas kernels  71.5 us (16%)
  local copies, waits for them, and re-layouts  62.5 us (14%)
  other arithmetic  41.5 us (9%)
  matrix products  31.1 us (7%)
    ppermute x27, waiting for transfers between devices, swap_groups(): lax.ppermute(pieces[k], 'wsh', xor_pairs(count, k))  95.7 us
    pallas_call x1, Pallas kernels, mixer_backward(): pl.pallas_call(partial(backward_kernel, heads, base), out_shape=(jax.Shap...  40.5 us
    ppermute x27, starting transfers between devices, swap_groups(): lax.ppermute(pieces[k], 'wsh', xor_pairs(count, k))  37.6 us
    pallas_call x1, Pallas kernels, mixer_forward(): pl.pallas_call(partial(forward_kernel, heads, base), out_shape=(jax.Shape...  24.1 us
    all_to_all x4, starting transfers between devices, trade_ctx(): return lax.all_to_all(parts, 'ctx', 0, 0, tiled=True)  17.3 us
    ppermute x5, waiting for transfers between devices, gather_ctx(): near_y = lax.ppermute(values, 'ctx', xor_pairs(count, 4))  14.4 us
    all_to_all x4, waiting for transfers between devices, trade_ctx(): return lax.all_to_all(parts, 'ctx', 0, 0, tiled=True)  12.4 us
    dot_general x4, matrix products, matmul_back(): lax.dot_general(left, right, (((1,), (1,)), ((), ())), preferred_element_...  11.7 us
  transfers between devices with their start and end apart: 63, of which 33 were waited for; matrix products, arithmetic and copies ran while one was open for 24% of the time, Pallas kernels for 6%

profile of v2, /device:TPU:8, one launch (start us, length us, event | category | flops | bytes accessed | tf_op | source)
XLA Modules:
  0.0 457.6 jit_solution(4067790937320731148)
XLA Ops:
  52.3 21.0 %collective-permute-done.4 = bf16[896,256]{1,0:T(8,128)(2,1)S(1)} collective-permute-done((bf16[896,256]{1,0:T(8,128)(2,1)}, bf16[896,256]{1,0:T(8,128)(2,1)S(1)}, u32[]{:S(2)}, u32[]{:S(2)}) %collective-permute-start.4) | collective-permute-done | bytes 458784 | tf_op jit(solution)/shard_map/ppermute | solution.py:523
  74.7 5.4 %collective-permute-done.5 = bf16[896,256]{1,0:T(8,128)(2,1)} collective-permute-done((bf16[896,256]{1,0:T(8,128)(2,1)}, bf16[896,256]{1,0:T(8,128)(2,1)}, u32[]{:S(2)}, u32[]{:S(2)}) %collective-permute-start.5) | collective-permute-done | bytes 458784 | tf_op jit(solution)/shard_map/ppermute | solution.py:523
  83.6 4.2 collective-permute-start.8
  90.3 5.9 %collective-permute-done.7 = bf16[256,256]{1,0:T(8,128)(2,1)S(1)} collective-permute-done((bf16[256,256]{1,0:T(8,128)(2,1)S(1)}, bf16[256,256]{1,0:T(8,128)(2,1)S(1)}, u32[]{:S(2)}, u32[]{:S(2)}) %collective-permute-start.7) | collective-permute-done | bytes 131104 | tf_op jit(solution)/shard_map/ppermute | solution.py:523
  99.3 3.3 collective-permute-start.24
  103.4 9.1 %collective-permute-done.24 = bf16[64,1024]{1,0:T(8,128)(2,1)S(1)} collective-permute-done((bf16[64,1024]{1,0:T(8,128)(2,1)S(1)}, bf16[64,1024]{1,0:T(8,128)(2,1)S(1)}, u32[]{:S(2)}, u32[]{:S(2)}) %collective-permute-start.24) | collective-permute-done | bytes 131104 | tf_op jit(solution)/shard_map/ppermute | solution.py:523
  115.9 6.4 %fusion.3.proj_ref.before_ref = f32[16,64,896]{2,1,0:T(8,128)} fusion(bf16[16,64,1024]{2,1,0:T(8,128)(2,1)S(1)} %bitcast.316, bf16[896,1024]{0,1:T(8,128)(2,1)} %constant_dynamic-update-slice_fusion.41), kind=kOutput, calls=%fused_computation.18 | convolution fusion | flops 1879048192 | bytes 7602176 | tf_op jit(solution)/shard_map/dot_general | solution.py:64
  122.9 24.1 %mixer_forward.1 = (bf16[16,64,256]{2,1,0:T(8,128)(2,1)}, f32[16,64,384]{2,1,0:T(8,128)}, f32[16,192,128]{2,1,0:T(8,128)}, bf16[16,64,128]{2,1,0:T(8,128)(2,1)}) custom-call(s32[32]{0:T(128)} %pad_add_fusion.sched_ref, f32[16,64,896]{2,1,0:T(8,128)} %fusion.3.proj_ref.before_ref, f32[8,512]{1,0:T(8,128)} %pad.8.filt_ref, ...), custom_call_target="tpu_custom_call" | custom-call | flops 24999999488 | bytes 12000000 | tf_op jit(solution)/shard_map/mixer_forward/pallas_call | solution.py:940
  154.8 5.8 %collective-permute-done.11 = bf16[128,1024]{1,0:T(8,128)(2,1)S(1)} collective-permute-done((bf16[128,1024]{1,0:T(8,128)(2,1)S(1)}, bf16[128,1024]{1,0:T(8,128)(2,1)S(1)}, u32[]{:S(2)}, u32[]{:S(2)}) %collective-permute-start.11) | collective-permute-done | bytes 262176 | tf_op jit(solution)/shard_map/ppermute | solution.py:500
  162.0 4.2 collective-permute-done.27
  166.5 5.3 %collective-permute-done.12 = bf16[128,1024]{1,0:T(8,128)(2,1)S(1)} collective-permute-done((bf16[128,1024]{1,0:T(8,128)(2,1)S(1)}, bf16[128,1024]{1,0:T(8,128)(2,1)S(1)}, u32[]{:S(2)}, u32[]{:S(2)}) %collective-permute-start.12) | collective-permute-done | bytes 262176 | tf_op jit(solution)/shard_map/ppermute | solution.py:507
  174.7 3.9 collective-permute-done.18
  183.1 4.3 collective-permute-done.19
  205.6 4.5 collective-permute-done.32
  213.1 5.2 %collective-permute-done.33 = bf16[128,1024]{1,0:T(8,128)(2,1)S(1)} collective-permute-done((bf16[128,1024]{1,0:T(8,128)(2,1)S(1)}, bf16[128,1024]{1,0:T(8,128)(2,1)S(1)}, u32[]{:S(2)}, u32[]{:S(2)}) %collective-permute-start.33) | collective-permute-done | bytes 262176 | tf_op jit(solution)/shard_map/ppermute | solution.py:507
  223.2 3.6 collective-permute-done.36
  237.4 6.6 %collective-permute-done.46 = bf16[1024,192]{0,1:T(8,128)(2,1)S(1)} collective-permute-done((bf16[1024,192]{0,1:T(8,128)(2,1)S(1)}, bf16[1024,192]{0,1:T(8,128)(2,1)S(1)}, u32[]{:S(2)}, u32[]{:S(2)}) %collective-permute-start.46) | collective-permute-done | bytes 393248 | tf_op jit(solution)/shard_map/ppermute | solution.py:523
  244.0 13.4 %collective-permute-done.47 = bf16[1024,192]{0,1:T(8,128)(2,1)S(1)} collective-permute-done((bf16[1024,192]{0,1:T(8,128)(2,1)S(1)}, bf16[1024,192]{0,1:T(8,128)(2,1)S(1)}, u32[]{:S(2)}, u32[]{:S(2)}) %collective-permute-start.47) | collective-permute-done | bytes 393248 | tf_op jit(solution)/shard_map/ppermute | solution.py:523
  257.5 7.0 %collective-permute-done.48 = bf16[1024,192]{0,1:T(8,128)(2,1)S(1)} collective-permute-done((bf16[1024,192]{0,1:T(8,128)(2,1)S(1)}, bf16[1024,192]{0,1:T(8,128)(2,1)S(1)}, u32[]{:S(2)}, u32[]{:S(2)}) %collective-permute-start.48) | collective-permute-done | bytes 393248 | tf_op jit(solution)/shard_map/ppermute | solution.py:523
  267.7 40.5 %mixer_backward.1 = (bf16[16,64,896]{2,1,0:T(8,128)(2,1)}, f32[8,512]{1,0:T(8,128)}, f32[8,128]{1,0:T(8,128)}) custom-call(s32[32]{0:T(128)} %pad_add_fusion.sched_ref, f32[16,64,896]{2,1,0:T(8,128)} %fusion.3.proj_ref.before_ref, f32[16,64,896]{2,1,0:T(8,128)} %fusion.3.proj_ref.before_ref, f32[8,512]{1,0:T(8,128)} %pad.8.filt_ref, ...), custom_call_target="tpu_custom_call" | custom-call | flops 40000000000 | bytes 16000000 | tf_op jit(solution)/shard_map/mixer_backward/pallas_call | solution.py:985
  313.6 7.6 %fusion = (f32[1024]{0:T(1024)}, f32[1024,896]{1,0:T(8,128)}) fusion(bf16[896,1024]{0,1:T(8,128)(2,1)} %constant_dynamic-update-slice_fusion.41, bf16[1024,1024]{1,0:T(8,128)(2,1)} %bitcast.317, bf16[1024,896]{1,0:T(8,128)(2,1)} %bitcast.324), kind=kOutput, calls=%fused_computation.6 | convolution fusion | flops 1881799680 | bytes 9441280 | tf_op jit(solution)/shard_map/dot_general | solution.py:58
  321.3 3.9 fusion.69
  330.3 3.8 gather_fusion.2
  334.1 4.5 all-to-all-start
  352.5 6.6 %collective-permute-done.56 = f32[40,128]{1,0:T(8,128)S(1)} collective-permute-done((f32[40,128]{1,0:T(8,128)S(1)}, f32[40,128]{1,0:T(8,128)S(1)}, u32[]{:S(2)}, u32[]{:S(2)}) %collective-permute-start.56) | collective-permute-done | bytes 20512 | tf_op jit(solution)/shard_map/ppermute | solution.py:480
  360.3 4.4 collective-permute-done.55
  372.7 24.6 %collective-permute-done.51 = bf16[8,32,256]{2,1,0:T(8,128)(2,1)S(1)} collective-permute-done((bf16[8,32,256]{2,1,0:T(8,128)(2,1)S(1)}, bf16[8,32,256]{2,1,0:T(8,128)(2,1)S(1)}, u32[]{:S(2)}, u32[]{:S(2)}) %collective-permute-start.51) | collective-permute-done | bytes 131104 | tf_op jit(solution)/shard_map/ppermute | solution.py:523
  418.5 5.2 %all-to-all-start.2 = ((bf16[8,32,256]{2,1,0:T(8,128)(2,1)}), bf16[8,32,256]{2,1,0:T(8,128)(2,1)}, u32[]{:S(2)}, u32[]{:S(2)}) async-start(bf16[8,32,256]{2,1,0:T(8,128)(2,1)} %fusion.45), calls=%async_computation.2 | async-start | bytes 262144 | tf_op jit(solution)/shard_map/all_to_all | solution.py:513
  425.8 3.5 all-to-all-done.2.out_ref
  429.3 3.5 all-to-all-start.1
  435.0 6.1 %all-to-all-done.1 = bf16[8,128,192]{1,2,0:T(8,128)(2,1)S(1)} async-done(((bf16[8,128,192]{1,2,0:T(8,128)(2,1)}), bf16[8,128,192]{1,2,0:T(8,128)(2,1)S(1)}, u32[]{:S(2)}, u32[]{:S(2)}) %all-to-all-start.1) | async-done | bytes 393248 | tf_op jit(solution)/shard_map/all_to_all | solution.py:513
  441.0 4.1 all-to-all-start.3
  (397 shorter events, 194.2 us)
Async XLA Ops:
  3.8 45.7 %collective-permute-start.1 = (bf16[128,1024]{1,0:T(8,128)(2,1)}, bf16[128,1024]{1,0:T(8,128)(2,1)S(1)}, u32[]{:S(2)}, u32[]{:S(2)}) collective-permute-start(bf16[128,1024]{1,0:T(8,128)(2,1)} %fusion.34), channel_id=1, source_target_pairs={{0,16},{4,20},{8,24},{12,28},{16,0},{20,4},{24,8},{28,12},{1,17},{... | collective-permute-start | bytes 786440 | tf_op jit(solution)/shard_map/ppermute | solution.py:480
  5.4 44.2 %collective-permute-start = (bf16[128,1024]{1,0:T(8,128)(2,1)}, bf16[128,1024]{1,0:T(8,128)(2,1)S(1)}, u32[]{:S(2)}, u32[]{:S(2)}) collective-permute-start(bf16[128,1024]{1,0:T(8,128)(2,1)} %fusion.34), channel_id=1, source_target_pairs={{0,8},{4,12},{8,0},{12,4},{16,24},{20,28},{24,16},{28,20},{1,9},{5... | collective-permute-start | bytes 786440 | tf_op jit(solution)/shard_map/ppermute | solution.py:479
  10.3 35.4 %collective-permute-start.16 = (bf16[2,256]{1,0:T(2,128)(2,1)}, bf16[2,256]{1,0:T(2,128)(2,1)}, u32[]{:S(2)}, u32[]{:S(2)}) collective-permute-start(bf16[2,256]{1,0:T(2,128)(2,1)} %refs_11_.1), channel_id=1, source_target_pairs={{0,3},{1,2},{2,1},{3,0},{4,7},{5,6},{6,5},{7,4},{8,11},{9,10},{10,... | collective-permute-start | bytes 3080 | tf_op jit(solution)/shard_map/ppermute | solution.py:523
  11.9 30.9 %collective-permute-start.15 = (bf16[2,256]{1,0:T(2,128)(2,1)}, bf16[2,256]{1,0:T(2,128)(2,1)}, u32[]{:S(2)}, u32[]{:S(2)}) collective-permute-start(bf16[2,256]{1,0:T(2,128)(2,1)} %refs_11_.1), channel_id=1, source_target_pairs={{0,2},{1,3},{2,0},{3,1},{4,6},{5,7},{6,4},{7,5},{8,10},{9,11},{10,... | collective-permute-start | bytes 3080 | tf_op jit(solution)/shard_map/ppermute | solution.py:523
  13.1 26.9 %collective-permute-start.14 = (bf16[2,256]{1,0:T(2,128)(2,1)}, bf16[2,256]{1,0:T(2,128)(2,1)}, u32[]{:S(2)}, u32[]{:S(2)}) collective-permute-start(bf16[2,256]{1,0:T(2,128)(2,1)} %refs_11_.1), channel_id=1, source_target_pairs={{0,1},{1,0},{2,3},{3,2},{4,5},{5,4},{6,7},{7,6},{8,9},{9,8},{10,11... | collective-permute-start | bytes 3080 | tf_op jit(solution)/shard_map/ppermute | solution.py:523
  40.1 34.4 %collective-permute-start.6 = (bf16[896,256]{1,0:T(8,128)(2,1)}, bf16[896,256]{1,0:T(8,128)(2,1)S(1)}, u32[]{:S(2)}, u32[]{:S(2)}) collective-permute-start(bf16[896,256]{1,0:T(8,128)(2,1)} %pick_columns.1), channel_id=1, source_target_pairs={{0,3},{1,2},{2,1},{3,0},{4,7},{5,6},{6,5},{7,4},{8,11},{9,10},{10,... | collective-permute-start | bytes 1376264 | tf_op jit(solution)/shard_map/ppermute | solution.py:523
  42.8 37.2 %collective-permute-start.5 = (bf16[896,256]{1,0:T(8,128)(2,1)}, bf16[896,256]{1,0:T(8,128)(2,1)}, u32[]{:S(2)}, u32[]{:S(2)}) collective-permute-start(bf16[896,256]{1,0:T(8,128)(2,1)} %pick_columns.1), channel_id=1, source_target_pairs={{0,2},{1,3},{2,0},{3,1},{4,6},{5,7},{6,4},{7,5},{8,10},{9,11},{10,... | collective-permute-start | bytes 1376264 | tf_op jit(solution)/shard_map/ppermute | solution.py:523
  45.7 27.5 %collective-permute-start.4 = (bf16[896,256]{1,0:T(8,128)(2,1)}, bf16[896,256]{1,0:T(8,128)(2,1)S(1)}, u32[]{:S(2)}, u32[]{:S(2)}) collective-permute-start(bf16[896,256]{1,0:T(8,128)(2,1)} %pick_columns.1), channel_id=1, source_target_pairs={{0,1},{1,0},{2,3},{3,2},{4,5},{5,4},{6,7},{7,6},{8,9},{9,8},{10,11... | collective-permute-start | bytes 1376264 | tf_op jit(solution)/shard_map/ppermute | solution.py:523
  50.3 39.0 %collective-permute-start.2 = (bf16[128,1024]{1,0:T(8,128)(2,1)}, bf16[128,1024]{1,0:T(8,128)(2,1)S(1)}, u32[]{:S(2)}, u32[]{:S(2)}) collective-permute-start(bf16[128,1024]{1,0:T(8,128)(2,1)} %broadcast_select_fusion.3), channel_id=1, source_target_pairs={{0,16},{4,12},{8,24},{12,4},{16,0},{20,28},{24,8},{28,20},{1,17},{... | collective-permute-start | bytes 786440 | tf_op jit(solution)/shard_map/ppermute | solution.py:481
  82.9 19.8 %collective-permute-start.9 = (bf16[256,256]{1,0:T(8,128)(2,1)S(1)}, bf16[256,256]{1,0:T(8,128)(2,1)S(1)}, u32[]{:S(2)}, u32[]{:S(2)}) collective-permute-start(bf16[256,256]{1,0:T(8,128)(2,1)S(1)} %copy-done.16), channel_id=1, source_target_pairs={{0,3},{1,2},{2,1},{3,0},{4,7},{5,6},{6,5},{7,4},{8,11},{9,10},{10,... | collective-permute-start | bytes 393224 | tf_op jit(solution)/shard_map/ppermute | solution.py:523
  83.6 15.8 %collective-permute-start.8 = (bf16[256,256]{1,0:T(8,128)(2,1)S(1)}, bf16[256,256]{1,0:T(8,128)(2,1)S(1)}, u32[]{:S(2)}, u32[]{:S(2)}) collective-permute-start(bf16[256,256]{1,0:T(8,128)(2,1)S(1)} %copy-done.16), channel_id=1, source_target_pairs={{0,2},{1,3},{2,0},{3,1},{4,6},{5,7},{6,4},{7,5},{8,10},{9,11},{10,... | collective-permute-start | bytes 393224 | tf_op jit(solution)/shard_map/ppermute | solution.py:523
  87.8 61.2 %collective-permute-start.26 = (bf16[64,1024]{1,0:T(8,128)(2,1)S(1)}, bf16[64,1024]{1,0:T(8,128)(2,1)S(1)}, u32[]{:S(2)}, u32[]{:S(2)}) collective-permute-start(bf16[64,1024]{1,0:T(8,128)(2,1)S(1)} %constant_dynamic-slice_fusion), channel_id=1, source_target_pairs={{0,3},{1,2},{2,1},{3,0},{4,7},{5,6},{6,5},{7,4},{8,11},{9,10},{10,... | collective-permute-start | bytes 393224 | tf_op jit(solution)/shard_map/ppermute | solution.py:523
  89.4 26.2 %collective-permute-start.3 = (bf16[4,128,1024]{2,1,0:T(8,128)(2,1)S(1)}, bf16[4,128,1024]{2,1,0:T(8,128)(2,1)S(1)}, u32[]{:S(2)}, u32[]{:S(2)}) collective-permute-start(bf16[4,128,1024]{2,1,0:T(8,128)(2,1)S(1)} %pad_maximum_fusion), channel_id=1, source_target_pairs={{0,4},{4,0},{8,12},{12,8},{16,20},{20,16},{24,28},{28,24},{1,5},{5... | collective-permute-start | bytes 3145736 | tf_op jit(solution)/shard_map/ppermute | solution.py:487
  96.2 52.7 %collective-permute-start.25 = (bf16[64,1024]{1,0:T(8,128)(2,1)S(1)}, bf16[64,1024]{1,0:T(8,128)(2,1)S(1)}, u32[]{:S(2)}, u32[]{:S(2)}) collective-permute-start(bf16[64,1024]{1,0:T(8,128)(2,1)S(1)} %constant_dynamic-slice_fusion), channel_id=1, source_target_pairs={{0,2},{1,3},{2,0},{3,1},{4,6},{5,7},{6,4},{7,5},{8,10},{9,11},{10,... | collective-permute-start | bytes 393224 | tf_op jit(solution)/shard_map/ppermute | solution.py:523
  102.7 47.3 %collective-permute-start.23 = (bf16[2,1024,64]{1,2,0:T(8,128)(2,1)S(1)}, bf16[2,1024,64]{1,2,0:T(8,128)(2,1)S(1)}, u32[]{:S(2)}, u32[]{:S(2)}) collective-permute-start(bf16[2,1024,64]{1,2,0:T(8,128)(2,1)S(1)} %copy.103), channel_id=1, source_target_pairs={{0,3},{1,2},{2,1},{3,0},{4,7},{5,6},{6,5},{7,4},{8,11},{9,10},{10,... | collective-permute-start | bytes 786440 | tf_op jit(solution)/shard_map/ppermute | solution.py:523
  112.5 37.5 %collective-permute-start.22 = (bf16[2,1024,64]{1,2,0:T(8,128)(2,1)S(1)}, bf16[2,1024,64]{1,2,0:T(8,128)(2,1)S(1)}, u32[]{:S(2)}, u32[]{:S(2)}) collective-permute-start(bf16[2,1024,64]{1,2,0:T(8,128)(2,1)S(1)} %copy.103), channel_id=1, source_target_pairs={{0,2},{1,3},{2,0},{3,1},{4,6},{5,7},{6,4},{7,5},{8,10},{9,11},{10,... | collective-permute-start | bytes 786440 | tf_op jit(solution)/shard_map/ppermute | solution.py:523
  115.7 33.4 %collective-permute-start.21 = (bf16[2,1024,64]{1,2,0:T(8,128)(2,1)S(1)}, bf16[2,1024,64]{1,2,0:T(8,128)(2,1)S(1)}, u32[]{:S(2)}, u32[]{:S(2)}) collective-permute-start(bf16[2,1024,64]{1,2,0:T(8,128)(2,1)S(1)} %copy.103), channel_id=1, source_target_pairs={{0,1},{1,0},{2,3},{3,2},{4,5},{5,4},{6,7},{7,6},{8,9},{9,8},{10,11... | collective-permute-start | bytes 786440 | tf_op jit(solution)/shard_map/ppermute | solution.py:523
  228.6 15.4 %collective-permute-start.46 = (bf16[1024,192]{0,1:T(8,128)(2,1)S(1)}, bf16[1024,192]{0,1:T(8,128)(2,1)S(1)}, u32[]{:S(2)}, u32[]{:S(2)}) collective-permute-start(bf16[1024,192]{0,1:T(8,128)(2,1)S(1)} %pad_maximum_fusion.8), channel_id=1, source_target_pairs={{0,1},{1,0},{2,3},{3,2},{4,5},{5,4},{6,7},{7,6},{8,9},{9,8},{10,11... | collective-permute-start | bytes 1179656 | tf_op jit(solution)/shard_map/ppermute | solution.py:523
  230.7 26.8 %collective-permute-start.47 = (bf16[1024,192]{0,1:T(8,128)(2,1)S(1)}, bf16[1024,192]{0,1:T(8,128)(2,1)S(1)}, u32[]{:S(2)}, u32[]{:S(2)}) collective-permute-start(bf16[1024,192]{0,1:T(8,128)(2,1)S(1)} %pad_maximum_fusion.9), channel_id=1, source_target_pairs={{0,2},{1,3},{2,0},{3,1},{4,6},{5,7},{6,4},{7,5},{8,10},{9,11},{10,... | collective-permute-start | bytes 1179656 | tf_op jit(solution)/shard_map/ppermute | solution.py:523
  231.1 33.3 %collective-permute-start.48 = (bf16[1024,192]{0,1:T(8,128)(2,1)S(1)}, bf16[1024,192]{0,1:T(8,128)(2,1)S(1)}, u32[]{:S(2)}, u32[]{:S(2)}) collective-permute-start(bf16[1024,192]{0,1:T(8,128)(2,1)S(1)} %pad_maximum_fusion.10), channel_id=1, source_target_pairs={{0,3},{1,2},{2,1},{3,0},{4,7},{5,6},{6,5},{7,4},{8,11},{9,10},{10,... | collective-permute-start | bytes 1179656 | tf_op jit(solution)/shard_map/ppermute | solution.py:523
  234.5 30.3 %collective-permute-start.38 = (bf16[4,128,1024]{2,1,0:T(8,128)(2,1)S(1)}, bf16[4,128,1024]{2,1,0:T(8,128)(2,1)S(1)}, u32[]{:S(2)}, u32[]{:S(2)}) collective-permute-start(bf16[4,128,1024]{2,1,0:T(8,128)(2,1)S(1)} %pad_maximum_fusion.4), channel_id=1, source_target_pairs={{0,4},{4,0},{8,12},{12,8},{16,20},{20,16},{24,28},{28,24},{1,5},{5... | collective-permute-start | bytes 3145736 | tf_op jit(solution)/shard_map/ppermute | solution.py:487
  310.2 37.7 %collective-permute-start.53 = (f32[1,40,128]{2,1,0:T(8,128)}, f32[1,40,128]{2,1,0:T(8,128)}, u32[]{:S(2)}, u32[]{:S(2)}) collective-permute-start(f32[1,40,128]{2,1,0:T(8,128)} %maximum_bitcast_fusion), channel_id=1, source_target_pairs={{0,2},{1,3},{2,0},{3,1},{4,6},{5,7},{6,4},{7,5},{8,10},{9,11},{10,... | collective-permute-start | bytes 61448 | tf_op jit(solution)/shard_map/ppermute | solution.py:523
  310.2 36.0 %collective-permute-start.52 = (f32[1,40,128]{2,1,0:T(8,128)}, f32[1,40,128]{2,1,0:T(8,128)}, u32[]{:S(2)}, u32[]{:S(2)}) collective-permute-start(f32[1,40,128]{2,1,0:T(8,128)} %maximum_bitcast_fusion), channel_id=1, source_target_pairs={{0,1},{1,0},{2,3},{3,2},{4,5},{5,4},{6,7},{7,6},{8,9},{9,8},{10,11... | collective-permute-start | bytes 61448 | tf_op jit(solution)/shard_map/ppermute | solution.py:523
  312.5 36.1 %collective-permute-start.54 = (f32[1,40,128]{2,1,0:T(8,128)}, f32[1,40,128]{2,1,0:T(8,128)}, u32[]{:S(2)}, u32[]{:S(2)}) collective-permute-start(f32[1,40,128]{2,1,0:T(8,128)} %maximum_bitcast_fusion), channel_id=1, source_target_pairs={{0,3},{1,2},{2,1},{3,0},{4,7},{5,6},{6,5},{7,4},{8,11},{9,10},{10,... | collective-permute-start | bytes 61448 | tf_op jit(solution)/shard_map/ppermute | solution.py:523
  334.1 84.3 %all-to-all-start = ((bf16[8,128,1024]{2,1,0:T(8,128)(2,1)}), bf16[8,128,1024]{2,1,0:T(8,128)(2,1)}, u32[]{:S(2)}, u32[]{:S(2)}) async-start(bf16[8,128,1024]{2,1,0:T(8,128)(2,1)} %gather_fusion.2), calls=%async_computation | async-start | bytes 4194304 | tf_op jit(solution)/shard_map/all_to_all | solution.py:513
  338.7 62.4 %collective-permute-start.39 = (bf16[4,128,1024]{2,1,0:T(8,128)(2,1)}, bf16[4,128,1024]{2,1,0:T(8,128)(2,1)}, u32[]{:S(2)}, u32[]{:S(2)}) collective-permute-start(bf16[4,128,1024]{2,1,0:T(8,128)(2,1)} %bitcast.59), channel_id=1, source_target_pairs={{0,4},{4,0},{8,12},{12,8},{16,20},{20,16},{24,28},{28,24},{1,5},{5... | collective-permute-start | bytes 3145736 | tf_op jit(solution)/shard_map/ppermute | solution.py:496
  342.8 72.6 %collective-permute-start.43 = (bf16[8,32,896]{2,1,0:T(8,128)(2,1)}, bf16[8,32,896]{2,1,0:T(8,128)(2,1)}, u32[]{:S(2)}, u32[]{:S(2)}) collective-permute-start(bf16[8,32,896]{2,1,0:T(8,128)(2,1)} %get-tuple-element.134), channel_id=1, source_target_pairs={{0,1},{1,0},{2,3},{3,2},{4,5},{5,4},{6,7},{7,6},{8,9},{9,8},{10,11... | collective-permute-start | bytes 1376264 | tf_op jit(solution)/shard_map/ppermute | solution.py:523
  346.1 23.2 %collective-permute-start.49 = (bf16[8,32,256]{2,1,0:T(8,128)(2,1)}, bf16[8,32,256]{2,1,0:T(8,128)(2,1)S(1)}, u32[]{:S(2)}, u32[]{:S(2)}) collective-permute-start(bf16[8,32,256]{2,1,0:T(8,128)(2,1)} %get-tuple-element.145), channel_id=1, source_target_pairs={{0,1},{1,0},{2,3},{3,2},{4,5},{5,4},{6,7},{7,6},{8,9},{9,8},{10,11... | collective-permute-start | bytes 393224 | tf_op jit(solution)/shard_map/ppermute | solution.py:523
  351.0 13.6 %collective-permute-start.55 = (f32[40,128]{1,0:T(8,128)S(1)}, f32[40,128]{1,0:T(8,128)S(1)}, u32[]{:S(2)}, u32[]{:S(2)}) collective-permute-start(f32[40,128]{1,0:T(8,128)S(1)} %reduce_sum.98), channel_id=1, source_target_pairs={{0,8},{4,12},{8,0},{12,4},{16,24},{20,28},{24,16},{28,20},{1,9},{5... | collective-permute-start | bytes 61448 | tf_op jit(solution)/shard_map/ppermute | solution.py:479
  368.5 28.8 %collective-permute-start.51 = (bf16[8,32,256]{2,1,0:T(8,128)(2,1)S(1)}, bf16[8,32,256]{2,1,0:T(8,128)(2,1)S(1)}, u32[]{:S(2)}, u32[]{:S(2)}) collective-permute-start(bf16[8,32,256]{2,1,0:T(8,128)(2,1)S(1)} %get-tuple-element.147), channel_id=1, source_target_pairs={{0,3},{1,2},{2,1},{3,0},{4,7},{5,6},{6,5},{7,4},{8,11},{9,10},{10,... | collective-permute-start | bytes 393224 | tf_op jit(solution)/shard_map/ppermute | solution.py:523
  369.4 46.0 %collective-permute-start.44 = (bf16[8,32,896]{2,1,0:T(8,128)(2,1)}, bf16[8,32,896]{2,1,0:T(8,128)(2,1)}, u32[]{:S(2)}, u32[]{:S(2)}) collective-permute-start(bf16[8,32,896]{2,1,0:T(8,128)(2,1)} %get-tuple-element.135), channel_id=1, source_target_pairs={{0,2},{1,3},{2,0},{3,1},{4,6},{5,7},{6,4},{7,5},{8,10},{9,11},{10,... | collective-permute-start | bytes 1376264 | tf_op jit(solution)/shard_map/ppermute | solution.py:523
  371.8 44.2 %collective-permute-start.45 = (bf16[8,32,896]{2,1,0:T(8,128)(2,1)}, bf16[8,32,896]{2,1,0:T(8,128)(2,1)}, u32[]{:S(2)}, u32[]{:S(2)}) collective-permute-start(bf16[8,32,896]{2,1,0:T(8,128)(2,1)} %get-tuple-element.136), channel_id=1, source_target_pairs={{0,3},{1,2},{2,1},{3,0},{4,7},{5,6},{6,5},{7,4},{8,11},{9,10},{10,... | collective-permute-start | bytes 1376264 | tf_op jit(solution)/shard_map/ppermute | solution.py:523
  (90 other events, 637.0 us)

commit v3 on v2

--- a/solution.py
+++ b/solution.py
@@ -24,8 +24,9 @@
 EPS = 1e-05
 ROPE_BASE = 100000000000.0
 HIGH = lax.Precision.HIGHEST
-SSD = HIGH
+SSD = None
 NEG_LARGE = -1e30
+GAIN_ROW = 880
 
 
 def rms_norm(values, gain):
@@ -473,7 +474,7 @@
     return list(range(0, count, 2)) + list(range(1, count, 2))
 
 
-def gather_ctx(values):
+def gather_ctx(values, with_far=False):
     count = lax.axis_size("ctx")
     first_core = lax.axis_index("ctx") % 2 == 0
     near_x = lax.ppermute(values, "ctx", xor_pairs(count, 2))
@@ -485,7 +486,8 @@
     )
     mine = jnp.stack([values, near_x, near_y, far], axis=0)
     other = lax.ppermute(mine, "ctx", xor_pairs(count, 1))
-    return jnp.concatenate([mine, other], axis=0)
+    whole = jnp.concatenate([mine, other], axis=0)
+    return (whole, far) if with_far else whole
 
 
 def scatter_ctx(parts):
@@ -493,9 +495,8 @@
     half = count // 2
     first_core = lax.axis_index("ctx") % 2 == 0
     wire = lambda piece: piece.astype(jnp.bfloat16)
-    sums = parts[:half] + lax.ppermute(
-        wire(parts[half:]), "ctx", xor_pairs(count, 1)
-    ).astype(jnp.float32)
+    crossed = lax.ppermute(wire(parts[half:]), "ctx", xor_pairs(count, 1))
+    sums = parts[:half] + crossed.astype(jnp.float32)
     own, near_x, near_y, far = [sums[place] for place in range(half)]
     passed = lax.ppermute(
         wire(far), "ctx", [(index, index ^ (2 if index % 2 == 0 else 4)) for index in range(count)]
@@ -612,6 +613,10 @@
     here = lax.broadcasted_iota(jnp.int32, (HEAD_M, HEAD_M), 1)
     chosen = jnp.where((here == there + ctx * heads) & (there < heads), 1.0, 0.0)
     put(768 + HD, dot_dims(chosen.astype(jnp.bfloat16), steps, 1, 0))
+    turn_row = lax.broadcasted_iota(jnp.int32, (16, width), 0)
+    second = gain_ref[1:2, :].astype(jnp.float32)
+    both = jnp.where(turn_row == 0, gain, jnp.where(turn_row == 1, second, 0.0))
+    out_ref[GAIN_ROW : GAIN_ROW + 16, :] = both.astype(jnp.bfloat16)
 
 
 def pick_columns(where, mixer_in, attend_in, gains, heads):
@@ -685,31 +690,34 @@
     )(final)
 
 
-def finish_rest_kernel(chans, mlp_ref, out_ref, gate_up_ref, down_ref, mixer_ref, attend_ref):
-    count = mlp_ref.shape[0]
-    units = mlp_ref.shape[2] // 3
-    parts = [mlp_ref[c].astype(jnp.float32) for c in range(count)]
-    gate_up_ref[0] = jnp.concatenate([p[:, :units] for p in parts], axis=1)
-    gate_up_ref[1] = jnp.concatenate([p[:, units : 2 * units] for p in parts], axis=1)
-    for c in range(count):
-        down_ref[c * units : (c + 1) * units, :] = jnp.transpose(parts[c][:, 2 * units :])
-    outs = [out_ref[c].astype(jnp.float32) for c in range(count)]
+def finish_rest_kernel(chans, units, share, parts_ref, gate_up_ref, down_ref, mixer_ref, attend_ref):
+    count = parts_ref.shape[0]
+    parts = [parts_ref[c].astype(jnp.float32) for c in range(count)]
+    for place in range(2):
+        gate_up_ref[place] = jnp.concatenate(
+            [jnp.transpose(p[place * units : (place + 1) * units]) for p in parts], axis=1
+        )
+    outs = []
+    for c, p in enumerate(parts):
+        down_ref[c * units : (c + 1) * units, :] = p[2 * units : 3 * units]
+        rest = range(3 * units, p.shape[0], share)
+        outs.append(jnp.concatenate([p[start : start + share] for start in rest], axis=1))
     mixer_ref[...] = jnp.concatenate([item[:, :chans] for item in outs], axis=1)
     attend_ref[...] = jnp.concatenate([item[:, chans:] for item in outs], axis=1)
 
 
-def finish_rest(mlp, out, chans):
-    count, share, units = mlp.shape[0], mlp.shape[1], mlp.shape[2] // 3
+def finish_rest(parts, chans, units, share):
+    count, _, wide = parts.shape
     return pl.pallas_call(
-        partial(finish_rest_kernel, chans),
+        partial(finish_rest_kernel, chans, units, share),
         out_shape=(
-            jax.ShapeDtypeStruct((2, share, count * units), jnp.float32),
-            jax.ShapeDtypeStruct((count * units, share), jnp.float32),
-            jax.ShapeDtypeStruct((out.shape[1], count * chans), jnp.float32),
-            jax.ShapeDtypeStruct((out.shape[1], count * HD), jnp.float32),
+            jax.ShapeDtypeStruct((2, wide, count * units), jnp.float32),
+            jax.ShapeDtypeStruct((count * units, wide), jnp.float32),
+            jax.ShapeDtypeStruct((share, count * chans), jnp.float32),
+            jax.ShapeDtypeStruct((share, count * HD), jnp.float32),
         ),
         name="finish_rest",
-    )(mlp, out)
+    )(parts)
 
 
 def forward_kernel(
@@ -1064,7 +1072,7 @@
         jnp.stack([ctx, kv_head]), mixer_in, attend_in, norm_gains, heads
     )
     in_all = gather_wsh(in_cols, 1)
-    gains = gather_wsh(after(norm_gains, in_cols), 1).astype(jnp.float32)
+    gains = in_all[GAIN_ROW : GAIN_ROW + 2].astype(jnp.float32)
     out_rows = jnp.concatenate(
         [
             lax.dynamic_slice_in_dim(mixer_out, ctx * chans, chans, 0),
@@ -1072,15 +1080,21 @@
         ],
         axis=0,
     )
-    mlp_cols = cols(gate_up, ctx * units, units)
-    mlp_rows = lax.dynamic_slice_in_dim(down_weight, ctx * units, units, 0)
-    out_rows, mlp_cols, mlp_rows = after((out_rows, mlp_cols, mlp_rows), in_all)
+    mlp_pack = jnp.concatenate(
+        [
+            jnp.transpose(cols(gate_up[0], ctx * units, units)),
+            jnp.transpose(cols(gate_up[1], ctx * units, units)),
+            lax.dynamic_slice_in_dim(down_weight, ctx * units, units, 0),
+        ],
+        axis=0,
+    )
+    out_rows, mlp_pack = after((out_rows, mlp_pack), in_all)
     out_mine = gather_wsh(out_rows, 1)
-    mlp_parts = swap_groups([mlp_cols] * groups)
-    down_all = jnp.concatenate(swap_groups([mlp_rows] * groups), axis=0)
-    gate_up_cols = jnp.concatenate(
-        [part[0] for part in mlp_parts] + [part[1] for part in mlp_parts], axis=1
-    )
+    packs = swap_groups([mlp_pack] * groups)
+    gate_up_rows = jnp.concatenate(
+        [pack[:units] for pack in packs] + [pack[units : 2 * units] for pack in packs], axis=0
+    )
+    down_all = jnp.concatenate([pack[2 * units :] for pack in packs], axis=0)
 
     peers = ctx ^ jnp.array(held_order(count), dtype=jnp.int32)
     held = jnp.take(slot_block.reshape(count, 2), peers, axis=0, mode="clip").reshape(blocks)
@@ -1114,9 +1128,11 @@
     params = jnp.pad(params, ((0, 6), (base, 128 - base - heads)))
     skip = jnp.broadcast_to(jnp.repeat(mine(skip_gain), HEAD_M)[None, :], (8, chans))
 
+    tokens = after(tokens, in_cols)
     first_scale = lax.rsqrt(jnp.mean(tokens * tokens, axis=-1, keepdims=True) + EPS)
     unit_tokens = tokens * first_scale
     units_first = gather_ctx(unit_tokens.astype(jnp.bfloat16)).reshape(total_rows, width)
+    units_t = lax.optimization_barrier(jnp.transpose(units_first))
     cot_all = gather_ctx(after(cotangent.astype(jnp.bfloat16), units_first))
     cot_all = cot_all.reshape(total_rows, width)
     projected = matmul_back(units_first, in_all).reshape(blocks, block_rows, in_all.shape[0])
@@ -1136,7 +1152,7 @@
     normed_second = gather_ctx((unit_hidden * gains[1]).astype(jnp.bfloat16)).reshape(
         total_rows, width
     )
-    both = jnp.dot(normed_second, gate_up_cols, preferred_element_type=jnp.float32)
+    both = matmul_back(normed_second, gate_up_rows)
     gate_part = both[:, : groups * units]
     up_part = both[:, groups * units :]
     silu_gate = jax.nn.silu(gate_part)
@@ -1145,34 +1161,40 @@
     d_gate = (d_mlp * up_part * silu_slope(gate_part)).astype(jnp.bfloat16)
     d_up = (d_mlp * silu_gate).astype(jnp.bfloat16)
     d_both = jnp.concatenate([d_gate, d_up], axis=1)
-    d_normed_second = scatter_ctx(matmul_back(d_both, gate_up_cols).reshape(count, rows, width))
-    mlp_parts = jnp.dot(mlp_act, down_all, preferred_element_type=jnp.float32)
-    mlp_parts = mlp_parts.astype(jnp.bfloat16).reshape(count, rows, width)
+    d_normed_second = scatter_ctx(
+        jnp.dot(d_both, gate_up_rows, preferred_element_type=jnp.float32).reshape(
+            count, rows, width
+        )
+    )
 
     def norm_back(d_normed, gain, unit, unit_scale):
         scaled = d_normed * gain
         return unit_scale * (scaled - unit * jnp.mean(scaled * unit, axis=-1, keepdims=True))
 
     hidden_grad = cotangent + norm_back(d_normed_second, gains[1], unit_hidden, second_scale)
-    hidden_b = gather_ctx(hidden_grad.astype(jnp.bfloat16)).reshape(total_rows, width)
-
-    both_grad = matmul_t(normed_second, d_both)
-    down_grad_t = matmul_t(cot_all, mlp_act)
-    gain_second_grad = jnp.sum(both_grad * gate_up_cols.astype(jnp.float32), axis=1) / gains[1]
+    hidden_b, hidden_far = gather_ctx(hidden_grad.astype(jnp.bfloat16), True)
+    hidden_b = hidden_b.reshape(total_rows, width)
+
+    both_grad = matmul_t(d_both, normed_second)
+    down_local = matmul_t(mlp_act, cot_all)
+    gain_second_grad = jnp.sum(both_grad * gate_up_rows.astype(jnp.float32), axis=0) / gains[1]
+    inner_units = groups * units
     mlp_grads = [
         jnp.concatenate(
             [
-                both_grad[:, k * units : (k + 1) * units],
-                both_grad[:, (groups + k) * units : (groups + k + 1) * units],
-                down_grad_t[:, k * units : (k + 1) * units],
+                both_grad[k * units : (k + 1) * units],
+                both_grad[inner_units + k * units : inner_units + (k + 1) * units],
+                down_local[k * units : (k + 1) * units],
             ],
-            axis=1,
+            axis=0,
         ).astype(jnp.bfloat16)
         for k in range(groups)
     ]
     mlp_swapped = swap_groups(mlp_grads)
     mlp_sum = sum(piece.astype(jnp.float32) for piece in mlp_swapped)
-    mlp_sum = mlp_sum.astype(jnp.bfloat16).reshape(count, width // count, 3 * units)
+    mlp_sum = jnp.transpose(
+        mlp_sum.astype(jnp.bfloat16).reshape(3 * units, count, width // count), (1, 0, 2)
+    )
 
     d_mix = matmul_back(hidden_b, out_mine).reshape(blocks, block_rows, chans + HD)
     share = width // (count * groups)
@@ -1184,32 +1206,43 @@
             for k in range(groups)
         ]
 
-    mlp_parts = after(mlp_parts, hidden_b)
     places = jnp.array([held_order(count).index(k) for k in range(count)], dtype=jnp.int32)
     by_device = jnp.take(places, ctx ^ jnp.arange(count, dtype=jnp.int32), mode="clip")
-    mlp_parts = jnp.take(mlp_parts, by_device, axis=0, mode="clip")
+    act_by_device = jnp.take(
+        mlp_act.reshape(count, rows, inner_units), by_device, axis=0, mode="clip"
+    ).reshape(total_rows, inner_units)
+    mlp_parts = jnp.dot(act_by_device, down_all, preferred_element_type=jnp.float32)
+    mlp_parts = mlp_parts.astype(jnp.bfloat16).reshape(count, rows, width)
+    mlp_parts = after(mlp_parts, hidden_far)
     mlp_parts = trade_ctx(mlp_parts)
     output = hidden + jnp.sum(mlp_parts.astype(jnp.float32), axis=0)
-    mlp_final = trade_ctx(after(mlp_sum, mlp_parts))
     out_grads = to_groups(matmul_t(hidden_b, mixed_held))
     out_swapped = swap_groups(out_grads)
     out_sum = sum(piece.astype(jnp.float32) for piece in out_swapped)
     d_held, filt_grad, head_grad = mixer_backward(
         sched, projected, filt, table, params, skip, saved, states, kv, d_mix, heads, base
     )
-    out_final = trade_ctx(after(out_sum.astype(jnp.bfloat16), mlp_parts))
+    out_sum = out_sum.astype(jnp.bfloat16)
+    payload = jnp.concatenate(
+        [mlp_sum]
+        + [out_sum[:, :, start : start + 128] for start in range(0, out_sum.shape[2], 128)],
+        axis=1,
+    )
+    payload = trade_ctx(after(payload, (mlp_parts, d_held)))
     gate_up_grad, down_grad, mixer_out_grad, attend_out_grad = finish_rest(
-        mlp_final, out_final, chans
+        payload, chans, units, share
     )
     mixer_out_grad = jnp.transpose(mixer_out_grad)
     attend_out_grad = jnp.transpose(attend_out_grad)
     d_held = d_held.reshape(total_rows, -1)
     d_unit_first = scatter_ctx(
-        jnp.dot(d_held, in_all, preferred_element_type=jnp.float32).reshape(count, rows, width)
+        jnp.dot(d_held, in_all, preferred_element_type=jnp.float32).reshape(
+            count, rows, width
+        )
     )
     input_grad = hidden_grad + norm_back(d_unit_first, 1.0, unit_tokens, first_scale)
 
-    in_grad = matmul_t(units_first, d_held)
+    in_grad = jnp.dot(units_t, d_held, preferred_element_type=jnp.float32)
     gain_first_grad = jnp.sum(in_grad * jnp.transpose(in_all).astype(jnp.float32), axis=1) / gains[0]
     in_grad = in_grad * gains[0][:, None]
     lane = jnp.arange(in_all.shape[0], dtype=jnp.int32)[None, :]
@@ -1220,14 +1253,15 @@
     in_swapped = swap_groups(in_grads)
     in_sum = sum(piece.astype(jnp.float32) for piece in in_swapped)
     mixer_in_grad, attend_in_grad, last_cols = finish_in(
-        trade_ctx(after(in_sum.astype(jnp.bfloat16), (mlp_final, out_final))), heads
+        trade_ctx(after(in_sum.astype(jnp.bfloat16), payload)), heads
     )
     gain_place = gain_lane % 128
     gains_grad = jnp.transpose(last_cols[:, gain_place : gain_place + 2])
     side_by_side = lambda array: jnp.transpose(array, (1, 0, 2)).reshape(array.shape[1], -1)
 
     small = jnp.concatenate([filt_grad.reshape(-1, 128), head_grad], axis=0)
-    small = gather_ctx(jnp.sum(gather_wsh(small[None]), axis=0))
+    small = gather_wsh(small[None])
+    small = gather_ctx(jnp.sum(small, axis=0))
     small = jnp.take(small, by_device, axis=0, mode="clip")
     filters = small[:, :-8].reshape(count, 8, 512)[:, : KERNEL + 1]
     filter_grad = jnp.concatenate(

time: 460 us -> 393 us (0.85)
  waiting for transfers between devices: 168 us -> 116 us
  Pallas kernels: 71.5 us -> 61.4 us
  starting transfers between devices: 80.7 us -> 71.1 us
  other arithmetic: 41.5 us -> 46.8 us
  matrix products: 31.1 us -> 26.1 us
    ppermute x27 -> x21, waiting for transfers between devices: 95.7 us -> 76.4 us  [swap_groups(): lax.ppermute(pieces[k], 'wsh', xor_pairs(count, k))]
    unnamed x143 -> x138, local copies, waits for them, and re-layouts: 9.99 us -> 24.5 us
    ppermute x27 -> x21, starting transfers between devices: 37.6 us -> 28.8 us  [swap_groups(): lax.ppermute(pieces[k], 'wsh', xor_pairs(count, k))]
    ppermute x5, waiting for transfers between devices: 10.8 us -> 2.23 us  [gather_ctx(): near_x = lax.ppermute(values, 'ctx', xor_pairs(count, 2))]
    all_to_all x4 -> x3, waiting for transfers between devices: 12.4 us -> 4.76 us  [trade_ctx(): return lax.all_to_all(parts, 'ctx', 0, 0, tiled=True)]
    dynamic_update_slice x15 -> x11, local copies, waits for them, and re-layouts: 10.9 us -> 3.49 us  [gather_wsh(): whole = lax.dynamic_update_slice_in_dim(whole, piece, start, axis)]
    ppermute x5, waiting for transfers between devices: 14.4 us -> 7.59 us  [gather_ctx(): near_y = lax.ppermute(values, 'ctx', xor_pairs(count, 4))]
    all_to_all x4 -> x3, starting transfers between devices: 17.3 us -> 11.5 us  [trade_ctx(): return lax.all_to_all(parts, 'ctx', 0, 0, tiled=True)]
  transfers between devices with their start and end apart: 63 -> 56, of which waited for: 33 -> 27; matrix products, arithmetic and copies ran while one was open for 24% -> 30% of each run, Pallas kernels for 6% -> 15%
where the time goes in v3:
time: 393 us; the launch traced here: 389 us
  waiting for transfers between devices  116 us (30%)
  starting transfers between devices  71.1 us (18%)
  local copies, waits for them, and re-layouts  66.2 us (17%)
  Pallas kernels  61.4 us (16%)
  other arithmetic  46.8 us (12%)
  matrix products  26.1 us (7%)
    ppermute x21, waiting for transfers between devices, swap_groups(): lax.ppermute(pieces[k], 'wsh', xor_pairs(count, k))  76.4 us
    pallas_call x1, Pallas kernels, mixer_backward(): pl.pallas_call(partial(backward_kernel, heads, base), out_shape=(jax.Shap...  35 us
    ppermute x21, starting transfers between devices, swap_groups(): lax.ppermute(pieces[k], 'wsh', xor_pairs(count, k))  28.8 us
    unnamed x138, local copies, waits for them, and re-layouts  24.5 us
    pallas_call x1, Pallas kernels, mixer_forward(): pl.pallas_call(partial(forward_kernel, heads, base), out_shape=(jax.Shape...  19.2 us
    all_to_all x3, starting transfers between devices, trade_ctx(): return lax.all_to_all(parts, 'ctx', 0, 0, tiled=True)  11.5 us
    dot_general x4, matrix products, matmul_back(): lax.dot_general(left, right, (((1,), (1,)), ((), ())), preferred_element_...  9.86 us
  transfers between devices with their start and end apart: 56, of which 27 were waited for; matrix products, arithmetic and copies ran while one was open for 30% of the time, Pallas kernels for 15%

profile of v3, /device:TPU:8, one launch (start us, length us, event | category | flops | bytes accessed | tf_op | source)
XLA Modules:
  0.0 389.5 jit_solution(7797420414628656533)
XLA Ops:
  6.1 2.9 pick_columns.1
  45.8 7.3 %collective-permute-done.5 = bf16[896,256]{1,0:T(8,128)(2,1)} collective-permute-done((bf16[896,256]{1,0:T(8,128)(2,1)}, bf16[896,256]{1,0:T(8,128)(2,1)}, u32[]{:S(2)}, u32[]{:S(2)}) %collective-permute-start.5) | collective-permute-done | bytes 458784 | tf_op jit(solution)/shard_map/ppermute | solution.py:524
  59.7 4.3 %collective-permute-start.8 = (bf16[256,256]{1,0:T(8,128)(2,1)S(1)}, bf16[256,256]{1,0:T(8,128)(2,1)S(1)}, u32[]{:S(2)}, u32[]{:S(2)}) collective-permute-start(bf16[256,256]{1,0:T(8,128)(2,1)S(1)} %pad_maximum_fusion.14), channel_id=1, source_target_pairs={{0,2},{1,3},{2,0},{3,1},{4,6},{5,7},{6,4},{7,5},{8,10},{9,11},{10,... | collective-permute-start | bytes 393224 | tf_op jit(solution)/shard_map/ppermute | solution.py:524
  65.3 7.3 %collective-permute-done.7 = bf16[256,256]{1,0:T(8,128)(2,1)S(1)} collective-permute-done((bf16[256,256]{1,0:T(8,128)(2,1)S(1)}, bf16[256,256]{1,0:T(8,128)(2,1)S(1)}, u32[]{:S(2)}, u32[]{:S(2)}) %collective-permute-start.7) | collective-permute-done | bytes 131104 | tf_op jit(solution)/shard_map/ppermute | solution.py:524
  72.8 4.2 %fusion.3.proj_ref.before_ref = f32[16,64,896]{2,1,0:T(8,128)} fusion(bf16[16,64,1024]{2,1,0:T(8,128)(2,1)S(1)} %bitcast.278, bf16[896,1024]{0,1:T(8,128)(2,1)S(1)} %copy-done.10), kind=kOutput, calls=%fused_computation.18 | convolution fusion | flops 1879048192 | bytes 7602176 | tf_op jit(solution)/shard_map/dot_general | solution.py:65
  77.6 19.2 %mixer_forward.1 = (bf16[16,64,256]{2,1,0:T(8,128)(2,1)}, f32[16,64,384]{2,1,0:T(8,128)}, f32[16,192,128]{2,1,0:T(8,128)}, bf16[16,64,128]{2,1,0:T(8,128)(2,1)}) custom-call(s32[32]{0:T(128)} %pad_add_fusion.1.sched_ref, f32[16,64,896]{2,1,0:T(8,128)} %fusion.3.proj_ref.before_ref, f32[8,512]{1,0:T(8,128)} %pad.8.filt_ref, ...), custom_call_target="tpu_custom_call" | custom-call | flops 24999999488 | bytes 12000000 | tf_op jit(solution)/shard_map/mixer_forward/pallas_call | solution.py:948
  103.7 3.2 collective-permute-start.19
  113.1 2.5 collective-permute-done.11
  117.3 14.7 %collective-permute-done.18 = bf16[192,1024]{1,0:T(8,128)(2,1)S(1)} collective-permute-done((bf16[192,1024]{1,0:T(8,128)(2,1)S(1)}, bf16[192,1024]{1,0:T(8,128)(2,1)S(1)}, u32[]{:S(2)}, u32[]{:S(2)}) %collective-permute-start.18) | collective-permute-done | bytes 393248 | tf_op jit(solution)/shard_map/ppermute | solution.py:524
  133.5 3.7 collective-permute-done.19
  142.9 3.5 collective-permute-done.15
  148.5 5.8 %collective-permute-done.16 = bf16[128,1024]{1,0:T(8,128)(2,1)S(1)} collective-permute-done((bf16[128,1024]{1,0:T(8,128)(2,1)S(1)}, bf16[128,1024]{1,0:T(8,128)(2,1)S(1)}, u32[]{:S(2)}, u32[]{:S(2)}) %collective-permute-start.16) | collective-permute-done | bytes 262176 | tf_op jit(solution)/shard_map/ppermute | solution.py:482
  154.7 2.4 collective-permute-done.17
  173.3 3.0 collective-permute-done.26
  179.2 5.0 %collective-permute-done.27 = bf16[128,1024]{1,0:T(8,128)(2,1)S(1)} collective-permute-done((bf16[128,1024]{1,0:T(8,128)(2,1)S(1)}, bf16[128,1024]{1,0:T(8,128)(2,1)S(1)}, u32[]{:S(2)}, u32[]{:S(2)}) %collective-permute-start.27) | collective-permute-done | bytes 262176 | tf_op jit(solution)/shard_map/ppermute | solution.py:508
  189.4 4.0 %collective-permute-done.30 = bf16[128,1024]{1,0:T(8,128)(2,1)S(1)} collective-permute-done((bf16[128,1024]{1,0:T(8,128)(2,1)S(1)}, bf16[128,1024]{1,0:T(8,128)(2,1)S(1)}, u32[]{:S(2)}, u32[]{:S(2)}) %collective-permute-start.30) | collective-permute-done | bytes 262176 | tf_op jit(solution)/shard_map/ppermute | solution.py:481
  197.9 2.5 collective-permute-start.41
  206.6 2.4 collective-permute-done.40
  209.0 16.2 %collective-permute-done.41 = bf16[192,1024]{1,0:T(8,128)(2,1)} collective-permute-done((bf16[192,1024]{1,0:T(8,128)(2,1)}, bf16[192,1024]{1,0:T(8,128)(2,1)}, u32[]{:S(2)}, u32[]{:S(2)}) %collective-permute-start.41) | collective-permute-done | bytes 393248 | tf_op jit(solution)/shard_map/ppermute | solution.py:524
  225.3 6.1 %collective-permute-done.42 = bf16[192,1024]{1,0:T(8,128)(2,1)} collective-permute-done((bf16[192,1024]{1,0:T(8,128)(2,1)}, bf16[192,1024]{1,0:T(8,128)(2,1)}, u32[]{:S(2)}, u32[]{:S(2)}) %collective-permute-start.42) | collective-permute-done | bytes 393248 | tf_op jit(solution)/shard_map/ppermute | solution.py:524
  235.0 4.6 %all-to-all-start = ((bf16[8,128,1024]{2,1,0:T(8,128)(2,1)}), bf16[8,128,1024]{2,1,0:T(8,128)(2,1)}, u32[]{:S(2)}, u32[]{:S(2)}) async-start(bf16[8,128,1024]{2,1,0:T(8,128)(2,1)} %bitcast.32), calls=%async_computation | async-start | bytes 4194304 | tf_op jit(solution)/shard_map/all_to_all | solution.py:514
  243.6 3.3 fusion.31.d_mix_ref
  246.9 35.0 %mixer_backward.1 = (bf16[16,64,896]{2,1,0:T(8,128)(2,1)}, f32[8,512]{1,0:T(8,128)}, f32[8,128]{1,0:T(8,128)}) custom-call(s32[32]{0:T(128)} %pad_add_fusion.1.sched_ref, f32[16,64,896]{2,1,0:T(8,128)} %fusion.3.proj_ref.before_ref, f32[16,64,896]{2,1,0:T(8,128)} %fusion.3.proj_ref.before_ref, f32[8,512]{1,0:T(8,128)} %pad.8.filt_ref, ...), custom_call_target="tpu_custom_call" | custom-call | flops 40000000000 | bytes 16000000 | tf_op jit(solution)/shard_map/mixer_backward/pallas_call | solution.py:993
  284.0 2.9 collective-permute-start.46
  287.4 3.9 fusion.69
  295.4 2.5 fusion
  302.4 4.0 %copy.80 = bf16[1024,1024]{0,1:T(8,128)(2,1)} copy(bf16[1024,1024]{1,0:T(8,128)(2,1)} %bitcast.70) | data formatting | bytes 4194304 | tf_op jit(solution)/shard_map/reshape | solution.py:1176
  327.4 13.9 %collective-permute-done.44 = bf16[8,32,256]{2,1,0:T(8,128)(2,1)S(1)} collective-permute-done((bf16[8,32,256]{2,1,0:T(8,128)(2,1)}, bf16[8,32,256]{2,1,0:T(8,128)(2,1)S(1)}, u32[]{:S(2)}, u32[]{:S(2)}) %collective-permute-start.44) | collective-permute-done | bytes 131104 | tf_op jit(solution)/shard_map/ppermute | solution.py:524
  341.2 2.8 collective-permute-done.45
  359.2 3.5 all-to-all-start.1
  372.9 3.5 all-to-all-start.2
  382.2 3.1 all-to-all-done.2.final_ref
  (378 shorter events, 184.4 us)
Async XLA Ops:
  2.5 30.7 %collective-permute-start.22 = (bf16[128,1024]{1,0:T(8,128)(2,1)}, bf16[128,1024]{1,0:T(8,128)(2,1)}, u32[]{:S(2)}, u32[]{:S(2)}) collective-permute-start(bf16[128,1024]{1,0:T(8,128)(2,1)} %bitcast_convert_fusion.4), channel_id=1, source_target_pairs={{0,16},{4,20},{8,24},{12,28},{16,0},{20,4},{24,8},{28,12},{1,17},{... | collective-permute-start | bytes 786440 | tf_op jit(solution)/shard_map/ppermute | solution.py:481
  4.0 30.2 %collective-permute-start.21 = (bf16[128,1024]{1,0:T(8,128)(2,1)}, bf16[128,1024]{1,0:T(8,128)(2,1)}, u32[]{:S(2)}, u32[]{:S(2)}) collective-permute-start(bf16[128,1024]{1,0:T(8,128)(2,1)} %bitcast_convert_fusion.4), channel_id=1, source_target_pairs={{0,8},{4,12},{8,0},{12,4},{16,24},{20,28},{24,16},{28,20},{1,9},{5... | collective-permute-start | bytes 786440 | tf_op jit(solution)/shard_map/ppermute | solution.py:480
  9.0 35.5 %collective-permute-start.6 = (bf16[896,256]{1,0:T(8,128)(2,1)}, bf16[896,256]{1,0:T(8,128)(2,1)}, u32[]{:S(2)}, u32[]{:S(2)}) collective-permute-start(bf16[896,256]{1,0:T(8,128)(2,1)} %pick_columns.1), channel_id=1, source_target_pairs={{0,3},{1,2},{2,1},{3,0},{4,7},{5,6},{6,5},{7,4},{8,11},{9,10},{10,... | collective-permute-start | bytes 1376264 | tf_op jit(solution)/shard_map/ppermute | solution.py:524
  12.3 25.2 %collective-permute-start.1 = (bf16[128,1024]{1,0:T(8,128)(2,1)}, bf16[128,1024]{1,0:T(8,128)(2,1)}, u32[]{:S(2)}, u32[]{:S(2)}) collective-permute-start(bf16[128,1024]{1,0:T(8,128)(2,1)} %get-tuple-element.107), channel_id=1, source_target_pairs={{0,16},{4,20},{8,24},{12,28},{16,0},{20,4},{24,8},{28,12},{1,17},{... | collective-permute-start | bytes 786440 | tf_op jit(solution)/shard_map/ppermute | solution.py:481
  12.8 26.2 %collective-permute-start = (bf16[128,1024]{1,0:T(8,128)(2,1)}, bf16[128,1024]{1,0:T(8,128)(2,1)}, u32[]{:S(2)}, u32[]{:S(2)}) collective-permute-start(bf16[128,1024]{1,0:T(8,128)(2,1)} %get-tuple-element.107), channel_id=1, source_target_pairs={{0,8},{4,12},{8,0},{12,4},{16,24},{20,28},{24,16},{28,20},{1,9},{5... | collective-permute-start | bytes 786440 | tf_op jit(solution)/shard_map/ppermute | solution.py:480
  33.2 19.9 %collective-permute-start.5 = (bf16[896,256]{1,0:T(8,128)(2,1)}, bf16[896,256]{1,0:T(8,128)(2,1)}, u32[]{:S(2)}, u32[]{:S(2)}) collective-permute-start(bf16[896,256]{1,0:T(8,128)(2,1)} %pick_columns.1), channel_id=1, source_target_pairs={{0,2},{1,3},{2,0},{3,1},{4,6},{5,7},{6,4},{7,5},{8,10},{9,11},{10,... | collective-permute-start | bytes 1376264 | tf_op jit(solution)/shard_map/ppermute | solution.py:524
  34.3 20.7 %collective-permute-start.4 = (bf16[896,256]{1,0:T(8,128)(2,1)}, bf16[896,256]{1,0:T(8,128)(2,1)}, u32[]{:S(2)}, u32[]{:S(2)}) collective-permute-start(bf16[896,256]{1,0:T(8,128)(2,1)} %pick_columns.1), channel_id=1, source_target_pairs={{0,1},{1,0},{2,3},{3,2},{4,5},{5,4},{6,7},{7,6},{8,9},{9,8},{10,11... | collective-permute-start | bytes 1376264 | tf_op jit(solution)/shard_map/ppermute | solution.py:524
  37.5 73.2 %collective-permute-start.23 = (bf16[128,1024]{1,0:T(8,128)(2,1)}, bf16[128,1024]{1,0:T(8,128)(2,1)}, u32[]{:S(2)}, u32[]{:S(2)}) collective-permute-start(bf16[128,1024]{1,0:T(8,128)(2,1)} %broadcast_select_fusion.1), channel_id=1, source_target_pairs={{0,16},{4,12},{8,24},{12,4},{16,0},{20,28},{24,8},{28,20},{1,17},{... | collective-permute-start | bytes 786440 | tf_op jit(solution)/shard_map/ppermute | solution.py:482
  40.7 16.3 %collective-permute-start.2 = (bf16[128,1024]{1,0:T(8,128)(2,1)}, bf16[128,1024]{1,0:T(8,128)(2,1)}, u32[]{:S(2)}, u32[]{:S(2)}) collective-permute-start(bf16[128,1024]{1,0:T(8,128)(2,1)} %broadcast_select_fusion.3), channel_id=1, source_target_pairs={{0,16},{4,12},{8,24},{12,4},{16,0},{20,28},{24,8},{28,20},{1,17},{... | collective-permute-start | bytes 786440 | tf_op jit(solution)/shard_map/ppermute | solution.py:482
  58.4 14.3 %collective-permute-start.3 = (bf16[4,128,1024]{2,1,0:T(8,128)(2,1)S(1)}, bf16[4,128,1024]{2,1,0:T(8,128)(2,1)S(1)}, u32[]{:S(2)}, u32[]{:S(2)}) collective-permute-start(bf16[4,128,1024]{2,1,0:T(8,128)(2,1)S(1)} %pad_maximum_fusion), channel_id=1, source_target_pairs={{0,4},{4,0},{8,12},{12,8},{16,20},{20,16},{24,28},{28,24},{1,5},{5... | collective-permute-start | bytes 3145736 | tf_op jit(solution)/shard_map/ppermute | solution.py:488
  58.7 14.0 %collective-permute-start.9 = (bf16[256,256]{1,0:T(8,128)(2,1)S(1)}, bf16[256,256]{1,0:T(8,128)(2,1)S(1)}, u32[]{:S(2)}, u32[]{:S(2)}) collective-permute-start(bf16[256,256]{1,0:T(8,128)(2,1)S(1)} %pad_maximum_fusion.14), channel_id=1, source_target_pairs={{0,3},{1,2},{2,1},{3,0},{4,7},{5,6},{6,5},{7,4},{8,11},{9,10},{10,... | collective-permute-start | bytes 393224 | tf_op jit(solution)/shard_map/ppermute | solution.py:524
  59.7 12.9 %collective-permute-start.8 = (bf16[256,256]{1,0:T(8,128)(2,1)S(1)}, bf16[256,256]{1,0:T(8,128)(2,1)S(1)}, u32[]{:S(2)}, u32[]{:S(2)}) collective-permute-start(bf16[256,256]{1,0:T(8,128)(2,1)S(1)} %pad_maximum_fusion.14), channel_id=1, source_target_pairs={{0,2},{1,3},{2,0},{3,1},{4,6},{5,7},{6,4},{7,5},{8,10},{9,11},{10,... | collective-permute-start | bytes 393224 | tf_op jit(solution)/shard_map/ppermute | solution.py:524
  102.1 40.8 %collective-permute-start.20 = (bf16[192,1024]{1,0:T(8,128)(2,1)S(1)}, bf16[192,1024]{1,0:T(8,128)(2,1)S(1)}, u32[]{:S(2)}, u32[]{:S(2)}) collective-permute-start(bf16[192,1024]{1,0:T(8,128)(2,1)S(1)} %copy-done.18), channel_id=1, source_target_pairs={{0,3},{1,2},{2,1},{3,0},{4,7},{5,6},{6,5},{7,4},{8,11},{9,10},{10,... | collective-permute-start | bytes 1179656 | tf_op jit(solution)/shard_map/ppermute | solution.py:524
  103.7 33.4 %collective-permute-start.19 = (bf16[192,1024]{1,0:T(8,128)(2,1)S(1)}, bf16[192,1024]{1,0:T(8,128)(2,1)S(1)}, u32[]{:S(2)}, u32[]{:S(2)}) collective-permute-start(bf16[192,1024]{1,0:T(8,128)(2,1)S(1)} %copy-done.18), channel_id=1, source_target_pairs={{0,2},{1,3},{2,0},{3,1},{4,6},{5,7},{6,4},{7,5},{8,10},{9,11},{10,... | collective-permute-start | bytes 1179656 | tf_op jit(solution)/shard_map/ppermute | solution.py:524
  106.9 25.1 %collective-permute-start.18 = (bf16[192,1024]{1,0:T(8,128)(2,1)S(1)}, bf16[192,1024]{1,0:T(8,128)(2,1)S(1)}, u32[]{:S(2)}, u32[]{:S(2)}) collective-permute-start(bf16[192,1024]{1,0:T(8,128)(2,1)S(1)} %copy-done.18), channel_id=1, source_target_pairs={{0,1},{1,0},{2,3},{3,2},{4,5},{5,4},{6,7},{7,6},{8,9},{9,8},{10,11... | collective-permute-start | bytes 1179656 | tf_op jit(solution)/shard_map/ppermute | solution.py:524
  112.0 42.5 %collective-permute-start.24 = (bf16[4,128,1024]{2,1,0:T(8,128)(2,1)S(1)}, bf16[4,128,1024]{2,1,0:T(8,128)(2,1)S(1)}, u32[]{:S(2)}, u32[]{:S(2)}) collective-permute-start(bf16[4,128,1024]{2,1,0:T(8,128)(2,1)S(1)} %pad_maximum_fusion.2), channel_id=1, source_target_pairs={{0,4},{4,0},{8,12},{12,8},{16,20},{20,16},{24,28},{28,24},{1,5},{5... | collective-permute-start | bytes 3145736 | tf_op jit(solution)/shard_map/ppermute | solution.py:488
  115.7 21.5 %collective-permute-start.12 = (bf16[128,1024]{1,0:T(8,128)(2,1)S(1)}, bf16[128,1024]{1,0:T(8,128)(2,1)S(1)}, u32[]{:S(2)}, u32[]{:S(2)}) collective-permute-start(bf16[128,1024]{1,0:T(8,128)(2,1)S(1)} %get-tuple-element.114), channel_id=1, source_target_pairs={{0,8},{4,12},{8,0},{12,4},{16,24},{20,28},{24,16},{28,20},{1,9},{5... | collective-permute-start | bytes 786440 | tf_op jit(solution)/shard_map/ppermute | solution.py:508
  197.9 27.4 %collective-permute-start.41 = (bf16[192,1024]{1,0:T(8,128)(2,1)}, bf16[192,1024]{1,0:T(8,128)(2,1)}, u32[]{:S(2)}, u32[]{:S(2)}) collective-permute-start(bf16[192,1024]{1,0:T(8,128)(2,1)} %pad_maximum_fusion.12), channel_id=1, source_target_pairs={{0,2},{1,3},{2,0},{3,1},{4,6},{5,7},{6,4},{7,5},{8,10},{9,11},{10,... | collective-permute-start | bytes 1179656 | tf_op jit(solution)/shard_map/ppermute | solution.py:524
  201.2 30.2 %collective-permute-start.42 = (bf16[192,1024]{1,0:T(8,128)(2,1)}, bf16[192,1024]{1,0:T(8,128)(2,1)}, u32[]{:S(2)}, u32[]{:S(2)}) collective-permute-start(bf16[192,1024]{1,0:T(8,128)(2,1)} %pad_maximum_fusion.13), channel_id=1, source_target_pairs={{0,3},{1,2},{2,1},{3,0},{4,7},{5,6},{6,5},{7,4},{8,11},{9,10},{10,... | collective-permute-start | bytes 1179656 | tf_op jit(solution)/shard_map/ppermute | solution.py:524
  204.5 36.8 %collective-permute-start.32 = (bf16[4,128,1024]{2,1,0:T(8,128)(2,1)}, bf16[4,128,1024]{2,1,0:T(8,128)(2,1)}, u32[]{:S(2)}, u32[]{:S(2)}) collective-permute-start(bf16[4,128,1024]{2,1,0:T(8,128)(2,1)} %pad_maximum_fusion.4), channel_id=1, source_target_pairs={{0,4},{4,0},{8,12},{12,8},{16,20},{20,16},{24,28},{28,24},{1,5},{5... | collective-permute-start | bytes 3145736 | tf_op jit(solution)/shard_map/ppermute | solution.py:488
  235.0 124.1 %all-to-all-start = ((bf16[8,128,1024]{2,1,0:T(8,128)(2,1)}), bf16[8,128,1024]{2,1,0:T(8,128)(2,1)}, u32[]{:S(2)}, u32[]{:S(2)}) async-start(bf16[8,128,1024]{2,1,0:T(8,128)(2,1)} %bitcast.32), calls=%async_computation | async-start | bytes 4194304 | tf_op jit(solution)/shard_map/all_to_all | solution.py:514
  284.0 28.1 %collective-permute-start.47 = (f32[1,40,128]{2,1,0:T(8,128)}, f32[1,40,128]{2,1,0:T(8,128)}, u32[]{:S(2)}, u32[]{:S(2)}) collective-permute-start(f32[1,40,128]{2,1,0:T(8,128)} %maximum_bitcast_fusion), channel_id=1, source_target_pairs={{0,2},{1,3},{2,0},{3,1},{4,6},{5,7},{6,4},{7,5},{8,10},{9,11},{10,... | collective-permute-start | bytes 61448 | tf_op jit(solution)/shard_map/ppermute | solution.py:524
  284.0 26.4 %collective-permute-start.46 = (f32[1,40,128]{2,1,0:T(8,128)}, f32[1,40,128]{2,1,0:T(8,128)}, u32[]{:S(2)}, u32[]{:S(2)}) collective-permute-start(f32[1,40,128]{2,1,0:T(8,128)} %maximum_bitcast_fusion), channel_id=1, source_target_pairs={{0,1},{1,0},{2,3},{3,2},{4,5},{5,4},{6,7},{7,6},{8,9},{9,8},{10,11... | collective-permute-start | bytes 61448 | tf_op jit(solution)/shard_map/ppermute | solution.py:524
  286.9 25.9 %collective-permute-start.48 = (f32[1,40,128]{2,1,0:T(8,128)}, f32[1,40,128]{2,1,0:T(8,128)}, u32[]{:S(2)}, u32[]{:S(2)}) collective-permute-start(f32[1,40,128]{2,1,0:T(8,128)} %maximum_bitcast_fusion), channel_id=1, source_target_pairs={{0,3},{1,2},{2,1},{3,0},{4,7},{5,6},{6,5},{7,4},{8,11},{9,10},{10,... | collective-permute-start | bytes 61448 | tf_op jit(solution)/shard_map/ppermute | solution.py:524
  299.5 57.3 %collective-permute-start.37 = (bf16[8,32,896]{2,1,0:T(8,128)(2,1)}, bf16[8,32,896]{2,1,0:T(8,128)(2,1)}, u32[]{:S(2)}, u32[]{:S(2)}) collective-permute-start(bf16[8,32,896]{2,1,0:T(8,128)(2,1)} %get-tuple-element.121), channel_id=1, source_target_pairs={{0,1},{1,0},{2,3},{3,2},{4,5},{5,4},{6,7},{7,6},{8,9},{9,8},{10,11... | collective-permute-start | bytes 1376264 | tf_op jit(solution)/shard_map/ppermute | solution.py:524
  300.4 56.4 %collective-permute-start.38 = (bf16[8,32,896]{2,1,0:T(8,128)(2,1)}, bf16[8,32,896]{2,1,0:T(8,128)(2,1)}, u32[]{:S(2)}, u32[]{:S(2)}) collective-permute-start(bf16[8,32,896]{2,1,0:T(8,128)(2,1)} %get-tuple-element.122), channel_id=1, source_target_pairs={{0,2},{1,3},{2,0},{3,1},{4,6},{5,7},{6,4},{7,5},{8,10},{9,11},{10,... | collective-permute-start | bytes 1376264 | tf_op jit(solution)/shard_map/ppermute | solution.py:524
  310.3 15.6 %collective-permute-start.43 = (bf16[8,32,256]{2,1,0:T(8,128)(2,1)}, bf16[8,32,256]{2,1,0:T(8,128)(2,1)}, u32[]{:S(2)}, u32[]{:S(2)}) collective-permute-start(bf16[8,32,256]{2,1,0:T(8,128)(2,1)} %get-tuple-element.136), channel_id=1, source_target_pairs={{0,1},{1,0},{2,3},{3,2},{4,5},{5,4},{6,7},{7,6},{8,9},{9,8},{10,11... | collective-permute-start | bytes 393224 | tf_op jit(solution)/shard_map/ppermute | solution.py:524
  317.6 23.7 %collective-permute-start.44 = (bf16[8,32,256]{2,1,0:T(8,128)(2,1)}, bf16[8,32,256]{2,1,0:T(8,128)(2,1)S(1)}, u32[]{:S(2)}, u32[]{:S(2)}) collective-permute-start(bf16[8,32,256]{2,1,0:T(8,128)(2,1)} %get-tuple-element.137), channel_id=1, source_target_pairs={{0,2},{1,3},{2,0},{3,1},{4,6},{5,7},{6,4},{7,5},{8,10},{9,11},{10,... | collective-permute-start | bytes 393224 | tf_op jit(solution)/shard_map/ppermute | solution.py:524
  323.1 21.0 %collective-permute-start.45 = (bf16[8,32,256]{2,1,0:T(8,128)(2,1)S(1)}, bf16[8,32,256]{2,1,0:T(8,128)(2,1)S(1)}, u32[]{:S(2)}, u32[]{:S(2)}) collective-permute-start(bf16[8,32,256]{2,1,0:T(8,128)(2,1)S(1)} %get-tuple-element.138), channel_id=1, source_target_pairs={{0,3},{1,2},{2,1},{3,0},{4,7},{5,6},{6,5},{7,4},{8,11},{9,10},{10,... | collective-permute-start | bytes 393224 | tf_op jit(solution)/shard_map/ppermute | solution.py:524
  325.9 30.9 %collective-permute-start.39 = (bf16[8,32,896]{2,1,0:T(8,128)(2,1)}, bf16[8,32,896]{2,1,0:T(8,128)(2,1)}, u32[]{:S(2)}, u32[]{:S(2)}) collective-permute-start(bf16[8,32,896]{2,1,0:T(8,128)(2,1)} %get-tuple-element.123), channel_id=1, source_target_pairs={{0,3},{1,2},{2,1},{3,0},{4,7},{5,6},{6,5},{7,4},{8,11},{9,10},{10,... | collective-permute-start | bytes 1376264 | tf_op jit(solution)/shard_map/ppermute | solution.py:524
  359.2 13.7 %all-to-all-start.1 = ((bf16[8,256,128]{2,1,0:T(8,128)(2,1)}), bf16[8,256,128]{2,1,0:T(8,128)(2,1)S(1)}, u32[]{:S(2)}, u32[]{:S(2)}) async-start(bf16[8,256,128]{2,1,0:T(8,128)(2,1)} %pad_maximum_fusion.9), calls=%async_computation.1 | async-start | bytes 1048576 | tf_op jit(solution)/shard_map/all_to_all | solution.py:514
  372.9 12.4 %all-to-all-start.2 = ((bf16[8,32,896]{2,1,0:T(8,128)(2,1)}), bf16[8,32,896]{2,1,0:T(8,128)(2,1)S(1)}, u32[]{:S(2)}, u32[]{:S(2)}) async-start(bf16[8,32,896]{2,1,0:T(8,128)(2,1)} %fusion.8), calls=%async_computation.2 | async-start | bytes 917504 | tf_op jit(solution)/shard_map/all_to_all | solution.py:514
  (84 other events, 614.1 us)

commit v4 on v3

--- a/solution.py
+++ b/solution.py
@@ -586,15 +586,14 @@
 
 def pick_kernel(heads, where_ref, *refs):
     xs, zs = refs[:heads], refs[heads : 2 * heads]
-    bc0, step0, q0, k0, v0, gain_ref, out_ref = refs[2 * heads :]
+    bc0, step0, q0, k0, v0, gain_ref, out_ref, all_ref = refs[2 * heads :]
     chans = heads * HEAD_M
     ctx = where_ref[0]
     gain = gain_ref[0:1, :].astype(jnp.float32)
     width = gain.shape[1]
 
     def put(start, values):
-        scaled = values.astype(jnp.float32) * gain
-        out_ref[start : start + values.shape[0], :] = scaled.astype(jnp.bfloat16)
+        all_ref[start : start + values.shape[0], :] = values.astype(jnp.float32) * gain
 
     def half_tile(ref, odd):
         window = jnp.transpose(ref[...].astype(jnp.float32))
@@ -616,7 +615,8 @@
     turn_row = lax.broadcasted_iota(jnp.int32, (16, width), 0)
     second = gain_ref[1:2, :].astype(jnp.float32)
     both = jnp.where(turn_row == 0, gain, jnp.where(turn_row == 1, second, 0.0))
-    out_ref[GAIN_ROW : GAIN_ROW + 16, :] = both.astype(jnp.bfloat16)
+    all_ref[GAIN_ROW : GAIN_ROW + 16, :] = both
+    out_ref[...] = jnp.transpose(all_ref[...]).astype(jnp.bfloat16)
 
 
 def pick_columns(where, mixer_in, attend_in, gains, heads):
@@ -628,7 +628,7 @@
     from_z = [rows_at(lambda s, h=h: (s[0] * heads + h) * HEAD_M) for h in range(heads)]
     return pl.pallas_call(
         partial(pick_kernel, heads),
-        out_shape=jax.ShapeDtypeStruct((896, width), jnp.bfloat16),
+        out_shape=jax.ShapeDtypeStruct((width, 896), jnp.bfloat16),
         grid_spec=pltpu.PrefetchScalarGridSpec(
             num_scalar_prefetch=1,
             grid=(1,),
@@ -642,7 +642,8 @@
                 tile_at(lambda s: AQ + KVH * HD + s[1] * HD),
                 pl.BlockSpec(gains.shape, lambda i, s: (0, 0)),
             ],
-            out_specs=pl.BlockSpec((896, width), lambda i, s: (0, 0)),
+            out_specs=pl.BlockSpec((width, 896), lambda i, s: (0, 0)),
+            scratch_shapes=[pltpu.VMEM((896, width), jnp.float32)],
         ),
         name="pick_columns",
     )(where, *[turned] * (2 * heads + 2), *[attend_in] * 3, gains)
@@ -1071,8 +1072,8 @@
     in_cols = pick_columns(
         jnp.stack([ctx, kv_head]), mixer_in, attend_in, norm_gains, heads
     )
-    in_all = gather_wsh(in_cols, 1)
-    gains = in_all[GAIN_ROW : GAIN_ROW + 2].astype(jnp.float32)
+    in_all = gather_wsh(in_cols)
+    gains = jnp.transpose(in_all[:, GAIN_ROW : GAIN_ROW + 2].astype(jnp.float32))
     out_rows = jnp.concatenate(
         [
             lax.dynamic_slice_in_dim(mixer_out, ctx * chans, chans, 0),
@@ -1135,7 +1136,8 @@
     units_t = lax.optimization_barrier(jnp.transpose(units_first))
     cot_all = gather_ctx(after(cotangent.astype(jnp.bfloat16), units_first))
     cot_all = cot_all.reshape(total_rows, width)
-    projected = matmul_back(units_first, in_all).reshape(blocks, block_rows, in_all.shape[0])
+    projected = jnp.dot(units_first, in_all, preferred_element_type=jnp.float32)
+    projected = projected.reshape(blocks, block_rows, in_all.shape[1])
     mixed_held, saved, states, kv = mixer_forward(
         sched, projected, filt, table, params, skip, heads, base
     )
@@ -1236,17 +1238,15 @@
     attend_out_grad = jnp.transpose(attend_out_grad)
     d_held = d_held.reshape(total_rows, -1)
     d_unit_first = scatter_ctx(
-        jnp.dot(d_held, in_all, preferred_element_type=jnp.float32).reshape(
-            count, rows, width
-        )
+        matmul_back(d_held, in_all).reshape(count, rows, width)
     )
     input_grad = hidden_grad + norm_back(d_unit_first, 1.0, unit_tokens, first_scale)
 
     in_grad = jnp.dot(units_t, d_held, preferred_element_type=jnp.float32)
-    gain_first_grad = jnp.sum(in_grad * jnp.transpose(in_all).astype(jnp.float32), axis=1) / gains[0]
+    gain_first_grad = jnp.sum(in_grad * in_all.astype(jnp.float32), axis=1) / gains[0]
     in_grad = in_grad * gains[0][:, None]
-    lane = jnp.arange(in_all.shape[0], dtype=jnp.int32)[None, :]
-    gain_lane = in_all.shape[0] - step_pad
+    lane = jnp.arange(in_all.shape[1], dtype=jnp.int32)[None, :]
+    gain_lane = in_all.shape[1] - step_pad
     in_grad = jnp.where(lane == gain_lane, gain_first_grad[:, None], in_grad)
     in_grad = jnp.where(lane == gain_lane + 1, gain_second_grad[:, None], in_grad)
     in_grads = to_groups(in_grad)

time: 393 us -> 387 us (0.985)
  local copies, waits for them, and re-layouts: 66.2 us -> 60.8 us
    ppermute x3 -> x0, local copies, waits for them, and re-layouts: 4.51 us -> none  [swap_groups(): lax.ppermute(pieces[k], 'wsh', xor_pairs(count, k))]
    unnamed x138 -> x140, local copies, waits for them, and re-layouts: 24.5 us -> 23.4 us
  transfers between devices with their start and end apart: 56 -> 56, of which waited for: 27 -> 29; matrix products, arithmetic and copies ran while one was open for 30% -> 29% of each run, Pallas kernels for 15% -> 15%
where the time goes in v4:
time: 387 us; the launch traced here: 384 us
  waiting for transfers between devices  117 us (30%)
  starting transfers between devices  71.3 us (18%)
  Pallas kernels  61.5 us (16%)
  local copies, waits for them, and re-layouts  60.8 us (16%)
  other arithmetic  46 us (12%)
  matrix products  26.2 us (7%)
    ppermute x21, waiting for transfers between devices, swap_groups(): lax.ppermute(pieces[k], 'wsh', xor_pairs(count, k))  74.5 us
    pallas_call x1, Pallas kernels, mixer_backward(): pl.pallas_call(partial(backward_kernel, heads, base), out_shape=(jax.Shap...  35 us
    ppermute x21, starting transfers between devices, swap_groups(): lax.ppermute(pieces[k], 'wsh', xor_pairs(count, k))  28.4 us
    unnamed x140, local copies, waits for them, and re-layouts  23.4 us
    pallas_call x1, Pallas kernels, mixer_forward(): pl.pallas_call(partial(forward_kernel, heads, base), out_shape=(jax.Shape...  19.2 us
    all_to_all x3, starting transfers between devices, trade_ctx(): return lax.all_to_all(parts, 'ctx', 0, 0, tiled=True)  11.6 us
    ppermute x5, waiting for transfers between devices, gather_ctx(): lax.ppermute(jnp.where(first_core, near_x, near_y), 'ctx', [(index, index...  9.95 us
    dot_general x4, matrix products, matmul_back(): lax.dot_general(left, right, (((1,), (1,)), ((), ())), preferred_element_...  9.53 us
  transfers between devices with their start and end apart: 56, of which 29 were waited for; matrix products, arithmetic and copies ran while one was open for 29% of the time, Pallas kernels for 15%

profile of v4, /device:TPU:8, one launch (start us, length us, event | category | flops | bytes accessed | tf_op | source)
XLA Modules:
  0.0 384.2 jit_solution(11053159026948579358)
XLA Ops:
  6.1 3.0 pick_columns.1
  43.1 3.0 collective-permute-done.2
  47.4 6.7 %collective-permute-done.4 = bf16[256,896]{1,0:T(8,128)(2,1)S(1)} collective-permute-done((bf16[256,896]{1,0:T(8,128)(2,1)}, bf16[256,896]{1,0:T(8,128)(2,1)S(1)}, u32[]{:S(2)}, u32[]{:S(2)}) %collective-permute-start.4) | collective-permute-done | bytes 458784 | tf_op jit(solution)/shard_map/ppermute | solution.py:524
  56.2 3.4 collective-permute-start.8
  59.7 6.8 %collective-permute-done.7 = bf16[256,256]{1,0:T(8,128)(2,1)S(1)} collective-permute-done((bf16[256,256]{1,0:T(8,128)(2,1)S(1)}, bf16[256,256]{1,0:T(8,128)(2,1)S(1)}, u32[]{:S(2)}, u32[]{:S(2)}) %collective-permute-start.7) | collective-permute-done | bytes 131104 | tf_op jit(solution)/shard_map/ppermute | solution.py:524
  67.4 4.2 %fusion.2.proj_ref.before_ref = f32[16,64,896]{2,1,0:T(8,128)} fusion(bf16[16,64,1024]{2,1,0:T(8,128)(2,1)S(1)} %bitcast.277, bf16[1024,896]{1,0:T(8,128)(2,1)S(1)} %copy-done.10), kind=kOutput, calls=%fused_computation.17 | convolution fusion | flops 1879048192 | bytes 7602176 | tf_op jit(solution)/shard_map/dot_general | solution.py:1139
  72.2 19.2 %mixer_forward.1 = (bf16[16,64,256]{2,1,0:T(8,128)(2,1)}, f32[16,64,384]{2,1,0:T(8,128)}, f32[16,192,128]{2,1,0:T(8,128)}, bf16[16,64,128]{2,1,0:T(8,128)(2,1)}) custom-call(s32[32]{0:T(128)} %pad_add_fusion.1.sched_ref, f32[16,64,896]{2,1,0:T(8,128)} %fusion.2.proj_ref.before_ref, f32[8,512]{1,0:T(8,128)} %pad.8.filt_ref, ...), custom_call_target="tpu_custom_call" | custom-call | flops 24999999488 | bytes 12000000 | tf_op jit(solution)/shard_map/mixer_forward/pallas_call | solution.py:949
  98.5 3.6 collective-permute-start.19
  108.3 2.5 collective-permute-done.11
  112.5 13.8 %collective-permute-done.18 = bf16[192,1024]{1,0:T(8,128)(2,1)S(1)} collective-permute-done((bf16[192,1024]{1,0:T(8,128)(2,1)S(1)}, bf16[192,1024]{1,0:T(8,128)(2,1)S(1)}, u32[]{:S(2)}, u32[]{:S(2)}) %collective-permute-start.18) | collective-permute-done | bytes 393248 | tf_op jit(solution)/shard_map/ppermute | solution.py:524
  127.8 3.7 collective-permute-done.19
  136.4 3.3 collective-permute-done.15
  139.7 2.5 collective-permute-done.14
  143.1 5.5 %collective-permute-done.16 = bf16[128,1024]{1,0:T(8,128)(2,1)S(1)} collective-permute-done((bf16[128,1024]{1,0:T(8,128)(2,1)S(1)}, bf16[128,1024]{1,0:T(8,128)(2,1)S(1)}, u32[]{:S(2)}, u32[]{:S(2)}) %collective-permute-start.16) | collective-permute-done | bytes 262176 | tf_op jit(solution)/shard_map/ppermute | solution.py:482
  167.6 3.0 collective-permute-done.26
  173.8 4.7 %collective-permute-done.27 = bf16[128,1024]{1,0:T(8,128)(2,1)S(1)} collective-permute-done((bf16[128,1024]{1,0:T(8,128)(2,1)S(1)}, bf16[128,1024]{1,0:T(8,128)(2,1)S(1)}, u32[]{:S(2)}, u32[]{:S(2)}) %collective-permute-start.27) | collective-permute-done | bytes 262176 | tf_op jit(solution)/shard_map/ppermute | solution.py:508
  184.0 3.7 collective-permute-done.30
  191.8 3.0 collective-permute-start.41
  203.3 16.6 %collective-permute-done.41 = bf16[192,1024]{1,0:T(8,128)(2,1)} collective-permute-done((bf16[192,1024]{1,0:T(8,128)(2,1)}, bf16[192,1024]{1,0:T(8,128)(2,1)}, u32[]{:S(2)}, u32[]{:S(2)}) %collective-permute-start.41) | collective-permute-done | bytes 393248 | tf_op jit(solution)/shard_map/ppermute | solution.py:524
  219.9 6.1 %collective-permute-done.42 = bf16[192,1024]{1,0:T(8,128)(2,1)} collective-permute-done((bf16[192,1024]{1,0:T(8,128)(2,1)}, bf16[192,1024]{1,0:T(8,128)(2,1)}, u32[]{:S(2)}, u32[]{:S(2)}) %collective-permute-start.42) | collective-permute-done | bytes 393248 | tf_op jit(solution)/shard_map/ppermute | solution.py:524
  229.6 4.6 %all-to-all-start = ((bf16[8,128,1024]{2,1,0:T(8,128)(2,1)}), bf16[8,128,1024]{2,1,0:T(8,128)(2,1)}, u32[]{:S(2)}, u32[]{:S(2)}) async-start(bf16[8,128,1024]{2,1,0:T(8,128)(2,1)} %bitcast.33), calls=%async_computation | async-start | bytes 4194304 | tf_op jit(solution)/shard_map/all_to_all | solution.py:514
  238.2 3.3 fusion.30.d_mix_ref
  241.5 35.0 %mixer_backward.1 = (bf16[16,64,896]{2,1,0:T(8,128)(2,1)}, f32[8,512]{1,0:T(8,128)}, f32[8,128]{1,0:T(8,128)}) custom-call(s32[32]{0:T(128)} %pad_add_fusion.1.sched_ref, f32[16,64,896]{2,1,0:T(8,128)} %fusion.2.proj_ref.before_ref, f32[16,64,896]{2,1,0:T(8,128)} %fusion.2.proj_ref.before_ref, f32[8,512]{1,0:T(8,128)} %pad.8.filt_ref, ...), custom_call_target="tpu_custom_call" | custom-call | flops 40000000000 | bytes 16000000 | tf_op jit(solution)/shard_map/mixer_backward/pallas_call | solution.py:994
  278.6 3.0 collective-permute-start.46
  282.1 3.9 %fusion.68 = f32[1024,1024]{1,0:T(8,128)S(1)} fusion(bf16[1024,896]{1,0:T(8,128)(2,1)} %bitcast.285, bf16[1024,896]{1,0:T(8,128)(2,1)S(1)} %copy-done.11), kind=kOutput, calls=%fused_computation.236 | convolution fusion | flops 1879048192 | bytes 7864320 | tf_op jit(solution)/shard_map/dot_general | solution.py:65
  290.0 2.5 multiply_reduce_fusion
  297.2 4.0 %copy.65 = bf16[1024,1024]{0,1:T(8,128)(2,1)} copy(bf16[1024,1024]{1,0:T(8,128)(2,1)} %bitcast.70) | data formatting | bytes 4194304 | tf_op jit(solution)/shard_map/reshape | solution.py:1178
  322.1 13.9 %collective-permute-done.44 = bf16[8,32,256]{2,1,0:T(8,128)(2,1)S(1)} collective-permute-done((bf16[8,32,256]{2,1,0:T(8,128)(2,1)}, bf16[8,32,256]{2,1,0:T(8,128)(2,1)S(1)}, u32[]{:S(2)}, u32[]{:S(2)}) %collective-permute-start.44) | collective-permute-done | bytes 131104 | tf_op jit(solution)/shard_map/ppermute | solution.py:524
  336.1 2.7 collective-permute-done.45
  353.9 3.5 all-to-all-start.1
  367.6 3.5 all-to-all-start.2
  377.0 3.1 all-to-all-done.2.final_ref
  (376 shorter events, 181.3 us)
Async XLA Ops:
  2.5 30.0 %collective-permute-start.22 = (bf16[128,1024]{1,0:T(8,128)(2,1)}, bf16[128,1024]{1,0:T(8,128)(2,1)}, u32[]{:S(2)}, u32[]{:S(2)}) collective-permute-start(bf16[128,1024]{1,0:T(8,128)(2,1)} %bitcast_convert_fusion.4), channel_id=1, source_target_pairs={{0,16},{4,20},{8,24},{12,28},{16,0},{20,4},{24,8},{28,12},{1,17},{... | collective-permute-start | bytes 786440 | tf_op jit(solution)/shard_map/ppermute | solution.py:481
  4.0 29.5 %collective-permute-start.21 = (bf16[128,1024]{1,0:T(8,128)(2,1)}, bf16[128,1024]{1,0:T(8,128)(2,1)}, u32[]{:S(2)}, u32[]{:S(2)}) collective-permute-start(bf16[128,1024]{1,0:T(8,128)(2,1)} %bitcast_convert_fusion.4), channel_id=1, source_target_pairs={{0,8},{4,12},{8,0},{12,4},{16,24},{20,28},{24,16},{28,20},{1,9},{5... | collective-permute-start | bytes 786440 | tf_op jit(solution)/shard_map/ppermute | solution.py:480
  9.1 45.2 %collective-permute-start.6 = (bf16[256,896]{1,0:T(8,128)(2,1)}, bf16[256,896]{1,0:T(8,128)(2,1)}, u32[]{:S(2)}, u32[]{:S(2)}) collective-permute-start(bf16[256,896]{1,0:T(8,128)(2,1)} %pick_columns.1), channel_id=1, source_target_pairs={{0,3},{1,2},{2,1},{3,0},{4,7},{5,6},{6,5},{7,4},{8,11},{9,10},{10,... | collective-permute-start | bytes 1376264 | tf_op jit(solution)/shard_map/ppermute | solution.py:524
  12.3 24.4 %collective-permute-start.1 = (bf16[128,1024]{1,0:T(8,128)(2,1)}, bf16[128,1024]{1,0:T(8,128)(2,1)}, u32[]{:S(2)}, u32[]{:S(2)}) collective-permute-start(bf16[128,1024]{1,0:T(8,128)(2,1)} %get-tuple-element.107), channel_id=1, source_target_pairs={{0,16},{4,20},{8,24},{12,28},{16,0},{20,4},{24,8},{28,12},{1,17},{... | collective-permute-start | bytes 786440 | tf_op jit(solution)/shard_map/ppermute | solution.py:481
  12.9 25.4 %collective-permute-start = (bf16[128,1024]{1,0:T(8,128)(2,1)}, bf16[128,1024]{1,0:T(8,128)(2,1)}, u32[]{:S(2)}, u32[]{:S(2)}) collective-permute-start(bf16[128,1024]{1,0:T(8,128)(2,1)} %get-tuple-element.107), channel_id=1, source_target_pairs={{0,8},{4,12},{8,0},{12,4},{16,24},{20,28},{24,16},{28,20},{1,9},{5... | collective-permute-start | bytes 786440 | tf_op jit(solution)/shard_map/ppermute | solution.py:480
  32.5 21.7 %collective-permute-start.5 = (bf16[256,896]{1,0:T(8,128)(2,1)}, bf16[256,896]{1,0:T(8,128)(2,1)S(1)}, u32[]{:S(2)}, u32[]{:S(2)}) collective-permute-start(bf16[256,896]{1,0:T(8,128)(2,1)} %pick_columns.1), channel_id=1, source_target_pairs={{0,2},{1,3},{2,0},{3,1},{4,6},{5,7},{6,4},{7,5},{8,10},{9,11},{10,... | collective-permute-start | bytes 1376264 | tf_op jit(solution)/shard_map/ppermute | solution.py:524
  33.5 20.6 %collective-permute-start.4 = (bf16[256,896]{1,0:T(8,128)(2,1)}, bf16[256,896]{1,0:T(8,128)(2,1)S(1)}, u32[]{:S(2)}, u32[]{:S(2)}) collective-permute-start(bf16[256,896]{1,0:T(8,128)(2,1)} %pick_columns.1), channel_id=1, source_target_pairs={{0,1},{1,0},{2,3},{3,2},{4,5},{5,4},{6,7},{7,6},{8,9},{9,8},{10,11... | collective-permute-start | bytes 1376264 | tf_op jit(solution)/shard_map/ppermute | solution.py:524
  36.7 69.2 %collective-permute-start.23 = (bf16[128,1024]{1,0:T(8,128)(2,1)}, bf16[128,1024]{1,0:T(8,128)(2,1)}, u32[]{:S(2)}, u32[]{:S(2)}) collective-permute-start(bf16[128,1024]{1,0:T(8,128)(2,1)} %broadcast_select_fusion.1), channel_id=1, source_target_pairs={{0,16},{4,12},{8,24},{12,4},{16,0},{20,28},{24,8},{28,20},{1,17},{... | collective-permute-start | bytes 786440 | tf_op jit(solution)/shard_map/ppermute | solution.py:482
  47.4 19.9 %collective-permute-start.3 = (bf16[4,128,1024]{2,1,0:T(8,128)(2,1)S(1)}, bf16[4,128,1024]{2,1,0:T(8,128)(2,1)S(1)}, u32[]{:S(2)}, u32[]{:S(2)}) collective-permute-start(bf16[4,128,1024]{2,1,0:T(8,128)(2,1)S(1)} %pad_maximum_fusion), channel_id=1, source_target_pairs={{0,4},{4,0},{8,12},{12,8},{16,20},{20,16},{24,28},{28,24},{1,5},{5... | collective-permute-start | bytes 3145736 | tf_op jit(solution)/shard_map/ppermute | solution.py:488
  55.4 11.9 %collective-permute-start.9 = (bf16[256,256]{1,0:T(8,128)(2,1)S(1)}, bf16[256,256]{1,0:T(8,128)(2,1)S(1)}, u32[]{:S(2)}, u32[]{:S(2)}) collective-permute-start(bf16[256,256]{1,0:T(8,128)(2,1)S(1)} %pad_maximum_fusion.14), channel_id=1, source_target_pairs={{0,3},{1,2},{2,1},{3,0},{4,7},{5,6},{6,5},{7,4},{8,11},{9,10},{10,... | collective-permute-start | bytes 393224 | tf_op jit(solution)/shard_map/ppermute | solution.py:524
  96.7 39.7 %collective-permute-start.20 = (bf16[192,1024]{1,0:T(8,128)(2,1)S(1)}, bf16[192,1024]{1,0:T(8,128)(2,1)S(1)}, u32[]{:S(2)}, u32[]{:S(2)}) collective-permute-start(bf16[192,1024]{1,0:T(8,128)(2,1)S(1)} %copy-done.17), channel_id=1, source_target_pairs={{0,3},{1,2},{2,1},{3,0},{4,7},{5,6},{6,5},{7,4},{8,11},{9,10},{10,... | collective-permute-start | bytes 1179656 | tf_op jit(solution)/shard_map/ppermute | solution.py:524
  98.5 33.0 %collective-permute-start.19 = (bf16[192,1024]{1,0:T(8,128)(2,1)S(1)}, bf16[192,1024]{1,0:T(8,128)(2,1)S(1)}, u32[]{:S(2)}, u32[]{:S(2)}) collective-permute-start(bf16[192,1024]{1,0:T(8,128)(2,1)S(1)} %copy-done.17), channel_id=1, source_target_pairs={{0,2},{1,3},{2,0},{3,1},{4,6},{5,7},{6,4},{7,5},{8,10},{9,11},{10,... | collective-permute-start | bytes 1179656 | tf_op jit(solution)/shard_map/ppermute | solution.py:524
  102.2 24.1 %collective-permute-start.18 = (bf16[192,1024]{1,0:T(8,128)(2,1)S(1)}, bf16[192,1024]{1,0:T(8,128)(2,1)S(1)}, u32[]{:S(2)}, u32[]{:S(2)}) collective-permute-start(bf16[192,1024]{1,0:T(8,128)(2,1)S(1)} %copy-done.17), channel_id=1, source_target_pairs={{0,1},{1,0},{2,3},{3,2},{4,5},{5,4},{6,7},{7,6},{8,9},{9,8},{10,11... | collective-permute-start | bytes 1179656 | tf_op jit(solution)/shard_map/ppermute | solution.py:524
  107.3 41.6 %collective-permute-start.24 = (bf16[4,128,1024]{2,1,0:T(8,128)(2,1)S(1)}, bf16[4,128,1024]{2,1,0:T(8,128)(2,1)S(1)}, u32[]{:S(2)}, u32[]{:S(2)}) collective-permute-start(bf16[4,128,1024]{2,1,0:T(8,128)(2,1)S(1)} %pad_maximum_fusion.2), channel_id=1, source_target_pairs={{0,4},{4,0},{8,12},{12,8},{16,20},{20,16},{24,28},{28,24},{1,5},{5... | collective-permute-start | bytes 3145736 | tf_op jit(solution)/shard_map/ppermute | solution.py:488
  111.0 20.6 %collective-permute-start.12 = (bf16[128,1024]{1,0:T(8,128)(2,1)S(1)}, bf16[128,1024]{1,0:T(8,128)(2,1)S(1)}, u32[]{:S(2)}, u32[]{:S(2)}) collective-permute-start(bf16[128,1024]{1,0:T(8,128)(2,1)S(1)} %get-tuple-element.114), channel_id=1, source_target_pairs={{0,8},{4,12},{8,0},{12,4},{16,24},{20,28},{24,16},{28,20},{1,9},{5... | collective-permute-start | bytes 786440 | tf_op jit(solution)/shard_map/ppermute | solution.py:508
  191.0 12.3 %collective-permute-start.40 = (bf16[192,1024]{1,0:T(8,128)(2,1)}, bf16[192,1024]{1,0:T(8,128)(2,1)}, u32[]{:S(2)}, u32[]{:S(2)}) collective-permute-start(bf16[192,1024]{1,0:T(8,128)(2,1)} %pad_maximum_fusion.11), channel_id=1, source_target_pairs={{0,1},{1,0},{2,3},{3,2},{4,5},{5,4},{6,7},{7,6},{8,9},{9,8},{10,11... | collective-permute-start | bytes 1179656 | tf_op jit(solution)/shard_map/ppermute | solution.py:524
  191.8 28.1 %collective-permute-start.41 = (bf16[192,1024]{1,0:T(8,128)(2,1)}, bf16[192,1024]{1,0:T(8,128)(2,1)}, u32[]{:S(2)}, u32[]{:S(2)}) collective-permute-start(bf16[192,1024]{1,0:T(8,128)(2,1)} %pad_maximum_fusion.12), channel_id=1, source_target_pairs={{0,2},{1,3},{2,0},{3,1},{4,6},{5,7},{6,4},{7,5},{8,10},{9,11},{10,... | collective-permute-start | bytes 1179656 | tf_op jit(solution)/shard_map/ppermute | solution.py:524
  195.6 30.4 %collective-permute-start.42 = (bf16[192,1024]{1,0:T(8,128)(2,1)}, bf16[192,1024]{1,0:T(8,128)(2,1)}, u32[]{:S(2)}, u32[]{:S(2)}) collective-permute-start(bf16[192,1024]{1,0:T(8,128)(2,1)} %pad_maximum_fusion.13), channel_id=1, source_target_pairs={{0,3},{1,2},{2,1},{3,0},{4,7},{5,6},{6,5},{7,4},{8,11},{9,10},{10,... | collective-permute-start | bytes 1179656 | tf_op jit(solution)/shard_map/ppermute | solution.py:524
  198.8 37.0 %collective-permute-start.32 = (bf16[4,128,1024]{2,1,0:T(8,128)(2,1)}, bf16[4,128,1024]{2,1,0:T(8,128)(2,1)}, u32[]{:S(2)}, u32[]{:S(2)}) collective-permute-start(bf16[4,128,1024]{2,1,0:T(8,128)(2,1)} %pad_maximum_fusion.4), channel_id=1, source_target_pairs={{0,4},{4,0},{8,12},{12,8},{16,20},{20,16},{24,28},{28,24},{1,5},{5... | collective-permute-start | bytes 3145736 | tf_op jit(solution)/shard_map/ppermute | solution.py:488
  229.6 124.3 %all-to-all-start = ((bf16[8,128,1024]{2,1,0:T(8,128)(2,1)}), bf16[8,128,1024]{2,1,0:T(8,128)(2,1)}, u32[]{:S(2)}, u32[]{:S(2)}) async-start(bf16[8,128,1024]{2,1,0:T(8,128)(2,1)} %bitcast.33), calls=%async_computation | async-start | bytes 4194304 | tf_op jit(solution)/shard_map/all_to_all | solution.py:514
  278.6 28.2 %collective-permute-start.47 = (f32[1,40,128]{2,1,0:T(8,128)}, f32[1,40,128]{2,1,0:T(8,128)}, u32[]{:S(2)}, u32[]{:S(2)}) collective-permute-start(f32[1,40,128]{2,1,0:T(8,128)} %maximum_bitcast_fusion), channel_id=1, source_target_pairs={{0,2},{1,3},{2,0},{3,1},{4,6},{5,7},{6,4},{7,5},{8,10},{9,11},{10,... | collective-permute-start | bytes 61448 | tf_op jit(solution)/shard_map/ppermute | solution.py:524
  278.6 26.5 %collective-permute-start.46 = (f32[1,40,128]{2,1,0:T(8,128)}, f32[1,40,128]{2,1,0:T(8,128)}, u32[]{:S(2)}, u32[]{:S(2)}) collective-permute-start(f32[1,40,128]{2,1,0:T(8,128)} %maximum_bitcast_fusion), channel_id=1, source_target_pairs={{0,1},{1,0},{2,3},{3,2},{4,5},{5,4},{6,7},{7,6},{8,9},{9,8},{10,11... | collective-permute-start | bytes 61448 | tf_op jit(solution)/shard_map/ppermute | solution.py:524
  281.6 25.9 %collective-permute-start.48 = (f32[1,40,128]{2,1,0:T(8,128)}, f32[1,40,128]{2,1,0:T(8,128)}, u32[]{:S(2)}, u32[]{:S(2)}) collective-permute-start(f32[1,40,128]{2,1,0:T(8,128)} %maximum_bitcast_fusion), channel_id=1, source_target_pairs={{0,3},{1,2},{2,1},{3,0},{4,7},{5,6},{6,5},{7,4},{8,11},{9,10},{10,... | collective-permute-start | bytes 61448 | tf_op jit(solution)/shard_map/ppermute | solution.py:524
  294.2 57.4 %collective-permute-start.37 = (bf16[8,32,896]{2,1,0:T(8,128)(2,1)}, bf16[8,32,896]{2,1,0:T(8,128)(2,1)}, u32[]{:S(2)}, u32[]{:S(2)}) collective-permute-start(bf16[8,32,896]{2,1,0:T(8,128)(2,1)} %get-tuple-element.121), channel_id=1, source_target_pairs={{0,1},{1,0},{2,3},{3,2},{4,5},{5,4},{6,7},{7,6},{8,9},{9,8},{10,11... | collective-permute-start | bytes 1376264 | tf_op jit(solution)/shard_map/ppermute | solution.py:524
  295.1 56.4 %collective-permute-start.38 = (bf16[8,32,896]{2,1,0:T(8,128)(2,1)}, bf16[8,32,896]{2,1,0:T(8,128)(2,1)}, u32[]{:S(2)}, u32[]{:S(2)}) collective-permute-start(bf16[8,32,896]{2,1,0:T(8,128)(2,1)} %get-tuple-element.122), channel_id=1, source_target_pairs={{0,2},{1,3},{2,0},{3,1},{4,6},{5,7},{6,4},{7,5},{8,10},{9,11},{10,... | collective-permute-start | bytes 1376264 | tf_op jit(solution)/shard_map/ppermute | solution.py:524
  305.1 15.5 %collective-permute-start.43 = (bf16[8,32,256]{2,1,0:T(8,128)(2,1)}, bf16[8,32,256]{2,1,0:T(8,128)(2,1)}, u32[]{:S(2)}, u32[]{:S(2)}) collective-permute-start(bf16[8,32,256]{2,1,0:T(8,128)(2,1)} %get-tuple-element.136), channel_id=1, source_target_pairs={{0,1},{1,0},{2,3},{3,2},{4,5},{5,4},{6,7},{7,6},{8,9},{9,8},{10,11... | collective-permute-start | bytes 393224 | tf_op jit(solution)/shard_map/ppermute | solution.py:524
  312.3 23.7 %collective-permute-start.44 = (bf16[8,32,256]{2,1,0:T(8,128)(2,1)}, bf16[8,32,256]{2,1,0:T(8,128)(2,1)S(1)}, u32[]{:S(2)}, u32[]{:S(2)}) collective-permute-start(bf16[8,32,256]{2,1,0:T(8,128)(2,1)} %get-tuple-element.137), channel_id=1, source_target_pairs={{0,2},{1,3},{2,0},{3,1},{4,6},{5,7},{6,4},{7,5},{8,10},{9,11},{10,... | collective-permute-start | bytes 393224 | tf_op jit(solution)/shard_map/ppermute | solution.py:524
  317.8 20.9 %collective-permute-start.45 = (bf16[8,32,256]{2,1,0:T(8,128)(2,1)S(1)}, bf16[8,32,256]{2,1,0:T(8,128)(2,1)S(1)}, u32[]{:S(2)}, u32[]{:S(2)}) collective-permute-start(bf16[8,32,256]{2,1,0:T(8,128)(2,1)S(1)} %get-tuple-element.138), channel_id=1, source_target_pairs={{0,3},{1,2},{2,1},{3,0},{4,7},{5,6},{6,5},{7,4},{8,11},{9,10},{10,... | collective-permute-start | bytes 393224 | tf_op jit(solution)/shard_map/ppermute | solution.py:524
  320.6 31.0 %collective-permute-start.39 = (bf16[8,32,896]{2,1,0:T(8,128)(2,1)}, bf16[8,32,896]{2,1,0:T(8,128)(2,1)}, u32[]{:S(2)}, u32[]{:S(2)}) collective-permute-start(bf16[8,32,896]{2,1,0:T(8,128)(2,1)} %get-tuple-element.123), channel_id=1, source_target_pairs={{0,3},{1,2},{2,1},{3,0},{4,7},{5,6},{6,5},{7,4},{8,11},{9,10},{10,... | collective-permute-start | bytes 1376264 | tf_op jit(solution)/shard_map/ppermute | solution.py:524
  353.9 13.7 %all-to-all-start.1 = ((bf16[8,256,128]{2,1,0:T(8,128)(2,1)}), bf16[8,256,128]{2,1,0:T(8,128)(2,1)S(1)}, u32[]{:S(2)}, u32[]{:S(2)}) async-start(bf16[8,256,128]{2,1,0:T(8,128)(2,1)} %pad_maximum_fusion.9), calls=%async_computation.1 | async-start | bytes 1048576 | tf_op jit(solution)/shard_map/all_to_all | solution.py:514
  361.7 11.8 %collective-permute-start.35 = (bf16[128,1024]{1,0:T(8,128)(2,1)}, bf16[128,1024]{1,0:T(8,128)(2,1)S(1)}, u32[]{:S(2)}, u32[]{:S(2)}) collective-permute-start(bf16[128,1024]{1,0:T(8,128)(2,1)} %get-tuple-element.110), channel_id=1, source_target_pairs={{0,8},{4,12},{8,0},{12,4},{16,24},{20,28},{24,16},{28,20},{1,9},{5... | collective-permute-start | bytes 786440 | tf_op jit(solution)/shard_map/ppermute | solution.py:508
  367.6 12.4 %all-to-all-start.2 = ((bf16[8,32,896]{2,1,0:T(8,128)(2,1)}), bf16[8,32,896]{2,1,0:T(8,128)(2,1)S(1)}, u32[]{:S(2)}, u32[]{:S(2)}) async-start(bf16[8,32,896]{2,1,0:T(8,128)(2,1)} %fusion.7), calls=%async_computation.2 | async-start | bytes 917504 | tf_op jit(solution)/shard_map/all_to_all | solution.py:514
  (85 other events, 605.6 us)
